TPU v7x, 32 devices: a whole 2x2x4 slice. The times are simulated.
32 devices in a mesh: fsdp: 32 (over z, y, x, core).
Axes of the slice: x: 2, y: 2, z: 4, core: 2. Of those that a mesh axis runs over, the one named last changes fastest.
Arguments:
- tokens: bfloat16 [4096, 2048], P('fsdp'), may hold values from -6 to 6
- segments: int32 [2, 2048], replicated, may hold values from 0 to 15, never falling along the last dimension, each value on 1 to 1024 neighbouring positions
- routes: int32 [4096, 8], P('fsdp'), may hold values from 0 to 15, all different within a row; in each aligned block of 128 rows (0 to 127, 128 to 255, ...) at most 128 rows name the same one
- gates: float32 [4096, 8], P('fsdp'), may hold values from 0.25 to 0.75
- sequence_adapter_index: int32 [2], replicated, may hold values from 0 to 7
- attention_norm_gain: bfloat16 [2048], replicated, may hold values from 0.5 to 1.5
- query_norm_gain: bfloat16 [128], replicated, may hold values from 0.25 to 1.75
- key_norm_gain: bfloat16 [128], replicated, may hold values from 0.25 to 1.75
- query_weight: bfloat16 [2048, 2048], P('fsdp'), may hold values from -0.125 to 0.125
- key_weight: bfloat16 [2048, 2048], P('fsdp'), may hold values from -0.125 to 0.125
- value_weight: bfloat16 [2048, 2048], P('fsdp'), may hold values from -0.125 to 0.125
- output_weight: bfloat16 [2048, 2048], P('fsdp'), may hold values from -0.5 to 0.5
- adapter_down_factors: bfloat16 [8, 4, 2048, 16], P(None, None, 'fsdp'), may hold values from -0.125 to 0.125
- adapter_up_factors: bfloat16 [8, 4, 16, 2048], P(None, None, None, 'fsdp'), may hold values from -0.75 to 0.75
- expert_norm_gain: bfloat16 [2048], replicated, may hold values from 0.5 to 1.5
- expert_gate_weight: bfloat16 [32, 2048, 512], P('fsdp'), may hold values from -0.125 to 0.125
- expert_up_weight: bfloat16 [32, 2048, 512], P('fsdp'), may hold values from -0.125 to 0.125
- expert_down_weight: bfloat16 [32, 512, 2048], P('fsdp'), may hold values from -0.1875 to 0.1875
- output_gradient: bfloat16 [4096, 2048], P('fsdp'), may hold values from -6 to 6
Outputs:
- output: bfloat16 [4096, 2048], P('fsdp')
- grad_tokens: bfloat16 [4096, 2048], P('fsdp')
- grad_lora_down: float32 [8, 4, 2048, 16], P(None, None, 'fsdp')
- grad_lora_up: float32 [8, 4, 16, 2048], P(None, None, None, 'fsdp')
Inputs may be any that keep to these rules, and one draw needn't show every extreme that they name: `segments`: segment numbers never fall along a sequence; a document holds at most 1024 positions, and one holds exactly that many. `routes`: A row names 8 different experts. In the rows of one device no expert is named by more than 128 rows, a bound that some block reaches.
All inputs are finite; a program needn't handle non-finite values.
Results may differ from a plain program's by a relative error of at most 0.018.
Values may be sent and summed in bfloat16 or wider, within the bound.
A program may use at most 384 MiB of HBM per device.

v0:
```python
import math

import jax
import jax.numpy as jnp
from jax import lax
from jax.sharding import PartitionSpec as P

HEAD_DIM = 128
TOPK = 8
ADAPTER_COUNT = 8
SEQ_LEN = 2048


epsilon = 1e-06
rope_base = 50000.0


def from_partner(value, axis, distance):
    mask = 2**distance
    pairs = [(source, source ^ mask) for source in range(lax.axis_size(axis))]
    return lax.ppermute(value, axis, pairs)


def matmul(left, right):
    return jnp.dot(left, right, preferred_element_type=jnp.float32)


def rms_scale(rows, gain):
    return rows * lax.rsqrt(jnp.mean(rows * rows, axis=-1, keepdims=True) + epsilon) * gain


def rms_back(rows, gain, upstream):
    inverse = lax.rsqrt(jnp.mean(rows * rows, axis=-1, keepdims=True) + epsilon)
    unit = rows * inverse
    scaled = upstream * gain
    return inverse * (scaled - unit * jnp.mean(scaled * unit, axis=-1, keepdims=True))


def rope_tables(positions):
    half = HEAD_DIM // 2
    frequency = rope_base ** (-(jnp.arange(half, dtype=jnp.float32) * 2.0 / HEAD_DIM))
    angle = positions[:, None] * frequency[None, :]
    return (jnp.cos(angle)[:, None, :], jnp.sin(angle)[:, None, :])


def rotate(rows, cosine, sine):
    half = rows.shape[-1] // 2
    first = rows[..., :half]
    second = rows[..., half:]
    return jnp.concatenate(
        [first * cosine - second * sine, second * cosine + first * sine], axis=-1
    )


def rotate_back(upstream, cosine, sine):
    half = upstream.shape[-1] // 2
    first = upstream[..., :half]
    second = upstream[..., half:]
    return jnp.concatenate(
        [first * cosine + second * sine, second * cosine - first * sine], axis=-1
    )


def pick(table, index):
    return lax.dynamic_index_in_dim(table, index, 0, keepdims=False)


def shards(
    tokens,
    segments,
    routes,
    gates,
    sequence_adapter_index,
    attention_norm_gain,
    query_norm_gain,
    key_norm_gain,
    query_weight,
    key_weight,
    value_weight,
    output_weight,
    adapter_down_factors,
    adapter_up_factors,
    expert_norm_gain,
    expert_gate_weight,
    expert_up_weight,
    expert_down_weight,
    output_gradient,
):
    rows_dev = tokens.shape[0]
    width = tokens.shape[1]
    heads = width // HEAD_DIM
    group = SEQ_LEN // rows_dev
    level_list = group.bit_length() - 1
    device = lax.axis_index("fsdp")
    place = device % group
    sequence = device // group
    segment_row = pick(segments, sequence)
    own_segment = lax.dynamic_slice_in_dim(segment_row, place * rows_dev, rows_dev)
    adapter = pick(sequence_adapter_index, sequence)
    scale = 1.0 / math.sqrt(HEAD_DIM)
    cosine, sine = rope_tables(
        (place * rows_dev + jnp.arange(rows_dev, dtype=jnp.int32)).astype(jnp.float32)
    )
    attn_scale = attention_norm_gain.astype(jnp.float32)
    query_scale = query_norm_gain.astype(jnp.float32)
    key_scale = key_norm_gain.astype(jnp.float32)
    ffn_scale = expert_norm_gain.astype(jnp.float32)
    gathered = (
        lax.all_gather(query_weight, "fsdp", axis=0, tiled=True),
        lax.all_gather(key_weight, "fsdp", axis=0, tiled=True),
        lax.all_gather(value_weight, "fsdp", axis=0, tiled=True),
        lax.all_gather(output_weight, "fsdp", axis=0, tiled=True),
        lax.all_gather(adapter_down_factors, "fsdp", axis=2, tiled=True),
        lax.all_gather(adapter_up_factors, "fsdp", axis=3, tiled=True),
    )
    matrices = gathered[:4]
    down_own = pick(gathered[4], adapter)
    up_own = pick(gathered[5], adapter)

    def project(inputs, index):
        inner = matmul(inputs, down_own[index]).astype(jnp.bfloat16)
        return (matmul(inputs, matrices[index]) + matmul(inner, up_own[index]), inner)

    rows = tokens.astype(jnp.float32)
    normed = rms_scale(rows, attn_scale).astype(jnp.bfloat16)
    query_proj, query_inner = project(normed, 0)
    key_proj, key_inner = project(normed, 1)
    value_proj, value_inner = project(normed, 2)
    query_heads = query_proj.reshape(rows_dev, heads, HEAD_DIM)
    key_heads = key_proj.reshape(rows_dev, heads, HEAD_DIM)
    query_rot = rotate(rms_scale(query_heads, query_scale), cosine, sine).astype(jnp.bfloat16)
    key_rot = (
        rotate(rms_scale(key_heads, key_scale), cosine, sine)
        .astype(jnp.bfloat16)
        .reshape(rows_dev, width)
    )
    value_low = value_proj.astype(jnp.bfloat16)
    held_keys = key_rot
    held_values = value_low
    for level in range(level_list):
        other_keys, other_values = from_partner((held_keys, held_values), "fsdp", level)
        upper_bit = place // (1 << level) % 2 == 1
        held_keys = jnp.where(
            upper_bit,
            jnp.concatenate([other_keys, held_keys], axis=0),
            jnp.concatenate([held_keys, other_keys], axis=0),
        )
        held_values = jnp.where(
            upper_bit,
            jnp.concatenate([other_values, held_values], axis=0),
            jnp.concatenate([held_values, other_values], axis=0),
        )
    keys_all = held_keys.reshape(SEQ_LEN, heads, HEAD_DIM)
    values_all = held_values.reshape(SEQ_LEN, heads, HEAD_DIM)
    allowed = (own_segment[:, None] == segment_row[None, :])[None]

    def masked_scores():
        raw = (
            jnp.einsum("thd,shd->hts", query_rot, keys_all, preferred_element_type=jnp.float32)
            * scale
        )
        return jnp.where(allowed, raw, -1e30)

    scores = masked_scores()
    maximum = jnp.max(scores, axis=-1, keepdims=True)
    weights = jnp.exp(scores - maximum)
    total = jnp.sum(weights, axis=-1, keepdims=True)
    probs = weights / total
    log_total = maximum + jnp.log(total)
    mixed = jnp.einsum(
        "hts,shd->thd", probs.astype(jnp.bfloat16), values_all, preferred_element_type=jnp.float32
    )
    mixed = mixed.astype(jnp.bfloat16).reshape(rows_dev, width)
    attn_proj, out_inner = project(mixed, 3)
    middle = rows + attn_proj
    normed_ffn = rms_scale(middle, ffn_scale).astype(jnp.bfloat16)
    experts = lax.axis_size("fsdp") // 2
    capacity = 2 * rows_dev * TOPK // experts
    flat_routes = routes.reshape(-1)
    onehot = (flat_routes[:, None] == jnp.arange(experts, dtype=jnp.int32)[None, :]).astype(
        jnp.int32
    )
    slot = jnp.sum(jnp.cumsum(onehot, axis=0) * onehot, axis=1) - 1
    target = flat_routes * capacity + slot

    def spread(entries):
        buffer = jnp.zeros((experts * capacity, width), jnp.bfloat16).at[target].set(entries)
        buffer = buffer.reshape(experts, 1, capacity, width)
        return jnp.broadcast_to(buffer, (experts, 2, capacity, width)).reshape(
            2 * experts, capacity, width
        )

    def collect(returned):
        halves = returned.reshape(experts, 2, capacity, width).astype(jnp.float32)
        summed = (halves[:, 0] + halves[:, 1]).reshape(experts * capacity, width)
        return summed[target].reshape(rows_dev, TOPK, width)

    slab_gate = expert_gate_weight[0]
    slab_up = expert_up_weight[0]
    slab_down = expert_down_weight[0]
    dispatched = lax.all_to_all(
        spread(jnp.repeat(normed_ffn, TOPK, axis=0)),
        "fsdp",
        split_axis=0,
        concat_axis=0,
        tiled=True,
    )
    gate_part = jnp.einsum("scd,dh->sch", dispatched, slab_gate, preferred_element_type=jnp.float32)
    up_part = jnp.einsum("scd,dh->sch", dispatched, slab_up, preferred_element_type=jnp.float32)
    hidden = (jax.nn.silu(gate_part) * up_part).astype(jnp.bfloat16)
    produced = jnp.einsum(
        "sch,hd->scd", hidden, slab_down, preferred_element_type=jnp.float32
    ).astype(jnp.bfloat16)
    returned = lax.all_to_all(produced, "fsdp", split_axis=0, concat_axis=0, tiled=True)
    moe = jnp.sum(gates[:, :, None] * collect(returned), axis=1)
    output = (middle + moe).astype(jnp.bfloat16)
    upstream = output_gradient.astype(jnp.float32)
    grad_parts = (
        (gates[:, :, None] * upstream[:, None, :])
        .astype(jnp.bfloat16)
        .reshape(rows_dev * TOPK, width)
    )
    grad_sent = lax.all_to_all(spread(grad_parts), "fsdp", split_axis=0, concat_axis=0, tiled=True)
    grad_hidden = jnp.einsum(
        "scd,hd->sch", grad_sent, slab_down, preferred_element_type=jnp.float32
    )
    sigmoid = jax.nn.sigmoid(gate_part)
    grad_gate = (grad_hidden * up_part * sigmoid * (1.0 + gate_part * (1.0 - sigmoid))).astype(
        jnp.bfloat16
    )
    grad_up = (grad_hidden * gate_part * sigmoid).astype(jnp.bfloat16)
    grad_inputs = jnp.einsum(
        "sch,dh->scd", grad_gate, slab_gate, preferred_element_type=jnp.float32
    )
    grad_inputs = (
        grad_inputs
        + jnp.einsum("sch,dh->scd", grad_up, slab_up, preferred_element_type=jnp.float32)
    ).astype(jnp.bfloat16)
    grad_back = lax.all_to_all(grad_inputs, "fsdp", split_axis=0, concat_axis=0, tiled=True)
    grad_ffn = jnp.sum(collect(grad_back), axis=1)
    grad_middle = upstream + rms_back(middle, ffn_scale, grad_ffn)
    grad_attn = grad_middle.astype(jnp.bfloat16)
    regathered = (
        lax.all_gather(query_weight, "fsdp", axis=0, tiled=True),
        lax.all_gather(key_weight, "fsdp", axis=0, tiled=True),
        lax.all_gather(value_weight, "fsdp", axis=0, tiled=True),
        lax.all_gather(output_weight, "fsdp", axis=0, tiled=True),
        lax.all_gather(adapter_down_factors, "fsdp", axis=2, tiled=True),
        lax.all_gather(adapter_up_factors, "fsdp", axis=3, tiled=True),
    )
    back_matrices = regathered[:4]
    back_down = pick(regathered[4], adapter)
    back_up = pick(regathered[5], adapter)

    def project_back(inputs, inner, upstream_low, index):
        grad_inner = matmul(upstream_low, back_up[index].T).astype(jnp.bfloat16)
        grad_input = matmul(upstream_low, back_matrices[index].T) + matmul(
            grad_inner, back_down[index].T
        )
        return (grad_input, matmul(inputs.T, grad_inner), matmul(inner.T, upstream_low))

    grad_mixed_full, down_output, up_output = project_back(mixed, out_inner, grad_attn, 3)
    grad_mixed = grad_mixed_full.astype(jnp.bfloat16).reshape(rows_dev, heads, HEAD_DIM)
    probs = jnp.exp(masked_scores() - log_total)
    grad_probs = jnp.einsum(
        "thd,shd->hts", grad_mixed, values_all, preferred_element_type=jnp.float32
    )
    grad_scores = (
        probs * (grad_probs - jnp.sum(probs * grad_probs, axis=-1, keepdims=True))
    ).astype(jnp.bfloat16)
    grad_query = (
        jnp.einsum("hts,shd->thd", grad_scores, keys_all, preferred_element_type=jnp.float32)
        * scale
    )
    grad_keys_part = (
        jnp.einsum("hts,thd->shd", grad_scores, query_rot, preferred_element_type=jnp.float32)
        * scale
    )
    grad_keys_part = grad_keys_part.reshape(group, rows_dev, width)
    grad_values_part = jnp.einsum(
        "hts,thd->shd", probs.astype(jnp.bfloat16), grad_mixed, preferred_element_type=jnp.float32
    )
    grad_values_part = grad_values_part.reshape(group, rows_dev, width)
    for level in reversed(range(level_list)):
        size_half = 1 << level
        upper_bit = place // size_half % 2 == 1
        keep_keys = jnp.where(upper_bit, grad_keys_part[size_half:], grad_keys_part[:size_half])
        send_keys = jnp.where(upper_bit, grad_keys_part[:size_half], grad_keys_part[size_half:])
        keep_values = jnp.where(
            upper_bit, grad_values_part[size_half:], grad_values_part[:size_half]
        )
        send_values = jnp.where(
            upper_bit, grad_values_part[:size_half], grad_values_part[size_half:]
        )
        got_keys, got_values = (
            from_partner(send_keys.astype(jnp.bfloat16), "fsdp", level).astype(send_keys.dtype),
            from_partner(send_values.astype(jnp.bfloat16), "fsdp", level).astype(send_values.dtype),
        )
        grad_keys_part = keep_keys + got_keys
        grad_values_part = keep_values + got_values
    grad_keys = grad_keys_part[0]
    grad_values = grad_values_part[0]
    grad_value_proj = grad_values.astype(jnp.bfloat16)
    grad_key_proj = rms_back(
        key_heads,
        key_scale,
        rotate_back(grad_keys.reshape(rows_dev, heads, HEAD_DIM), cosine, sine),
    )
    grad_key_proj = grad_key_proj.reshape(rows_dev, width).astype(jnp.bfloat16)
    grad_query_proj = rms_back(query_heads, query_scale, rotate_back(grad_query, cosine, sine))
    grad_query_proj = grad_query_proj.reshape(rows_dev, width).astype(jnp.bfloat16)
    grad_from_query, down_query, up_query = project_back(normed, query_inner, grad_query_proj, 0)
    grad_from_key, down_key, up_key = project_back(normed, key_inner, grad_key_proj, 1)
    grad_from_value, down_value, up_value = project_back(normed, value_inner, grad_value_proj, 2)
    grad_normed = grad_from_query + grad_from_key + grad_from_value
    grad_tokens = (grad_middle + rms_back(rows, attn_scale, grad_normed)).astype(jnp.bfloat16)
    down_terms = jnp.stack([down_query, down_key, down_value, down_output])
    up_terms = jnp.stack([up_query, up_key, up_value, up_output])
    selected = (jnp.arange(ADAPTER_COUNT, dtype=jnp.int32) == adapter).astype(jnp.float32)[
        :, None, None, None
    ]
    grad_down, grad_up = (
        lax.psum_scatter(selected * down_terms[None], "fsdp", scatter_dimension=2, tiled=True),
        lax.psum_scatter(selected * up_terms[None], "fsdp", scatter_dimension=3, tiled=True),
    )
    return (output, grad_tokens, grad_down, grad_up)


def solution(mesh):
    in_specs = (
        P("fsdp", None),
        P(),
        P("fsdp", None),
        P("fsdp", None),
        P(),
        P(),
        P(),
        P(),
        P("fsdp", None),
        P("fsdp", None),
        P("fsdp", None),
        P("fsdp", None),
        P(None, None, "fsdp", None),
        P(None, None, None, "fsdp"),
        P(),
        P("fsdp", None, None),
        P("fsdp", None, None),
        P("fsdp", None, None),
        P("fsdp", None),
    )
    out_specs = (
        P("fsdp", None),
        P("fsdp", None),
        P(None, None, "fsdp", None),
        P(None, None, None, "fsdp"),
    )
    return jax.shard_map(shards, mesh=mesh, in_specs=in_specs, out_specs=out_specs, check_vma=False)
```

profile of v0, /device:TPU:0, one launch (start us, length us, event | category | flops | bytes accessed | tf_op | source)
XLA Modules:
  0.0 3132.7 jit_solution(1447507734759613129)
XLA Ops:
  21.6 107.4 %all-gather.9.cloned.1.call-done = bf16[8,4,2048,16]{3,0,1,2:T(8,128)(2,1)} async-done(((bf16[8,4,64,16]{3,0,1,2:T(8,128)(2,1)}), bf16[8,4,2048,16]{3,0,1,2:T(8,128)(2,1)}) %all-gather.9.cloned.1.call-update) | async-done | bytes 2097168 | tf_op jit(solution)/shard_map/all_gather | solution.py:113
  140.8 104.8 %all-gather.11.cloned.1.call-done = bf16[8,4,16,2048]{2,0,1,3:T(8,128)(2,1)} async-done(((bf16[8,4,16,64]{2,0,1,3:T(8,128)(2,1)}), bf16[8,4,16,2048]{2,0,1,3:T(8,128)(2,1)}) %all-gather.11.cloned.1.call-update) | async-done | bytes 2097168 | tf_op jit(solution)/shard_map/all_gather | solution.py:114
  267.2 57.0 %all-gather.7.cloned.1.call-done = bf16[2048,2048]{1,0:T(8,128)(2,1)} async-done(((bf16[64,2048]{1,0:T(8,128)(2,1)}), bf16[2048,2048]{1,0:T(8,128)(2,1)}) %all-gather.7.cloned.1.call-update) | async-done | bytes 8388624 | tf_op jit(solution)/shard_map/all_gather | solution.py:111
  329.5 73.4 %all-gather.15.cloned.1.call-done = bf16[2048,2048]{1,0:T(8,128)(2,1)} async-done(((bf16[64,2048]{1,0:T(8,128)(2,1)}), bf16[2048,2048]{1,0:T(8,128)(2,1)}) %all-gather.15.cloned.1.call-update) | async-done | bytes 8388624 | tf_op jit(solution)/shard_map/all_gather | solution.py:110
  409.5 72.2 %all-gather.13.cloned.1.call-done = bf16[2048,2048]{1,0:T(8,128)(2,1)} async-done(((bf16[64,2048]{1,0:T(8,128)(2,1)}), bf16[2048,2048]{1,0:T(8,128)(2,1)}) %all-gather.13.cloned.1.call-update) | async-done | bytes 8388624 | tf_op jit(solution)/shard_map/all_gather | solution.py:109
  501.9 28.8 collective-permute-done.1
  537.2 28.1 collective-permute-done.5
  577.0 22.3 collective-permute-done.2
  606.9 35.0 %collective-permute-done.6 = bf16[512,2048]{1,0:T(8,128)(2,1)} collective-permute-done((bf16[512,2048]{1,0:T(8,128)(2,1)}, bf16[512,2048]{1,0:T(8,128)(2,1)}, u32[]{:S(2)}, u32[]{:S(2)}) %collective-permute-start.6) | collective-permute-done | bytes 2097184 | tf_op jit(solution)/shard_map/ppermute | solution.py:21
  673.7 25.6 collective-permute-done.3
  704.5 79.2 %collective-permute-done.7 = bf16[1024,2048]{1,0:T(8,128)(2,1)} collective-permute-done((bf16[1024,2048]{1,0:T(8,128)(2,1)}, bf16[1024,2048]{1,0:T(8,128)(2,1)}, u32[]{:S(2)}, u32[]{:S(2)}) %collective-permute-start.7) | collective-permute-done | bytes 4194336 | tf_op jit(solution)/shard_map/ppermute | solution.py:21
  788.9 15.1 fusion.110
  812.2 14.3 fusion.46
  833.0 11.5 scatter_custom_fusion
  844.5 10.8 broadcast_in_dim.30
  861.5 11.9 scatter_custom_fusion.1
  873.4 358.8 %all-to-all-done = bf16[32,128,2048]{2,1,0:T(8,128)(2,1)} async-done(((bf16[32,128,2048]{2,1,0:T(8,128)(2,1)}), bf16[32,128,2048]{2,1,0:T(8,128)(2,1)}, u32[]{:S(2)}, u32[]{:S(2)}) %all-to-all-start) | async-done | bytes 16777248 | tf_op jit(solution)/shard_map/all_to_all | solution.py:201
  1232.2 10.8 broadcast_in_dim.32
  1247.3 15.2 fusion.33
  1262.5 14.4 fusion.36
  1276.9 18.8 convolution_convert_fusion
  1295.7 324.2 %all-to-all-done.2 = bf16[32,128,2048]{2,1,0:T(8,128)(2,1)} async-done(((bf16[32,128,2048]{2,1,0:T(8,128)(2,1)}), bf16[32,128,2048]{2,1,0:T(8,128)(2,1)}, u32[]{:S(2)}, u32[]{:S(2)}) %all-to-all-start.2) | async-done | bytes 16777248 | tf_op jit(solution)/shard_map/all_to_all | solution.py:223
  1624.0 14.7 fusion.29
  1638.7 24.5 fusion.11
  1663.2 25.6 add_convert_fusion
  1688.8 307.9 %all-to-all-done.1 = bf16[32,128,2048]{2,1,0:T(8,128)(2,1)} async-done(((bf16[32,128,2048]{2,1,0:T(8,128)(2,1)}), bf16[32,128,2048]{2,1,0:T(8,128)(2,1)}, u32[]{:S(2)}, u32[]{:S(2)}) %all-to-all-start.1) | async-done | bytes 16777248 | tf_op jit(solution)/shard_map/all_to_all | solution.py:214
  2000.7 18.9 convert.18
  2019.6 17.5 slice_add_fusion.1
  2037.1 14.8 gather_fusion
  2058.3 315.0 %all-to-all-done.3 = bf16[32,128,2048]{2,1,0:T(8,128)(2,1)} async-done(((bf16[32,128,2048]{2,1,0:T(8,128)(2,1)}), bf16[32,128,2048]{2,1,0:T(8,128)(2,1)}, u32[]{:S(2)}, u32[]{:S(2)}) %all-to-all-start.3) | async-done | bytes 16777248 | tf_op jit(solution)/shard_map/all_to_all | solution.py:239
  2373.3 18.7 convert.19
  2392.0 17.5 slice_add_fusion
  2409.6 15.1 gather_fusion.1
  2439.3 19.2 multiply_reduce_fusion
  2458.5 15.6 multiply_convert_fusion
  2488.5 14.1 fusion.8
  2517.3 12.1 slice_select_fusion.1
  2538.2 12.0 slice_select_fusion
  2559.4 22.9 collective-permute-done.8
  2594.0 76.8 %collective-permute-done.12 = bf16[8,128,2048]{1,2,0:T(8,128)(2,1)} collective-permute-done((bf16[8,128,2048]{1,2,0:T(8,128)(2,1)}, bf16[8,128,2048]{1,2,0:T(8,128)(2,1)}, u32[]{:S(2)}, u32[]{:S(2)}) %collective-permute-start.12) | collective-permute-done | bytes 4194336 | tf_op jit(solution)/shard_map/ppermute | solution.py:21
  2698.4 32.5 %collective-permute-done.13 = bf16[4,128,2048]{1,2,0:T(8,128)(2,1)} collective-permute-done((bf16[4,128,2048]{1,2,0:T(8,128)(2,1)S(1)}, bf16[4,128,2048]{1,2,0:T(8,128)(2,1)}, u32[]{:S(2)}, u32[]{:S(2)}) %collective-permute-start.13) | collective-permute-done | bytes 2097184 | tf_op jit(solution)/shard_map/ppermute | solution.py:21
  2733.8 22.4 collective-permute-done.14
  2784.2 27.9 copy.320
  2812.1 33.1 %reshape.402 = f32[2048,512]{1,0:T(8,128)} reshape(f32[2048,8,4,16]{3,2,1,0:T(4,128)} %bitcast.330) | data formatting | bytes 8388608
  2849.8 28.0 copy.318
  2877.9 33.0 %reshape.400 = f32[2048,512]{1,0:T(8,128)} reshape(f32[2048,8,4,16]{3,2,1,0:T(4,128)} %bitcast.331) | data formatting | bytes 8388608
  2929.2 54.2 %reduce-scatter.9.cloned.1.call-done = f32[64,512]{1,0:T(8,128)} async-done(((f32[2048,512]{1,0:T(8,128)}), f32[64,512]{1,0:T(8,128)}) %reduce-scatter.9.cloned.1.call-update) | async-done | bytes 131088
  2986.5 135.9 %reduce-scatter.7.cloned.1.call-done = f32[64,512]{1,0:T(8,128)} async-done(((f32[2048,512]{1,0:T(8,128)}), f32[64,512]{1,0:T(8,128)}) %reduce-scatter.7.cloned.1.call-update) | async-done | bytes 131088
  (406 shorter events, 345.3 us)
Async XLA Ops:
  7.2 1269.8 %copy-start = (bf16[1,512,2048]{2,1,0:T(8,128)(2,1)S(1)}, bf16[1,512,2048]{2,1,0:T(8,128)(2,1)}, u32[]{:S(2)}) copy-start(bf16[1,512,2048]{2,1,0:T(8,128)(2,1)} %param.36) | copy-start | bytes 6291460
  7.2 121.9 %all-gather.9.cloned.1.call-start = ((), (), s32[]{:S(2)}) async-start(), calls=%async_computation.7 | async-start | bytes 17301504 | tf_op jit(solution)/shard_map/all_gather | solution.py:113
  9.8 235.7 %all-gather.11.cloned.1.call-start = ((), (), s32[]{:S(2)}) async-start(), calls=%async_computation.8 | async-start | bytes 17301504 | tf_op jit(solution)/shard_map/all_gather | solution.py:114
  12.3 311.9 %all-gather.7.cloned.1.call-start = ((), (), s32[]{:S(2)}) async-start(), calls=%async_computation.6 | async-start | bytes 8650752 | tf_op jit(solution)/shard_map/all_gather | solution.py:111
  13.0 389.9 %all-gather.15.cloned.1.call-start = ((), (), s32[]{:S(2)}) async-start(), calls=%async_computation.10 | async-start | bytes 8650752 | tf_op jit(solution)/shard_map/all_gather | solution.py:110
  13.6 468.1 %all-gather.13.cloned.1.call-start = ((), (), s32[]{:S(2)}) async-start(), calls=%async_computation.9 | async-start | bytes 8650752 | tf_op jit(solution)/shard_map/all_gather | solution.py:109
  14.2 812.5 %all-gather.17.cloned.1.call-start = ((), (), s32[]{:S(2)}) async-start(), calls=%async_computation.11 | async-start | bytes 8650752 | tf_op jit(solution)/shard_map/all_gather | solution.py:112
  18.6 463.1 %copy-start.64 = (f32[128]{0:T(128)}, f32[128]{0:T(128)S(1)}, u32[]{:S(2)}) copy-start(f32[128]{0:T(128)S(1)} %add_rsqrt_fusion.3) | copy-start | bytes 1540
  19.3 462.4 %copy-start.26 = (f32[2048]{0:T(1024)}, f32[2048]{0:T(1024)S(1)}, u32[]{:S(2)}) copy-start(f32[2048]{0:T(1024)S(1)} %convert_element_type.202) | copy-start | bytes 24580
  20.0 468.4 %copy-start.76 = (f32[128]{0:T(128)}, f32[128]{0:T(128)S(1)}, u32[]{:S(2)}) copy-start(f32[128]{0:T(128)S(1)} %convert_element_type.207) | copy-start | bytes 1540
  20.6 467.8 %copy-start.79 = (f32[128]{0:T(128)}, f32[128]{0:T(128)S(1)}, u32[]{:S(2)}) copy-start(f32[128]{0:T(128)S(1)} %convert_element_type.210) | copy-start | bytes 1540
  21.6 469.0 %copy-start.28 = (f32[128,64]{1,0:T(8,128)}, f32[128,64]{1,0:T(8,128)S(1)}, u32[]{:S(2)}) copy-start(f32[128,64]{1,0:T(8,128)S(1)} %get-tuple-element.32) | copy-start | bytes 98308
  21.6 469.0 %copy-start.30 = (f32[128,64]{1,0:T(8,128)}, f32[128,64]{1,0:T(8,128)S(1)}, u32[]{:S(2)}) copy-start(f32[128,64]{1,0:T(8,128)S(1)} %get-tuple-element.33) | copy-start | bytes 98308
  21.6 237.8 %copy-start.4 = (bf16[128,2048]{1,0:T(8,128)(2,1)S(1)}, bf16[128,2048]{1,0:T(8,128)(2,1)}, u32[]{:S(2)}) copy-start(bf16[128,2048]{1,0:T(8,128)(2,1)} %param.19) | copy-start | bytes 1572868
  260.1 147.5 %copy-start.71 = (bf16[128,16]{0,1:T(8,128)(2,1)}, bf16[128,16]{0,1:T(8,128)(2,1)S(1)}, u32[]{:S(2)}) copy-start(bf16[128,16]{0,1:T(8,128)(2,1)S(1)} %convolution_convert_fusion.6) | copy-start | bytes 12292
  262.4 145.3 %copy-start.36 = (bf16[1,1,16,2048]{3,2,1,0:T(8,128)(2,1)}, bf16[1,1,16,2048]{3,2,1,0:T(8,128)(2,1)S(1)}, u32[]{:S(2)}) copy-start(bf16[1,1,16,2048]{3,2,1,0:T(8,128)(2,1)S(1)} %copy.329) | copy-start | bytes 196612
  264.9 221.5 %copy-start.69 = (bf16[128,16]{0,1:T(8,128)(2,1)}, bf16[128,16]{0,1:T(8,128)(2,1)S(1)}, u32[]{:S(2)}) copy-start(bf16[128,16]{0,1:T(8,128)(2,1)S(1)} %convolution_convert_fusion.7) | copy-start | bytes 12292
  267.2 219.3 %copy-start.38 = (bf16[1,1,16,2048]{3,2,1,0:T(8,128)(2,1)}, bf16[1,1,16,2048]{3,2,1,0:T(8,128)(2,1)S(1)}, u32[]{:S(2)}) copy-start(bf16[1,1,16,2048]{3,2,1,0:T(8,128)(2,1)S(1)} %copy.327) | copy-start | bytes 196612
  329.2 165.3 %collective-permute-start = (bf16[128,2048]{1,0:T(8,128)(2,1)S(1)}, bf16[128,2048]{1,0:T(8,128)(2,1)}, u32[]{:S(2)}, u32[]{:S(2)}) collective-permute-start(bf16[128,2048]{1,0:T(8,128)(2,1)S(1)} %fusion.27), channel_id=1, source_target_pairs={{0,1},{1,0},{2,3},{3,2},{4,5},{5,4},{6,7},{7,6},{8,9},{9,8},{10,11... | collective-permute-start | bytes 1572872 | tf_op jit(solution)/shard_map/ppermute | solution.py:21
  494.2 4.2 collective-permute-start.4
  497.0 33.8 %collective-permute-start.1 = (bf16[256,2048]{1,0:T(8,128)(2,1)}, bf16[256,2048]{1,0:T(8,128)(2,1)}, u32[]{:S(2)}, u32[]{:S(2)}) collective-permute-start(bf16[256,2048]{1,0:T(8,128)(2,1)} %maximum_select_fusion.20), channel_id=1, source_target_pairs={{0,2},{1,3},{2,0},{3,1},{4,6},{5,7},{6,4},{7,5},{8,10},{9,11},{10,... | collective-permute-start | bytes 3145736 | tf_op jit(solution)/shard_map/ppermute | solution.py:21
  501.3 64.0 %collective-permute-start.5 = (bf16[256,2048]{1,0:T(8,128)(2,1)}, bf16[256,2048]{1,0:T(8,128)(2,1)}, u32[]{:S(2)}, u32[]{:S(2)}) collective-permute-start(bf16[256,2048]{1,0:T(8,128)(2,1)} %maximum_select_fusion.22), channel_id=1, source_target_pairs={{0,2},{1,3},{2,0},{3,1},{4,6},{5,7},{6,4},{7,5},{8,10},{9,11},{10,... | collective-permute-start | bytes 3145736 | tf_op jit(solution)/shard_map/ppermute | solution.py:21
  535.5 63.8 %collective-permute-start.2 = (bf16[512,2048]{1,0:T(8,128)(2,1)}, bf16[512,2048]{1,0:T(8,128)(2,1)}, u32[]{:S(2)}, u32[]{:S(2)}) collective-permute-start(bf16[512,2048]{1,0:T(8,128)(2,1)} %maximum_select_fusion.6), channel_id=1, source_target_pairs={{0,4},{1,5},{2,6},{3,7},{4,0},{5,1},{6,2},{7,3},{8,12},{9,13},{10,... | collective-permute-start | bytes 6291464 | tf_op jit(solution)/shard_map/ppermute | solution.py:21
  569.9 72.1 %collective-permute-start.6 = (bf16[512,2048]{1,0:T(8,128)(2,1)}, bf16[512,2048]{1,0:T(8,128)(2,1)}, u32[]{:S(2)}, u32[]{:S(2)}) collective-permute-start(bf16[512,2048]{1,0:T(8,128)(2,1)} %maximum_select_fusion.8), channel_id=1, source_target_pairs={{0,4},{1,5},{2,6},{3,7},{4,0},{5,1},{6,2},{7,3},{8,12},{9,13},{10,... | collective-permute-start | bytes 6291464 | tf_op jit(solution)/shard_map/ppermute | solution.py:21
  571.5 260.4 %copy-start.50 = (f32[2048]{0:T(1024)}, f32[2048]{0:T(1024)S(1)}, u32[]{:S(2)}) copy-start(f32[2048]{0:T(1024)S(1)} %convert_element_type.217) | copy-start | bytes 24580
  605.4 93.8 %collective-permute-start.3 = (bf16[1024,2048]{1,0:T(8,128)(2,1)}, bf16[1024,2048]{1,0:T(8,128)(2,1)}, u32[]{:S(2)}, u32[]{:S(2)}) collective-permute-start(bf16[1024,2048]{1,0:T(8,128)(2,1)} %maximum_select_fusion.2), channel_id=1, source_target_pairs={{0,8},{1,9},{2,10},{3,11},{4,12},{5,13},{6,14},{7,15},{8,0},{9,1},... | collective-permute-start | bytes 12582920 | tf_op jit(solution)/shard_map/ppermute | solution.py:21
  647.9 135.8 %collective-permute-start.7 = (bf16[1024,2048]{1,0:T(8,128)(2,1)}, bf16[1024,2048]{1,0:T(8,128)(2,1)}, u32[]{:S(2)}, u32[]{:S(2)}) collective-permute-start(bf16[1024,2048]{1,0:T(8,128)(2,1)} %maximum_select_fusion.4), channel_id=1, source_target_pairs={{0,8},{1,9},{2,10},{3,11},{4,12},{5,13},{6,14},{7,15},{8,0},{9,1},... | collective-permute-start | bytes 12582920 | tf_op jit(solution)/shard_map/ppermute | solution.py:21
  652.2 174.3 %copy-start.40 = (bf16[1,1,2048,16]{2,3,1,0:T(8,128)(2,1)}, bf16[1,1,2048,16]{2,3,1,0:T(8,128)(2,1)S(1)}, u32[]{:S(2)}) copy-start(bf16[1,1,2048,16]{2,3,1,0:T(8,128)(2,1)S(1)} %copy.330) | copy-start | bytes 196612
  654.4 177.0 %copy-start.42 = (bf16[1,1,16,2048]{3,2,1,0:T(8,128)(2,1)}, bf16[1,1,16,2048]{3,2,1,0:T(8,128)(2,1)S(1)}, u32[]{:S(2)}) copy-start(bf16[1,1,16,2048]{3,2,1,0:T(8,128)(2,1)S(1)} %copy.331) | copy-start | bytes 196612
  855.3 376.9 %all-to-all-start = ((bf16[32,128,2048]{2,1,0:T(8,128)(2,1)}), bf16[32,128,2048]{2,1,0:T(8,128)(2,1)}, u32[]{:S(2)}, u32[]{:S(2)}) async-start(bf16[32,128,2048]{2,1,0:T(8,128)(2,1)} %bitcast.332), calls=%async_computation | async-start | bytes 33554432 | tf_op jit(solution)/shard_map/all_to_all | solution.py:201
  1243.0 377.0 %all-to-all-start.2 = ((bf16[32,128,2048]{2,1,0:T(8,128)(2,1)}), bf16[32,128,2048]{2,1,0:T(8,128)(2,1)}, u32[]{:S(2)}, u32[]{:S(2)}) async-start(bf16[32,128,2048]{2,1,0:T(8,128)(2,1)} %bitcast.333), calls=%async_computation.2 | async-start | bytes 33554432 | tf_op jit(solution)/shard_map/all_to_all | solution.py:223
  1620.0 376.7 %all-to-all-start.1 = ((bf16[32,128,2048]{2,1,0:T(8,128)(2,1)}), bf16[32,128,2048]{2,1,0:T(8,128)(2,1)}, u32[]{:S(2)}, u32[]{:S(2)}) async-start(bf16[32,128,2048]{2,1,0:T(8,128)(2,1)} %convolution_convert_fusion), calls=%async_computation.1 | async-start | bytes 33554432 | tf_op jit(solution)/shard_map/all_to_all | solution.py:214
  1688.8 311.8 %copy-start.74 = (s32[1024,1]{0,1:T(1,128)S(1)}, s32[1024,1]{0,1:T(1,128)}, u32[]{:S(2)}) copy-start(s32[1024,1]{0,1:T(1,128)} %compare_select_fusion) | copy-start | bytes 12292
  1688.8 311.9 %copy-start.61 = (f32[16,128]{1,0:T(8,128)S(1)}, f32[16,128]{1,0:T(8,128)}, u32[]{:S(2)}) copy-start(f32[16,128]{1,0:T(8,128)} %copy-done.60) | copy-start | bytes 24580
  1688.8 311.9 %copy-start.63 = (f32[16,128]{1,0:T(8,128)S(1)}, f32[16,128]{1,0:T(8,128)}, u32[]{:S(2)}) copy-start(f32[16,128]{1,0:T(8,128)} %copy-done.62) | copy-start | bytes 24580
  1996.7 376.6 %all-to-all-start.3 = ((bf16[32,128,2048]{2,1,0:T(8,128)(2,1)}), bf16[32,128,2048]{2,1,0:T(8,128)(2,1)}, u32[]{:S(2)}, u32[]{:S(2)}) async-start(bf16[32,128,2048]{2,1,0:T(8,128)(2,1)} %add_convert_fusion), calls=%async_computation.3 | async-start | bytes 33554432 | tf_op jit(solution)/shard_map/all_to_all | solution.py:239
  2000.6 982.8 %reduce-scatter.9.cloned.1.call-start = ((), (), s32[]{:S(2)}) async-start(), calls=%async_computation.13 | async-start | bytes 4325376
  2432.0 127.1 %copy-start.11 = (f32[128,2048]{1,0:T(8,128)}, f32[128,2048]{1,0:T(8,128)S(1)}, u32[]{:S(2)}) copy-start(f32[128,2048]{1,0:T(8,128)S(1)} %get-tuple-element.26) | copy-start | bytes 3145732
  2488.5 93.8 %collective-permute-start.8 = (bf16[8,128,2048]{1,2,0:T(8,128)(2,1)}, bf16[8,128,2048]{1,2,0:T(8,128)(2,1)}, u32[]{:S(2)}, u32[]{:S(2)}) collective-permute-start(bf16[8,128,2048]{1,2,0:T(8,128)(2,1)} %copy.304), channel_id=1, source_target_pairs={{0,8},{1,9},{2,10},{3,11},{4,12},{5,13},{6,14},{7,15},{8,0},{9,1},... | collective-permute-start | bytes 12582920 | tf_op jit(solution)/shard_map/ppermute | solution.py:21
  2512.7 158.1 %collective-permute-start.12 = (bf16[8,128,2048]{1,2,0:T(8,128)(2,1)}, bf16[8,128,2048]{1,2,0:T(8,128)(2,1)}, u32[]{:S(2)}, u32[]{:S(2)}) collective-permute-start(bf16[8,128,2048]{1,2,0:T(8,128)(2,1)} %copy.311), channel_id=1, source_target_pairs={{0,8},{1,9},{2,10},{3,11},{4,12},{5,13},{6,14},{7,15},{8,0},{9,1},... | collective-permute-start | bytes 12582920 | tf_op jit(solution)/shard_map/ppermute | solution.py:21
  2594.0 99.5 %collective-permute-start.9 = (bf16[4,128,2048]{1,2,0:T(8,128)(2,1)S(1)}, bf16[4,128,2048]{1,2,0:T(8,128)(2,1)}, u32[]{:S(2)}, u32[]{:S(2)}) collective-permute-start(bf16[4,128,2048]{1,2,0:T(8,128)(2,1)S(1)} %select_convert_fusion.3), channel_id=1, source_target_pairs={{0,4},{1,5},{2,6},{3,7},{4,0},{5,1},{6,2},{7,3},{8,12},{9,13},{10,... | collective-permute-start | bytes 6291464 | tf_op jit(solution)/shard_map/ppermute | solution.py:21
  2684.5 46.4 %collective-permute-start.13 = (bf16[4,128,2048]{1,2,0:T(8,128)(2,1)S(1)}, bf16[4,128,2048]{1,2,0:T(8,128)(2,1)}, u32[]{:S(2)}, u32[]{:S(2)}) collective-permute-start(bf16[4,128,2048]{1,2,0:T(8,128)(2,1)S(1)} %select_convert_fusion.2), channel_id=1, source_target_pairs={{0,4},{1,5},{2,6},{3,7},{4,0},{5,1},{6,2},{7,3},{8,12},{9,13},{10,... | collective-permute-start | bytes 6291464 | tf_op jit(solution)/shard_map/ppermute | solution.py:21
  2698.3 35.0 %collective-permute-start.10 = (bf16[2,128,2048]{1,2,0:T(8,128)(2,1)S(1)}, bf16[2,128,2048]{1,2,0:T(8,128)(2,1)S(1)}, u32[]{:S(2)}, u32[]{:S(2)}) collective-permute-start(bf16[2,128,2048]{1,2,0:T(8,128)(2,1)S(1)} %select_convert_fusion.5), channel_id=1, source_target_pairs={{0,2},{1,3},{2,0},{3,1},{4,6},{5,7},{6,4},{7,5},{8,10},{9,11},{10,... | collective-permute-start | bytes 3145736 | tf_op jit(solution)/shard_map/ppermute | solution.py:21
  2733.2 22.9 collective-permute-start.14
  2733.7 24.9 collective-permute-start.11
  2758.6 20.9 collective-permute-start.15
  2845.3 277.2 %reduce-scatter.7.cloned.1.call-start = ((), (), s32[]{:S(2)}) async-start(), calls=%async_computation.12 | async-start | bytes 4325376
  2924.5 201.2 %copy-start.1 = (bf16[1,512,2048]{2,1,0:T(8,128)(2,1)S(1)}, bf16[1,512,2048]{2,1,0:T(8,128)(2,1)}, u32[]{:S(2)}) copy-start(bf16[1,512,2048]{2,1,0:T(8,128)(2,1)} %param.36) | copy-start | bytes 6291460
  (73 other events, 1741.5 us)
Sparse Core Ops, SparseCore 0:
  11.4 117.5 all-gather.8
  132.5 113.0 all-gather.10
  248.4 75.7 all-gather.6
  326.9 76.0 all-gather.14
  405.7 76.0 all-gather.12
  484.5 98.9 all-gather.16
  2845.4 137.9 reduce-scatter.8
  2985.7 136.7 reduce-scatter.6
where the time goes:
time: 3150 us; the launch traced here: 3130 us
  waiting for transfers between devices  2290 us (73%)
  local copies, waits for them, and re-layouts  300 us (10%)
  other arithmetic  262 us (8%)
  matrix products  238 us (8%)
    ppermute x16, waiting for transfers between devices, from_partner(): return lax.ppermute(value, axis, pairs)  374 us
    all_to_all x1, waiting for transfers between devices, shards(): lax.all_to_all(spread(jnp.repeat(normed_ffn, TOPK, axis=0)), 'fsdp', spli...  359 us
    all_to_all x1, waiting for transfers between devices, shards(): lax.all_to_all(spread(grad_parts), 'fsdp', split_axis=0, concat_axis=0, t...  324 us
    all_to_all x1, waiting for transfers between devices, shards(): lax.all_to_all(grad_inputs, 'fsdp', split_axis=0, concat_axis=0, tiled=True)  315 us
    all_to_all x1, waiting for transfers between devices, shards(): lax.all_to_all(produced, 'fsdp', split_axis=0, concat_axis=0, tiled=True)  308 us
    unnamed x10, waiting for transfers between devices  192 us
    unnamed x216, local copies, waits for them, and re-layouts  186 us
    all_gather x1, waiting for transfers between devices, shards(): lax.all_gather(adapter_down_factors, 'fsdp', axis=2, tiled=True)  107 us
  transfers between devices with their start and end apart: 28, of which 21 were waited for; matrix products, arithmetic and copies ran while one was open for 18% of the time, Pallas kernels for 0%

commit v1 on v0

--- a/solution.py
+++ b/solution.py
@@ -325,8 +325,230 @@
     )
     return (output, grad_tokens, grad_down, grad_up)
 
+def own_columns(value, axis, groups):
+    return lax.all_to_all(value, axis, split_axis=1, concat_axis=0, tiled=True, axis_index_groups=groups)
+
+
+def heads_plan(
+    tokens,
+    segments,
+    routes,
+    gates,
+    sequence_adapter_index,
+    attention_norm_gain,
+    query_norm_gain,
+    key_norm_gain,
+    query_weight,
+    key_weight,
+    value_weight,
+    output_weight,
+    adapter_down_factors,
+    adapter_up_factors,
+    expert_norm_gain,
+    expert_gate_weight,
+    expert_up_weight,
+    expert_down_weight,
+    output_gradient,
+):
+    bf, f32 = jnp.bfloat16, jnp.float32
+    devices = lax.axis_size("fsdp")
+    rows_dev, width = tokens.shape
+    group = SEQ_LEN // rows_dev
+    seqs = segments.shape[0]
+    experts = devices // 2
+    rank = adapter_down_factors.shape[3]
+    slots = 4 * rank
+    own_rows = query_weight.shape[0]
+    device = lax.axis_index("fsdp")
+    place = device % group
+    sequence = device // group
+    groups = [list(range(s * group, (s + 1) * group)) for s in range(seqs)]
+    scale = 1.0 / math.sqrt(HEAD_DIM)
+    segment_row = pick(segments, sequence)
+    cosine, sine = rope_tables(jnp.arange(SEQ_LEN, dtype=jnp.int32).astype(f32))
+    cosine, sine = cosine[:, 0], sine[:, 0]
+    attn_scale = attention_norm_gain.astype(f32)
+    query_scale = query_norm_gain.astype(f32)
+    key_scale = key_norm_gain.astype(f32)
+    ffn_scale = expert_norm_gain.astype(f32)
+
+    downs = jnp.take(adapter_down_factors, sequence_adapter_index, axis=0)
+    ups = jnp.take(adapter_up_factors, sequence_adapter_index, axis=0)
+    pair = jnp.concatenate(
+        [
+            downs.transpose(2, 0, 1, 3).reshape(own_rows, seqs * slots),
+            ups.transpose(3, 0, 1, 2).reshape(own_rows, seqs * slots),
+        ],
+        axis=1,
+    )
+    factors = lax.all_gather(pair, "fsdp", axis=0, tiled=True)
+    down_own = lax.dynamic_slice_in_dim(factors, sequence * slots, slots, 1)
+    up_own = lax.dynamic_slice_in_dim(factors, (seqs + sequence) * slots, slots, 1)
+    up_head = lax.dynamic_slice_in_dim(up_own, place * HEAD_DIM, HEAD_DIM, 0)
+
+    rows = tokens.astype(f32)
+    normed = rms_scale(rows, attn_scale).astype(bf)
+    normed_all = lax.all_gather(normed, "fsdp", axis=0, tiled=True, axis_index_groups=groups)
+
+    stacked = jnp.concatenate([query_weight, key_weight, value_weight], axis=0)
+    copies = [stacked]
+    for other in range(1, seqs):
+        copies.append(
+            lax.ppermute(
+                stacked, "fsdp", [(i, (i + other * group) % devices) for i in range(devices)]
+            )
+        )
+    mine = own_columns(jnp.concatenate(copies, axis=0), "fsdp", groups)
+    mine = mine.reshape(group, seqs, 3, own_rows, HEAD_DIM)
+    order = (sequence - jnp.arange(seqs)) % seqs
+    mine = jnp.take(mine, order, axis=1).transpose(2, 1, 0, 3, 4).reshape(3, width, HEAD_DIM)
+    output_matrix = lax.all_gather(output_weight, "fsdp", axis=0, tiled=True)
+
+    inner_all = matmul(normed_all, down_own).astype(bf)
+
+    def project(index):
+        inner = inner_all[:, index * rank : (index + 1) * rank]
+        up = up_head[:, index * rank : (index + 1) * rank]
+        return matmul(normed_all, mine[index]) + matmul(inner, up.T)
+
+    query_proj, key_proj, value_proj = project(0), project(1), project(2)
+    query = rotate(rms_scale(query_proj, query_scale), cosine, sine).astype(bf)
+    key = rotate(rms_scale(key_proj, key_scale), cosine, sine).astype(bf)
+    value = value_proj.astype(bf)
+    allowed = segment_row[:, None] == segment_row[None, :]
+    scores = jnp.where(allowed, matmul(query, key.T) * scale, -1e30)
+    maximum = jnp.max(scores, axis=-1, keepdims=True)
+    weights = jnp.exp(scores - maximum)
+    total = jnp.sum(weights, axis=-1, keepdims=True)
+    probs = weights / total
+    probs_low = probs.astype(bf)
+    mixed_head = matmul(probs_low, value).astype(bf)
+    mixed = lax.all_to_all(
+        mixed_head.reshape(group, rows_dev, HEAD_DIM),
+        "fsdp",
+        split_axis=0,
+        concat_axis=0,
+        axis_index_groups=groups,
+        tiled=True,
+    )
+    mixed = mixed.transpose(1, 0, 2).reshape(rows_dev, width)
+    down_out = down_own[:, 3 * rank :]
+    up_out = up_own[:, 3 * rank :]
+    out_inner = matmul(mixed, down_out).astype(bf)
+    middle = rows + matmul(mixed, output_matrix) + matmul(out_inner, up_out.T)
+    normed_ffn = rms_scale(middle, ffn_scale).astype(bf)
+
+    chosen = (routes[:, :, None] == jnp.arange(experts, dtype=jnp.int32)).astype(f32)
+    coeff = jnp.sum(gates[:, :, None] * chosen, axis=1)
+    coeff_all = lax.all_gather(coeff.T, "fsdp", axis=0, tiled=False)
+    coeff_own = lax.dynamic_index_in_dim(coeff_all, device // 2, 1, keepdims=False).reshape(-1, 1)
+    slab_gate = expert_gate_weight[0]
+    slab_up = expert_up_weight[0]
+    slab_down = expert_down_weight[0]
+    upstream_all = lax.all_gather(output_gradient, "fsdp", axis=0, tiled=True)
+    inputs = lax.all_gather(normed_ffn, "fsdp", axis=0, tiled=True)
+    gate_part = matmul(inputs, slab_gate)
+    up_part = matmul(inputs, slab_up)
+    sigmoid = jax.nn.sigmoid(gate_part)
+    hidden = (gate_part * sigmoid * up_part).astype(bf)
+    part = (coeff_own * matmul(hidden, slab_down)).astype(bf)
+    grad_part = (coeff_own * upstream_all.astype(f32)).astype(bf)
+    grad_hidden = matmul(grad_part, slab_down.T)
+    grad_gate = (grad_hidden * up_part * sigmoid * (1.0 + gate_part * (1.0 - sigmoid))).astype(bf)
+    grad_up = (grad_hidden * gate_part * sigmoid).astype(bf)
+    grad_slab = (matmul(grad_gate, slab_gate.T) + matmul(grad_up, slab_up.T)).astype(bf)
+    grad_ffn = lax.psum_scatter(grad_slab, "fsdp", scatter_dimension=0, tiled=True).astype(f32)
+    moe = lax.psum_scatter(part, "fsdp", scatter_dimension=0, tiled=True).astype(f32)
+    output = (middle + moe).astype(bf)
+    upstream = output_gradient.astype(f32)
+    grad_middle = upstream + rms_back(middle, ffn_scale, grad_ffn)
+    grad_attn = grad_middle.astype(bf)
+
+    grad_inner_out = matmul(grad_attn, up_out).astype(bf)
+    grad_mixed = matmul(grad_attn, output_matrix.T) + matmul(grad_inner_out, down_out.T)
+    grad_mixed = own_columns(grad_mixed.astype(bf), "fsdp", groups)
+    up_out_terms = matmul(out_inner.T, grad_attn)
+    down_out_terms = matmul(grad_inner_out.T, mixed)
+
+    grad_probs = matmul(grad_mixed, value.T)
+    grad_scores = (
+        probs * (grad_probs - jnp.sum(probs * grad_probs, axis=-1, keepdims=True))
+    ).astype(bf)
+    grad_query = matmul(grad_scores, key) * scale
+    grad_key = matmul(grad_scores.T, query) * scale
+    grad_value = matmul(probs_low.T, grad_mixed)
+    back = jnp.concatenate(
+        [
+            rms_back(query_proj, query_scale, rotate_back(grad_query, cosine, sine)).astype(bf),
+            rms_back(key_proj, key_scale, rotate_back(grad_key, cosine, sine)).astype(bf),
+            grad_value.astype(bf),
+        ],
+        axis=1,
+    )
+    grad_partial = sum(
+        matmul(back[:, j * HEAD_DIM : (j + 1) * HEAD_DIM], mine[j].T) for j in range(3)
+    ).astype(bf)
+    inner_partial = jnp.concatenate(
+        [
+            matmul(back[:, j * HEAD_DIM : (j + 1) * HEAD_DIM], up_head[:, j * rank : (j + 1) * rank])
+            for j in range(3)
+        ],
+        axis=1,
+    )
+    grad_sum = lax.psum_scatter(
+        grad_partial, "fsdp", scatter_dimension=0, tiled=True, axis_index_groups=groups
+    ).astype(f32)
+    inner_sum = lax.psum_scatter(
+        jnp.pad(inner_partial, ((0, 0), (0, 128 - 3 * rank))),
+        "fsdp",
+        scatter_dimension=0,
+        tiled=True,
+        axis_index_groups=groups,
+    )
+    grad_inner = inner_sum[:, : 3 * rank].astype(bf)
+    grad_normed = grad_sum + matmul(grad_inner, down_own[:, : 3 * rank].T)
+    grad_tokens = (grad_middle + rms_back(rows, attn_scale, grad_normed)).astype(bf)
+
+    up_head_terms = jnp.concatenate(
+        [
+            matmul(
+                inner_all[:, j * rank : (j + 1) * rank].T,
+                back[:, j * HEAD_DIM : (j + 1) * HEAD_DIM],
+            )
+            for j in range(3)
+        ],
+        axis=0,
+    )
+    down_terms = jnp.concatenate([matmul(grad_inner.T, normed), down_out_terms], axis=0)
+    head_slot = (jnp.arange(group) == place).astype(f32)
+    up_terms = jnp.concatenate(
+        [
+            (up_head_terms[:, None, :] * head_slot[None, :, None]).reshape(3 * rank, width),
+            up_out_terms,
+        ],
+        axis=0,
+    )
+    terms = jnp.concatenate([down_terms, up_terms], axis=0)
+    terms = lax.all_to_all(
+        terms.reshape(2 * slots, devices, own_rows).transpose(1, 0, 2),
+        "fsdp",
+        split_axis=0,
+        concat_axis=0,
+        tiled=True,
+    )
+    terms = jnp.sum(terms.reshape(seqs, group, 2 * slots, own_rows), axis=1)
+    selected = (
+        jnp.arange(ADAPTER_COUNT, dtype=jnp.int32)[:, None] == sequence_adapter_index[None, :]
+    ).astype(f32)
+    spread = jnp.sum(selected[:, :, None, None] * terms[None], axis=1)
+    spread = spread.reshape(ADAPTER_COUNT, 2, 4, rank, own_rows)
+    grad_down = spread[:, 0].transpose(0, 1, 3, 2)
+    grad_up = spread[:, 1]
+    return (output, grad_tokens, grad_down, grad_up)
+
 
 def solution(mesh):
+    plan = heads_plan if mesh.shape["fsdp"] == 32 else shards
     in_specs = (
         P("fsdp", None),
         P(),
@@ -354,4 +576,4 @@
         P(None, None, "fsdp", None),
         P(None, None, None, "fsdp"),
     )
-    return jax.shard_map(shards, mesh=mesh, in_specs=in_specs, out_specs=out_specs, check_vma=False)
+    return jax.shard_map(plan, mesh=mesh, in_specs=in_specs, out_specs=out_specs, check_vma=False)

time: 3150 us -> 1160 us (0.37)
  waiting for transfers between devices: 2290 us -> 769 us
  local copies, waits for them, and re-layouts: 300 us -> 16.2 us
  other arithmetic: 262 us -> 49.4 us
  blocking collectives: 0 us -> 40.8 us
    all_to_all x4, waiting for transfers between devices: 1310 us -> 71.1 us  [the longest x2 27.4 us: own_columns(): lax.all_to_all(value, axis, split_axis=1, concat_axis=0, tiled=True, axis...]
    reduce_scatter x0 -> x4, waiting for transfers between devices: none -> 427 us  [the longest x1 185 us: heads_plan(): lax.psum_scatter(part, 'fsdp', scatter_dimension=0, tiled=True).astype(f32)]
    ppermute x16 -> x1, waiting for transfers between devices: 374 us -> 35.2 us  [heads_plan(): lax.ppermute(stacked, 'fsdp', [(i, (i + other * group) % devices) for i i...]
    unnamed x10 -> x9, waiting for transfers between devices: 192 us -> 1.32 us
    dot_general x12 -> x0, matrix products: 191 us -> none  [the longest x1 25.6 us: shards(): jnp.einsum('sch,dh->scd', grad_up, slab_up, preferred_element_type=jnp.fl...]
    unnamed x216 -> x128, local copies, waits for them, and re-layouts: 186 us -> 3.13 us
    all_gather x6 -> x5, waiting for transfers between devices: 415 us -> 234 us  [the longest x1 101 us: heads_plan(): inputs = lax.all_gather(normed_ffn, 'fsdp', axis=0, tiled=True)]
    dot_general x32 -> x35, matrix products: 47.7 us -> 221 us  [matmul(): return jnp.dot(left, right, preferred_element_type=jnp.float32)]
  transfers between devices with their start and end apart: 28 -> 14, of which waited for: 21 -> 13; matrix products, arithmetic and copies ran while one was open for 18% -> 12% of each run, Pallas kernels for 0% -> 1%
where the time goes in v1:
time: 1160 us; the launch traced here: 1150 us
  waiting for transfers between devices  769 us (66%)
  matrix products  224 us (19%)
  other arithmetic  49.4 us (4%)
  blocking collectives  40.8 us (4%)
  starting transfers between devices  23.3 us (2%)
  local copies, waits for them, and re-layouts  16.2 us (1%)
  between operations  15.4 us (1%)
    dot_general x35, matrix products, matmul(): return jnp.dot(left, right, preferred_element_type=jnp.float32)  221 us
    reduce_scatter x1, waiting for transfers between devices, heads_plan(): lax.psum_scatter(part, 'fsdp', scatter_dimension=0, tiled=True).astype(f32)  185 us
    reduce_scatter x1, waiting for transfers between devices, heads_plan(): lax.psum_scatter(grad_slab, 'fsdp', scatter_dimension=0, tiled=True)  163 us
    all_gather x1, waiting for transfers between devices, heads_plan(): inputs = lax.all_gather(normed_ffn, 'fsdp', axis=0, tiled=True)  101 us
    all_gather x1, waiting for transfers between devices, heads_plan(): upstream_all = lax.all_gather(output_gradient, 'fsdp', axis=0, tiled=True)  69.8 us
    reduce_scatter x1, waiting for transfers between devices, heads_plan(): lax.psum_scatter(grad_partial, 'fsdp', scatter_dimension=0, tiled=True, a...  63.7 us
    all_gather x1, waiting for transfers between devices, heads_plan(): lax.all_gather(normed, 'fsdp', axis=0, tiled=True, axis_index_groups=groups)  46.2 us
    all_gather x1, blocking collectives, heads_plan(): coeff_all = lax.all_gather(coeff.T, 'fsdp', axis=0, tiled=False)  40.8 us
  transfers between devices with their start and end apart: 14, of which 13 were waited for; matrix products, arithmetic and copies ran while one was open for 12% of the time, Pallas kernels for 1%

profile of v1, /device:TPU:0, one launch (start us, length us, event | category | flops | bytes accessed | tf_op | source)
XLA Modules:
  0.0 1147.4 jit_solution(6838434227545533501)
XLA Ops:
  19.6 4.1 collective-permute-start
  23.7 35.2 %collective-permute-done = bf16[192,2048]{1,0:T(8,128)(2,1)S(1)} collective-permute-done((bf16[192,2048]{1,0:T(8,128)(2,1)S(1)}, bf16[192,2048]{1,0:T(8,128)(2,1)S(1)}, u32[]{:S(2)}, u32[]{:S(2)}) %collective-permute-start) | collective-permute-done | bytes 786464 | tf_op jit(solution)/shard_map/ppermute | solution.py:397
  58.9 2.7 copy_bitcast_fusion
  61.5 4.4 all-to-all-start
  66.2 25.1 %all-to-all-done = bf16[384,16,128]{2,0,1:T(8,128)(2,1)} async-done(((bf16[384,16,128]{2,0,1:T(8,128)(2,1)}), bf16[384,16,128]{2,0,1:T(8,128)(2,1)}, u32[]{:S(2)}, u32[]{:S(2)}) %all-to-all-start) | async-done | bytes 1572896 | tf_op jit(solution)/shard_map/all_to_all | solution.py:329
  91.3 3.3 gather_fusion
  97.1 46.2 %all-gather.7.cloned.1.call-done = bf16[2048,2048]{1,0:T(8,128)(2,1)} async-done(((bf16[128,2048]{1,0:T(8,128)(2,1)}), bf16[2048,2048]{1,0:T(8,128)(2,1)}) %all-gather.7.cloned.1.call-update) | async-done | bytes 8388624 | tf_op jit(solution)/shard_map/all_gather | solution.py:391
  143.4 6.3 convolution_convert_fusion
  149.7 2.9 fusion.116
  153.8 2.9 fusion.115
  157.9 2.4 fusion.117
  162.8 2.4 fusion.51
  165.2 8.3 fusion.114
  173.6 10.1 online-softmax
  185.9 3.8 all-to-all-start.1
  189.8 18.0 %all-to-all-done.1 = bf16[16,128,128]{1,2,0:T(8,128)(2,1)S(1)} async-done(((bf16[16,128,128]{1,2,0:T(8,128)(2,1)}), bf16[16,128,128]{1,2,0:T(8,128)(2,1)S(1)}, u32[]{:S(2)}, u32[]{:S(2)}) %all-to-all-start.1) | async-done | bytes 524320 | tf_op jit(solution)/shard_map/all_to_all | solution.py:426
  209.6 17.0 %all-gather.11.cloned.1.call-done = bf16[2048,2048]{1,0:T(8,128)(2,1)} async-done(((bf16[64,2048]{1,0:T(8,128)(2,1)}), bf16[2048,2048]{1,0:T(8,128)(2,1)}) %all-gather.11.cloned.1.call-update) | async-done | bytes 8388624 | tf_op jit(solution)/shard_map/all_gather | solution.py:405
  226.7 4.7 convolution_add_fusion.6
  233.1 40.8 %all-gather = f32[512,128]{1,0:T(8,128)S(1)} all-gather(f32[16,128]{1,0:T(8,128)S(1)} %bitcast.128), channel_id=2, replica_groups=mesh['fsdp'=32] {'fsdp'}, dimensions={0}, use_global_device_ids=true | all-gather | bytes 270336 | tf_op jit(solution)/shard_map/all_gather | solution.py:443
  273.8 69.8 %all-gather.15.cloned.1.call-done = bf16[4096,2048]{1,0:T(8,128)(2,1)} async-done(((bf16[128,2048]{1,0:T(8,128)(2,1)}), bf16[4096,2048]{1,0:T(8,128)(2,1)}) %all-gather.15.cloned.1.call-update) | async-done | bytes 16777232 | tf_op jit(solution)/shard_map/all_gather | solution.py:448
  343.6 15.5 %fusion = f32[4096,512]{1,0:T(8,128)} fusion(bf16[4096,2048]{1,0:T(8,128)(2,1)} %all-gather.15.cloned.1.call-done, f32[4096]{0:T(1024)S(1)} %bitcast.129, bf16[1,512,2048]{2,1,0:T(8,128)(2,1)} %param.36), kind=kOutput, calls=%fused_computation.6 | convolution fusion | flops 8615100416 | bytes 27279360 | tf_op jit(solution)/shard_map/dot_general | solution.py:25
  359.1 100.8 %all-gather.13.cloned.1.call-done = bf16[4096,2048]{1,0:T(8,128)(2,1)} async-done(((bf16[128,2048]{1,0:T(8,128)(2,1)}), bf16[4096,2048]{1,0:T(8,128)(2,1)}) %all-gather.13.cloned.1.call-update) | async-done | bytes 16777232 | tf_op jit(solution)/shard_map/all_gather | solution.py:449
  459.9 16.7 %fusion.21 = f32[4096,512]{1,0:T(8,128)} fusion(bf16[4096,2048]{1,0:T(8,128)(2,1)} %all-gather.13.cloned.1.call-done, bf16[1,2048,512]{2,1,0:T(8,128)(2,1)S(1)} %copy-done), kind=kOutput, calls=%fused_computation.44 | convolution fusion | flops 8589934592 | bytes 27262976 | tf_op jit(solution)/shard_map/dot_general | solution.py:25
  476.6 11.1 fusion.18
  487.7 24.6 %fusion.6 = f32[4096,2048]{1,0:T(8,128)} fusion(f32[4096,512]{1,0:T(8,128)} %fusion.21, f32[4096,512]{1,0:T(8,128)} %fusion, f32[4096,512]{1,0:T(8,128)} %fusion.18, bf16[1,2048,512]{2,1,0:T(8,128)(2,1)S(1)} %copy-done), kind=kOutput, calls=%fused_computation.21 | convolution fusion | flops 8610906112 | bytes 60817408 | tf_op jit(solution)/shard_map/dot_general | solution.py:25
  512.3 25.2 %add_convert_fusion = bf16[4096,2048]{1,0:T(8,128)(2,1)} fusion(f32[4096,2048]{1,0:T(8,128)} %fusion.6, f32[4096,512]{1,0:T(8,128)} %fusion, f32[4096,512]{1,0:T(8,128)} %fusion.21, bf16[1,2048,512]{2,1,0:T(8,128)(2,1)S(1)} %copy-done.56), kind=kOutput, calls=%fused_computation.3 | convolution fusion | flops 8619294720 | bytes 69206016 | tf_op jit(solution)/shard_map/dot_general | solution.py:25
  539.1 16.7 %multiply_convert_fusion.1 = bf16[4096,2048]{1,0:T(8,128)(2,1)} fusion(f32[4096]{0:T(1024)S(1)} %bitcast.130, f32[4096,512]{1,0:T(8,128)} %fusion.18, f32[4096,512]{1,0:T(8,128)} %fusion.21, bf16[1,512,2048]{2,1,0:T(8,128)(2,1)S(1)} %copy-done.57), kind=kOutput, calls=%fused_computation.5 | convolution fusion | flops 8619294720 | bytes 35667968 | tf_op jit(solution)/shard_map/dot_general | solution.py:25
  555.8 162.8 %reduce-scatter.7.cloned.1.call-done = bf16[128,2048]{1,0:T(8,128)(2,1)} async-done(((bf16[4096,2048]{1,0:T(8,128)(2,1)}), bf16[128,2048]{1,0:T(8,128)(2,1)}) %reduce-scatter.7.cloned.1.call-update) | async-done | bytes 524304 | tf_op jit(solution)/shard_map/reduce_scatter | solution.py:460
  720.0 185.5 %reduce-scatter.5.cloned.1.call-done = bf16[128,2048]{1,0:T(8,128)(2,1)} async-done(((bf16[4096,2048]{1,0:T(8,128)(2,1)}), bf16[128,2048]{1,0:T(8,128)(2,1)}) %reduce-scatter.5.cloned.1.call-update) | async-done | bytes 524304 | tf_op jit(solution)/shard_map/reduce_scatter | solution.py:461
  905.5 2.5 multiply_add_fusion
  908.0 6.6 fusion.107
  916.7 6.9 all-to-all-start.2
  923.7 8.1 fusion.3
  931.8 2.4 all-to-all-done.2
  934.2 11.1 fusion.12
  945.3 13.5 %multiply_reduce_fusion = (f32[2048]{0:T(1024)}, f32[2048,2048]{1,0:T(8,128)}) fusion(f32[2048]{0:T(1024)S(1)} %fusion.3, f32[2048,2048]{1,0:T(8,128)} %get-tuple-element.30, f32[2048]{0:T(1024)S(1)} %copy-done.41, bf16[2048,128]{1,0:T(8,128)(2,1)S(1)} %bitcast.124, f32[2048,128]{1,0:T(8,128)S(1)} %copy-done.19), kind=kOutput, calls=%fused_computation.9 | convolution fusion | flops 1090779136 | bytes 35151872 | tf_op jit(solution)/shard_map/dot_general | solution.py:25
  958.8 8.2 multiply_convert_fusion.3
  968.6 2.9 convolution_multiply_fusion.1
  971.5 2.4 fusion.60
  979.8 9.2 fusion.119
  989.1 8.1 fusion.118
  997.2 15.6 %add_convert_fusion.1 = bf16[2048,2048]{1,0:T(8,128)(2,1)} fusion(f32[2048,2048]{1,0:T(8,128)} %fusion.118, f32[2048,2048]{1,0:T(8,128)} %fusion.119, bf16[2048,128]{1,0:T(8,128)(2,1)S(1)} %copy-done.15, bf16[2048,128]{1,0:T(8,128)(2,1)} %bitcast.119), kind=kOutput, calls=%fused_computation.7 | convolution fusion | flops 1086324736 | bytes 42991616 | tf_op jit(solution)/shard_map/dot_general | solution.py:25
  1018.4 15.4 %reduce-scatter.11.cloned.1.call-done = f32[128,128]{0,1:T(8,128)} async-done(((f32[2048,128]{0,1:T(8,128)}), f32[128,128]{0,1:T(8,128)}) %reduce-scatter.11.cloned.1.call-update) | async-done | bytes 65552 | tf_op jit(solution)/shard_map/reduce_scatter | solution.py:501
  1035.4 3.8 maximum_bitcast_fusion.1
  1039.2 3.4 all-to-all-start.3
  1042.6 25.7 %all-to-all-done.3 = f32[32,128,64]{1,2,0:T(8,128)} async-done(((f32[32,128,64]{1,2,0:T(8,128)}), f32[32,128,64]{1,2,0:T(8,128)}, u32[]{:S(2)}, u32[]{:S(2)}) %all-to-all-start.3) | async-done | bytes 1048608 | tf_op jit(solution)/shard_map/all_to_all | solution.py:532
  1072.6 63.7 %reduce-scatter.9.cloned.1.call-done = bf16[128,2048]{1,0:T(8,128)(2,1)} async-done(((bf16[2048,2048]{1,0:T(8,128)(2,1)}), bf16[128,2048]{1,0:T(8,128)(2,1)}) %reduce-scatter.9.cloned.1.call-update) | async-done | bytes 524304 | tf_op jit(solution)/shard_map/reduce_scatter | solution.py:498
  1138.2 2.2 fusion.32
  (223 shorter events, 51.0 us)
Async XLA Ops:
  7.2 452.8 %copy-start = (bf16[1,2048,512]{2,1,0:T(8,128)(2,1)S(1)}, bf16[1,2048,512]{2,1,0:T(8,128)(2,1)}, u32[]{:S(2)}) copy-start(bf16[1,2048,512]{2,1,0:T(8,128)(2,1)} %param.34) | copy-start | bytes 6291460
  7.2 58.8 %copy-start.58 = (bf16[128]{0:T(256)(128)(2,1)S(1)}, bf16[128]{0:T(256)(128)(2,1)}, u32[]{:S(2)}) copy-start(bf16[128]{0:T(256)(128)(2,1)} %param.25) | copy-start | bytes 772
  7.2 58.8 %copy-start.59 = (bf16[128]{0:T(256)(128)(2,1)S(1)}, bf16[128]{0:T(256)(128)(2,1)}, u32[]{:S(2)}) copy-start(bf16[128]{0:T(256)(128)(2,1)} %param.26) | copy-start | bytes 772
  7.2 59.0 %copy-start.49 = (s32[2,2048]{1,0:T(2,128)S(1)}, s32[2,2048]{1,0:T(2,128)}, u32[]{:S(2)}) copy-start(s32[2,2048]{1,0:T(2,128)} %param.20) | copy-start | bytes 49156
  7.2 89.9 %all-gather.9.cloned.1.call-start = ((), (), s32[]{:S(2)}) async-start(), calls=%async_computation.9 | async-start | bytes 1081344 | tf_op jit(solution)/shard_map/all_gather | solution.py:384
  12.6 130.8 %all-gather.7.cloned.1.call-start = ((), (), s32[]{:S(2)}) async-start(), calls=%async_computation.8 | async-start | bytes 8912896 | tf_op jit(solution)/shard_map/all_gather | solution.py:391
  17.1 209.5 %all-gather.11.cloned.1.call-start = ((), (), s32[]{:S(2)}) async-start(), calls=%async_computation.10 | async-start | bytes 8650752 | tf_op jit(solution)/shard_map/all_gather | solution.py:405
  17.9 325.7 %all-gather.15.cloned.1.call-start = ((), (), s32[]{:S(2)}) async-start(), calls=%async_computation.13 | async-start | bytes 17301504 | tf_op jit(solution)/shard_map/all_gather | solution.py:448
  19.6 39.3 %collective-permute-start = (bf16[192,2048]{1,0:T(8,128)(2,1)S(1)}, bf16[192,2048]{1,0:T(8,128)(2,1)S(1)}, u32[]{:S(2)}, u32[]{:S(2)}) collective-permute-start(bf16[192,2048]{1,0:T(8,128)(2,1)S(1)} %pad_maximum_fusion), channel_id=1, source_target_pairs={{0,16},{1,17},{2,18},{3,19},{4,20},{5,21},{6,22},{7,23},{8,24},{9,... | collective-permute-start | bytes 2359304 | tf_op jit(solution)/shard_map/ppermute | solution.py:397
  61.5 29.8 %all-to-all-start = ((bf16[384,16,128]{2,0,1:T(8,128)(2,1)}), bf16[384,16,128]{2,0,1:T(8,128)(2,1)}, u32[]{:S(2)}, u32[]{:S(2)}) async-start(bf16[384,16,128]{2,0,1:T(8,128)(2,1)} %copy_bitcast_fusion), calls=%async_computation | async-start | bytes 3145728 | tf_op jit(solution)/shard_map/all_to_all | solution.py:329
  66.0 96.4 %copy-start.44 = (f32[128]{0:T(128)}, f32[128]{0:T(128)S(1)}, u32[]{:S(2)}) copy-start(f32[128]{0:T(128)S(1)} %convert_element_type.160) | copy-start | bytes 1540
  66.1 96.4 %copy-start.46 = (f32[128]{0:T(128)}, f32[128]{0:T(128)S(1)}, u32[]{:S(2)}) copy-start(f32[128]{0:T(128)S(1)} %convert_element_type.162) | copy-start | bytes 1540
  66.1 96.7 %copy-start.52 = (f32[64]{0:T(128)}, f32[64]{0:T(128)S(1)}, u32[]{:S(2)}) copy-start(f32[64]{0:T(128)S(1)} %negate_power_fusion) | copy-start | bytes 772
  66.2 96.6 %copy-start.37 = (f32[2048]{0:T(1024)}, f32[2048]{0:T(1024)S(1)}, u32[]{:S(2)}) copy-start(f32[2048]{0:T(1024)S(1)} %iota_convert_fusion) | copy-start | bytes 24580
  97.1 55.5 %copy-start.18 = (bf16[1,2,16,64,128]{4,3,0,2,1:T(8,128)(2,1)}, bf16[1,2,16,64,128]{4,3,0,2,1:T(8,128)(2,1)S(1)}, u32[]{:S(2)}) copy-start(bf16[1,2,16,64,128]{4,3,0,2,1:T(8,128)(2,1)S(1)} %get-tuple-element.5) | copy-start | bytes 1572868
  97.1 56.7 %copy-start.16 = (bf16[1,2,16,64,128]{4,3,0,2,1:T(8,128)(2,1)}, bf16[1,2,16,64,128]{4,3,0,2,1:T(8,128)(2,1)S(1)}, u32[]{:S(2)}) copy-start(bf16[1,2,16,64,128]{4,3,0,2,1:T(8,128)(2,1)S(1)} %get-tuple-element.6) | copy-start | bytes 1572868
  149.7 10.6 copy-start.20
  153.7 8.7 copy-start.7
  173.6 16.2 %copy-start.48 = (bf16[2048]{0:T(1024)(128)(2,1)S(1)}, bf16[2048]{0:T(1024)(128)(2,1)}, u32[]{:S(2)}) copy-start(bf16[2048]{0:T(1024)(128)(2,1)} %param.33) | copy-start | bytes 12292
  173.6 53.1 %copy-start.9 = (bf16[128,2048]{1,0:T(8,128)(2,1)S(1)}, bf16[128,2048]{1,0:T(8,128)(2,1)}, u32[]{:S(2)}) copy-start(bf16[128,2048]{1,0:T(8,128)(2,1)} %param.19) | copy-start | bytes 1572868
  185.9 21.9 %all-to-all-start.1 = ((bf16[16,128,128]{1,2,0:T(8,128)(2,1)}), bf16[16,128,128]{1,2,0:T(8,128)(2,1)S(1)}, u32[]{:S(2)}, u32[]{:S(2)}) async-start(bf16[16,128,128]{1,2,0:T(8,128)(2,1)} %copy.80), calls=%async_computation.1 | async-start | bytes 1048576 | tf_op jit(solution)/shard_map/all_to_all | solution.py:426
  189.8 270.2 %all-gather.13.cloned.1.call-start = ((), (), s32[]{:S(2)}) async-start(), calls=%async_computation.11 | async-start | bytes 17301504 | tf_op jit(solution)/shard_map/all_gather | solution.py:449
  207.8 18.8 %copy-start.10 = (bf16[16,128,128]{1,2,0:T(8,128)(2,1)}, bf16[16,128,128]{1,2,0:T(8,128)(2,1)S(1)}, u32[]{:S(2)}) copy-start(bf16[16,128,128]{1,2,0:T(8,128)(2,1)S(1)} %all-to-all-done.1) | copy-start | bytes 1572868
  209.6 21.8 %copy-start.39 = (bf16[128,16]{0,1:T(8,128)(2,1)}, bf16[128,16]{0,1:T(8,128)(2,1)S(1)}, u32[]{:S(2)}) copy-start(bf16[128,16]{0,1:T(8,128)(2,1)S(1)} %convolution_convert_fusion.2) | copy-start | bytes 12292
  209.6 23.4 %copy-start.50 = (f32[128,8]{0,1:T(8,128)S(1)}, f32[128,8]{0,1:T(8,128)}, u32[]{:S(2)}) copy-start(f32[128,8]{0,1:T(8,128)} %param.22) | copy-start | bytes 12292
  209.6 23.4 %copy-start.51 = (s32[128,8]{0,1:T(8,128)S(1)}, s32[128,8]{0,1:T(8,128)}, u32[]{:S(2)}) copy-start(s32[128,8]{0,1:T(8,128)} %param.21) | copy-start | bytes 12292
  232.9 485.7 %reduce-scatter.7.cloned.1.call-start = ((), (), s32[]{:S(2)}) async-start(), calls=%async_computation.14 | async-start | bytes 17301504 | tf_op jit(solution)/shard_map/reduce_scatter | solution.py:460
  459.9 16.7 %copy-start.55 = (bf16[4096,2048]{1,0:T(8,128)(2,1)S(1)}, bf16[4096,2048]{1,0:T(8,128)(2,1)}, u32[]{:S(2)}) copy-start(bf16[4096,2048]{1,0:T(8,128)(2,1)} %all-gather.13.cloned.1.call-done) | copy-start | bytes 50331652
  459.9 16.7 %copy-start.56 = (bf16[1,2048,512]{2,1,0:T(8,128)(2,1)S(1)}, bf16[1,2048,512]{2,1,0:T(8,128)(2,1)}, u32[]{:S(2)}) copy-start(bf16[1,2048,512]{2,1,0:T(8,128)(2,1)} %param.35) | copy-start | bytes 6291460
  537.6 367.9 %reduce-scatter.5.cloned.1.call-start = ((), (), s32[]{:S(2)}) async-start(), calls=%async_computation.12 | async-start | bytes 17301504 | tf_op jit(solution)/shard_map/reduce_scatter | solution.py:461
  555.8 358.8 %copy-start.13 = (bf16[2048,256]{1,0:T(8,128)(2,1)S(1)}, bf16[2048,256]{1,0:T(8,128)(2,1)}, u32[]{:S(2)}) copy-start(bf16[2048,256]{1,0:T(8,128)(2,1)} %all-gather.9.cloned.1.call-done) | copy-start | bytes 3145732
  908.0 107.1 %copy-start.3 = (f32[128,2048]{1,0:T(8,128)}, f32[128,2048]{1,0:T(8,128)S(1)}, u32[]{:S(2)}) copy-start(f32[128,2048]{1,0:T(8,128)S(1)} %get-tuple-element.15) | copy-start | bytes 3145732
  908.0 15.7 %copy-start.41 = (f32[2048]{0:T(1024)S(1)}, f32[2048]{0:T(1024)}, u32[]{:S(2)}) copy-start(f32[2048]{0:T(1024)} %get-tuple-element.29) | copy-start | bytes 24580
  916.7 17.5 %all-to-all-start.2 = ((bf16[128,16,128]{2,0,1:T(8,128)(2,1)}), bf16[128,16,128]{2,0,1:T(8,128)(2,1)S(1)}, u32[]{:S(2)}, u32[]{:S(2)}) async-start(bf16[128,16,128]{2,0,1:T(8,128)(2,1)} %bitcast.106), calls=%async_computation.4 | async-start | bytes 1048576 | tf_op jit(solution)/shard_map/all_to_all | solution.py:329
  923.6 110.2 %reduce-scatter.11.cloned.1.call-start = ((), (), s32[]{:S(2)}) async-start(), calls=%async_computation.16 | async-start | bytes 1114112 | tf_op jit(solution)/shard_map/reduce_scatter | solution.py:501
  934.2 11.1 copy-start.19
  934.2 24.6 %slice-start = ((s8[16777216]{0:T(1024)(128)(4,1)}), s8[4194304]{0:T(1024)(128)(4,1)S(1)}, s32[]{:S(2)}) async-start(s8[16777216]{0:T(1024)(128)(4,1)} %bitcast.107), calls=%async_computation.17 | async-start | bytes 8388608
  934.2 24.6 %slice-start.1 = ((s8[16777216]{0:T(1024)(128)(4,1)}), s8[4194304]{0:T(1024)(128)(4,1)S(1)}, s32[]{:S(2)}) async-start(s8[16777216]{0:T(1024)(128)(4,1)} %bitcast.107), calls=%async_computation.18 | async-start | bytes 8388608
  945.3 13.5 %slice-start.2 = ((s8[16777216]{0:T(1024)(128)(4,1)}), s8[4194304]{0:T(1024)(128)(4,1)S(1)}, s32[]{:S(2)}) async-start(s8[16777216]{0:T(1024)(128)(4,1)} %bitcast.107), calls=%async_computation.19 | async-start | bytes 8388608
  945.3 13.5 %slice-start.3 = ((s8[16777216]{0:T(1024)(128)(4,1)}), s8[4194304]{0:T(1024)(128)(4,1)S(1)}, s32[]{:S(2)}) async-start(s8[16777216]{0:T(1024)(128)(4,1)} %bitcast.107), calls=%async_computation.20 | async-start | bytes 8388608
  979.5 9.6 copy-start.17
  979.5 156.7 %reduce-scatter.9.cloned.1.call-start = ((), (), s32[]{:S(2)}) async-start(), calls=%async_computation.15 | async-start | bytes 8912896 | tf_op jit(solution)/shard_map/reduce_scatter | solution.py:498
  1015.1 27.5 %copy-start.54 = (s32[2]{0:T(128)S(1)}, s32[2]{0:T(128)}, u32[]{:S(2)}) copy-start(s32[2]{0:T(128)} %param.23) | copy-start | bytes 28
  1016.6 119.7 %copy-start.36 = (f32[2048]{0:T(1024)S(1)}, f32[2048]{0:T(1024)}, u32[]{:S(2)}) copy-start(f32[2048]{0:T(1024)} %copy-done.35) | copy-start | bytes 24580
  1016.6 119.7 %copy-start.43 = (f32[128]{0:T(128)S(1)}, f32[128]{0:T(128)}, u32[]{:S(2)}) copy-start(f32[128]{0:T(128)} %copy-done.42) | copy-start | bytes 1540
  1017.3 120.9 %copy-start.4 = (f32[128,2048]{1,0:T(8,128)S(1)}, f32[128,2048]{1,0:T(8,128)}, u32[]{:S(2)}) copy-start(f32[128,2048]{1,0:T(8,128)} %copy-done.3) | copy-start | bytes 3145732
  1033.8 106.6 %copy-start.1 = (bf16[1,2048,512]{2,1,0:T(8,128)(2,1)S(1)}, bf16[1,2048,512]{2,1,0:T(8,128)(2,1)}, u32[]{:S(2)}) copy-start(bf16[1,2048,512]{2,1,0:T(8,128)(2,1)} %param.34) | copy-start | bytes 6291460
  1039.2 29.1 %all-to-all-start.3 = ((f32[32,128,64]{1,2,0:T(8,128)}), f32[32,128,64]{1,2,0:T(8,128)}, u32[]{:S(2)}, u32[]{:S(2)}) async-start(f32[32,128,64]{1,2,0:T(8,128)} %maximum_bitcast_fusion.1), calls=%async_computation.7 | async-start | bytes 2097152 | tf_op jit(solution)/shard_map/all_to_all | solution.py:532
  (30 other events, 148.4 us)
Sparse Core Ops, SparseCore 0:
  12.7 79.2 all-gather.8
  94.1 49.2 all-gather.6
  146.2 80.3 all-gather.10
  229.4 114.1 all-gather.14
  346.9 113.0 all-gather.12
  537.7 180.9 reduce-scatter.6
  720.9 184.4 reduce-scatter.4
  979.6 54.1 reduce-scatter.10
  1036.3 99.9 reduce-scatter.8

commit v2 on v1

--- a/solution.py
+++ b/solution.py
@@ -1,8 +1,11 @@
+import functools
 import math
 
 import jax
 import jax.numpy as jnp
 from jax import lax
+from jax.experimental import pallas as pl
+from jax.experimental.pallas import tpu as pltpu
 from jax.sharding import PartitionSpec as P
 
 HEAD_DIM = 128
@@ -324,6 +327,431 @@
         lax.psum_scatter(selected * up_terms[None], "fsdp", scatter_dimension=3, tiled=True),
     )
     return (output, grad_tokens, grad_down, grad_up)
+
+
+MESH = pl.DeviceIdType.MESH
+LEVELS = 4
+CHIPS = 16
+
+
+class Place:
+    def __init__(self):
+        self.me = me = lax.axis_index("fsdp")
+        self.core = me % 2
+        self.x = me // 2 % 2
+        self.y = me // 4 % 2
+        self.z = me // 8
+        self.sibling = me + 1 - 2 * self.core
+        self.across_x = me + 2 - 4 * self.x
+        self.across_y = me + 4 - 8 * self.y
+
+    def level(self, i):
+        upper = self.z // 2
+        inner = self.z * (1 - upper) + (3 - self.z) * upper
+        turn = i + inner * (1 - 2 * i) * (1 - i // 2)
+        return turn + upper * (3 - 2 * turn)
+
+    def chip(self, half, side, level):
+        flip = 1 - 2 * side
+        y = self.y + (1 - half) * side * (1 - 2 * self.y)
+        x = self.x + half * side * (1 - 2 * self.x)
+        return level * 4 + y * 2 + x
+
+    def chip_at(self, dx, dy, level):
+        y = self.y + dy * (1 - 2 * self.y)
+        x = self.x + dx * (1 - 2 * self.x)
+        return level * 4 + y * 2 + x
+
+    def first(self, half):
+        return self.across_y * (1 - half) + self.across_x * half
+
+    def last(self, half):
+        return self.across_x * (1 - half) + self.across_y * half
+
+
+def scatter_kernel(rows, work, source, out, own, sib, cross_out, cross_in, z_out, z_in, first_out, first_in, total,
+                   own_sem, sib_send, sib_recv, cross_send, cross_recv, z_send, z_recv, first_send, first_recv):
+    place = Place()
+    half_rows = rows // 2
+    f32, bf = jnp.float32, jnp.bfloat16
+
+    def local(o):
+        return pltpu.make_async_copy(source.at[2 * o + place.core], own.at[o], own_sem.at[o])
+
+    def to_sibling(o):
+        return pltpu.make_async_remote_copy(
+            src_ref=source.at[2 * o + 1 - place.core], dst_ref=sib.at[o], send_sem=sib_send.at[o],
+            recv_sem=sib_recv.at[o], device_id=(place.sibling,), device_id_type=MESH)
+
+    def across(h, k, level):
+        return pltpu.make_async_remote_copy(
+            src_ref=cross_out.at[h, k, level], dst_ref=cross_in.at[h, k, level], send_sem=cross_send.at[h, k, level],
+            recv_sem=cross_recv.at[h, k, level], device_id=(place.last(h),), device_id_type=MESH)
+
+    def along(h, k, level, up):
+        return pltpu.make_async_remote_copy(
+            src_ref=z_out.at[h, k, level], dst_ref=z_in.at[up, h, k, level], send_sem=z_send.at[h, k, level],
+            recv_sem=z_recv.at[up, h, k, level], device_id=(place.me - 8 + 16 * up,), device_id_type=MESH)
+
+    def first(h):
+        return pltpu.make_async_remote_copy(
+            src_ref=first_out.at[h], dst_ref=first_in.at[h], send_sem=first_send.at[h],
+            recv_sem=first_recv.at[h], device_id=(place.first(h),), device_id_type=MESH)
+
+    def both(o, h):
+        part = pl.ds(h * half_rows, half_rows)
+        return own[o, part].astype(f32) + sib[o, part].astype(f32)
+
+    @pl.loop(0, CHIPS)
+    def _(q):
+        o = place.chip_at(q % 2, q // 2 % 2, place.level(3 - q // 4))
+        local(o).start()
+        to_sibling(o).start()
+
+    @pl.loop(0, CHIPS + 4)
+    def _(t):
+        @pl.when(t < CHIPS)
+        def _():
+            level = place.level(3 - t // 4)
+            dx, dy = t % 2, t // 2 % 2
+            o = place.chip_at(dx, dy, level)
+            local(o).wait()
+            to_sibling(o).wait_recv()
+            for h, away, k in ((0, dx, dy), (1, dy, dx)):
+                @pl.when(away == 1)
+                def _():
+                    cross_out[h, k, level] = both(o, h).astype(bf)
+                    across(h, k, level).start()
+
+        @pl.when(t >= 4)
+        def _():
+            i, h, k = (t - 4) // 4, t % 2, t // 2 % 2
+            level = place.level(3 - i)
+            o = place.chip(h, k, level)
+            across(h, k, level).wait_recv()
+            total[...] = both(o, h) + cross_in[h, k, level].astype(f32)
+
+            @pl.when((level >= place.z) & (place.z > 0))
+            def _():
+                along(h, k, level, 1).wait_recv()
+                total[...] += z_in[1, h, k, level].astype(f32)
+
+            @pl.when((level <= place.z) & (place.z < LEVELS - 1))
+            def _():
+                along(h, k, level, 0).wait_recv()
+                total[...] += z_in[0, h, k, level].astype(f32)
+
+            @pl.when(level > place.z)
+            def _():
+                z_out[h, k, level] = total[...].astype(bf)
+                along(h, k, level, 1).start()
+
+            @pl.when(level < place.z)
+            def _():
+                z_out[h, k, level] = total[...].astype(bf)
+                along(h, k, level, 0).start()
+
+            @pl.when((level == place.z) & (k == 1))
+            def _():
+                first_out[h] = total[...].astype(bf)
+                first(h).start()
+
+            @pl.when((level == place.z) & (k == 0))
+            def _():
+                out[pl.ds(h * half_rows, half_rows)] = total[...]
+
+        if work is not None:
+            work(t)
+
+    for h in range(2):
+        first(h).wait_recv()
+        out[pl.ds(h * half_rows, half_rows)] += first_in[h].astype(f32)
+
+    @pl.loop(0, CHIPS)
+    def _(q):
+        o = place.chip_at(q % 2, q // 2 % 2, place.level(3 - q // 4))
+        to_sibling(o).wait_send()
+        h, k, level = q % 2, q // 2 % 2, q // 4
+        across(h, k, level).wait_send()
+
+        @pl.when(level > place.z)
+        def _():
+            along(h, k, level, 1).wait_send()
+
+        @pl.when(level < place.z)
+        def _():
+            along(h, k, level, 0).wait_send()
+
+    for h in range(2):
+        first(h).wait_send()
+
+
+def scatter_scratch(rows, width):
+    bf = jnp.bfloat16
+    dma = pltpu.SemaphoreType.DMA
+    piece = (rows // 2, width)
+    return [
+        pltpu.VMEM((CHIPS, rows, width), bf),
+        pltpu.VMEM((CHIPS, rows, width), bf),
+        pltpu.VMEM((2, 2, LEVELS) + piece, bf),
+        pltpu.VMEM((2, 2, LEVELS) + piece, bf),
+        pltpu.VMEM((2, 2, LEVELS) + piece, bf),
+        pltpu.VMEM((2, 2, 2, LEVELS) + piece, bf),
+        pltpu.VMEM((2,) + piece, bf),
+        pltpu.VMEM((2,) + piece, bf),
+        pltpu.VMEM(piece, jnp.float32),
+        dma((CHIPS,)), dma((CHIPS,)), dma((CHIPS,)),
+        dma((2, 2, LEVELS)), dma((2, 2, LEVELS)),
+        dma((2, 2, LEVELS)), dma((2, 2, 2, LEVELS)),
+        dma((2,)), dma((2,)),
+    ]
+
+
+def scatter_all(partial):
+    devices, rows, width = partial.shape
+    return pl.pallas_call(
+        functools.partial(scatter_kernel, rows, None),
+        out_shape=jax.ShapeDtypeStruct((rows, width), jnp.float32),
+        in_specs=[pl.BlockSpec(memory_space=pl.ANY)],
+        out_specs=pl.BlockSpec(memory_space=pltpu.VMEM),
+        scratch_shapes=scatter_scratch(rows, width),
+        compiler_params=pltpu.CompilerParams(has_side_effects=True, vmem_limit_bytes=48 << 20),
+        name="scatter_all",
+    )(partial)
+
+
+def expert_kernel(rows, x_ref, gate_w, up_w, down_w, coeff, part_out, a_out, b_out,
+                  held, part_buf, a_buf, b_buf, own_sem, send, recv, out_sem):
+    place = Place()
+    half_rows = rows // 2
+    f32, bf = jnp.float32, jnp.bfloat16
+    me = place.me
+    UP, DOWN, LAST, SIB, FIRST = range(5)
+
+    def move(h, o, kind, target):
+        d = 2 * o + place.core
+        part = pl.ds(h * half_rows, half_rows)
+        return pltpu.make_async_remote_copy(
+            src_ref=held.at[d, part], dst_ref=held.at[d, part], send_sem=send.at[kind, h, o],
+            recv_sem=recv.at[1 if kind == SIB else 0, h, o], device_id=(target,), device_id_type=MESH)
+
+    def arrived(h, o, sib):
+        d = 2 * o + (1 - place.core if sib else place.core)
+        part = pl.ds(h * half_rows, half_rows)
+        pltpu.make_async_remote_copy(
+            src_ref=held.at[d, part], dst_ref=held.at[d, part], send_sem=send.at[SIB, h, o],
+            recv_sem=recv.at[1 if sib else 0, h, o], device_id=(place.sibling,), device_id_type=MESH).wait_recv()
+
+    def spread(h, o, level, act):
+        @pl.when((level <= place.z) & (place.z < LEVELS - 1))
+        def _():
+            act(move(h, o, UP, me + 8))
+
+        @pl.when((level >= place.z) & (place.z > 0))
+        def _():
+            act(move(h, o, DOWN, me - 8))
+
+        act(move(h, o, LAST, place.last(h)))
+        act(move(h, o, SIB, place.sibling))
+
+    start = lambda copy: copy.start()
+    done = lambda copy: copy.wait_send()
+    own = pltpu.make_async_copy(x_ref, held.at[me], own_sem)
+    own.start()
+    own.wait()
+    mine = me // 2
+    for h in range(2):
+        move(h, mine, FIRST, place.first(h)).start()
+        spread(h, mine, place.z, start)
+    for h in range(2):
+        o = place.chip(h, 1, place.z)
+        arrived(h, o, False)
+        spread(h, o, place.z, start)
+
+    def cross(q):
+        level, dx, dy = place.level(q // 4), q % 2, q // 2 % 2
+        o = place.chip_at(dx, dy, level)
+        for h, away in ((0, dx), (1, dy)):
+            @pl.when(away == 1)
+            def _():
+                arrived(h, o, False)
+                move(h, o, SIB, place.sibling).start()
+
+    def outputs(t, slot):
+        o = place.chip_at(t % 2, t // 2 % 2, place.level(t // 4))
+        two = pl.ds(2 * o, 2)
+        return (
+            pltpu.make_async_copy(part_buf.at[slot], part_out.at[two], out_sem.at[slot, 0]),
+            pltpu.make_async_copy(a_buf.at[slot], a_out.at[two], out_sem.at[slot, 1]),
+            pltpu.make_async_copy(b_buf.at[slot], b_out.at[two], out_sem.at[slot, 2]),
+        )
+
+    @pl.loop(0, CHIPS)
+    def _(t):
+        @pl.when(t < CHIPS - 4)
+        def _():
+            level, h, k = place.level(1 + t // 4), t % 2, t // 2 % 2
+            o = place.chip(h, k, level)
+            arrived(h, o, False)
+            spread(h, o, level, start)
+
+        @pl.when(t + 1 < CHIPS)
+        def _():
+            cross(t + 1)
+
+        o = place.chip_at(t % 2, t // 2 % 2, place.level(t // 4))
+        for h in range(2):
+            arrived(h, o, True)
+        slot = t % 2
+
+        @pl.when(t >= 2)
+        def _():
+            for copy in outputs(t - 2, slot):
+                copy.wait()
+
+        x = held[pl.ds(2 * o, 2)].reshape(2 * rows, -1)
+        gate = jnp.dot(x, gate_w[...], preferred_element_type=f32)
+        up = jnp.dot(x, up_w[...], preferred_element_type=f32)
+        sig = jax.nn.sigmoid(gate)
+        silu = gate * sig
+        hidden = (silu * up).astype(bf)
+        a_buf[slot] = (up * sig * (1.0 + gate * (1.0 - sig))).reshape(2, rows, -1)
+        b_buf[slot] = silu.reshape(2, rows, -1)
+        c = coeff[pl.ds(2 * o, 2)].reshape(2 * rows, 1)
+        part = jnp.dot(hidden, down_w[...], preferred_element_type=f32)
+        part_buf[slot] = (c * part).astype(bf).reshape(2, rows, -1)
+        for copy in outputs(t, slot):
+            copy.start()
+
+    for t in (CHIPS - 2, CHIPS - 1):
+        for copy in outputs(t, t % 2):
+            copy.wait()
+
+    for h in range(2):
+        move(h, mine, FIRST, place.first(h)).wait_send()
+        spread(h, mine, place.z, done)
+        spread(h, place.chip(h, 1, place.z), place.z, done)
+
+    @pl.loop(0, CHIPS)
+    def _(t):
+        @pl.when(t < CHIPS - 4)
+        def _():
+            level, h, k = place.level(1 + t // 4), t % 2, t // 2 % 2
+            spread(h, place.chip(h, k, level), level, done)
+
+        dx, dy = t % 2, t // 2 % 2
+        o = place.chip_at(dx, dy, place.level(t // 4))
+        for h, away in ((0, dx), (1, dy)):
+            @pl.when(away == 1)
+            def _():
+                move(h, o, SIB, place.sibling).wait_send()
+
+
+def experts_forward(x, gate_w, up_w, down_w, coeff):
+    rows, width = x.shape
+    devices, hidden = coeff.shape[0], gate_w.shape[1]
+    bf, f32 = jnp.bfloat16, jnp.float32
+    dma = pltpu.SemaphoreType.DMA
+    vmem, anywhere = pl.BlockSpec(memory_space=pltpu.VMEM), pl.BlockSpec(memory_space=pl.ANY)
+    return pl.pallas_call(
+        functools.partial(expert_kernel, rows),
+        out_shape=(
+            jax.ShapeDtypeStruct((devices, rows, width), bf),
+            jax.ShapeDtypeStruct((devices, rows, hidden), f32),
+            jax.ShapeDtypeStruct((devices, rows, hidden), f32),
+        ),
+        in_specs=[anywhere, vmem, vmem, vmem, vmem],
+        out_specs=(anywhere, anywhere, anywhere),
+        scratch_shapes=[
+            pltpu.VMEM((devices, rows, width), bf),
+            pltpu.VMEM((2, 2, rows, width), bf),
+            pltpu.VMEM((2, 2, rows, hidden), f32),
+            pltpu.VMEM((2, 2, rows, hidden), f32),
+            dma, dma((5, 2, CHIPS)), dma((2, 2, CHIPS)), dma((2, 3)),
+        ],
+        compiler_params=pltpu.CompilerParams(has_side_effects=True, vmem_limit_bytes=56 << 20),
+        name="experts_forward",
+    )(x, gate_w, up_w, down_w, coeff)
+
+
+def backward_kernel(rows, source, upstream, a_in, b_in, gate_w, up_w, down_w, coeff, out, grad_out, *scratch):
+    scatter, (u_buf, a_buf, b_buf, g_buf, in_sem, out_sem) = scratch[:-6], scratch[-6:]
+    f32, bf = jnp.float32, jnp.bfloat16
+    flip = (((1,), (1,)), ((), ()))
+
+    def inputs(t, slot):
+        two = pl.ds(2 * t, 2)
+        return (
+            pltpu.make_async_copy(upstream.at[two], u_buf.at[slot], in_sem.at[slot, 0]),
+            pltpu.make_async_copy(a_in.at[two], a_buf.at[slot], in_sem.at[slot, 1]),
+            pltpu.make_async_copy(b_in.at[two], b_buf.at[slot], in_sem.at[slot, 2]),
+        )
+
+    def output(t, slot):
+        return pltpu.make_async_copy(g_buf.at[slot], grad_out.at[pl.ds(2 * t, 2)], out_sem.at[slot])
+
+    def work(t):
+        @pl.when(t == 0)
+        def _():
+            for copy in inputs(0, 0):
+                copy.start()
+
+        @pl.when(t < CHIPS)
+        def _():
+            slot = t % 2
+
+            @pl.when(t + 1 < CHIPS)
+            def _():
+                for copy in inputs(t + 1, 1 - slot):
+                    copy.start()
+
+            for copy in inputs(t, slot):
+                copy.wait()
+
+            @pl.when(t >= 2)
+            def _():
+                output(t - 2, slot).wait()
+
+            c = coeff[pl.ds(2 * t, 2)].reshape(2 * rows, 1)
+            part = (c * u_buf[slot].reshape(2 * rows, -1).astype(f32)).astype(bf)
+            grad_hidden = lax.dot_general(part, down_w[...], flip, preferred_element_type=f32)
+            grad_gate = (grad_hidden * a_buf[slot].reshape(2 * rows, -1)).astype(bf)
+            grad_up = (grad_hidden * b_buf[slot].reshape(2 * rows, -1)).astype(bf)
+            grad = lax.dot_general(grad_gate, gate_w[...], flip, preferred_element_type=f32)
+            grad += lax.dot_general(grad_up, up_w[...], flip, preferred_element_type=f32)
+            g_buf[slot] = grad.astype(bf).reshape(2, rows, -1)
+            output(t, slot).start()
+
+    scatter_kernel(rows, work, source, out, *scatter)
+    for t in (CHIPS - 2, CHIPS - 1):
+        output(t, t % 2).wait()
+
+
+def scatter_beside_backward(partial, upstream, a, b, gate_w, up_w, down_w, coeff):
+    devices, rows, width = partial.shape
+    hidden = gate_w.shape[1]
+    bf, f32 = jnp.bfloat16, jnp.float32
+    dma = pltpu.SemaphoreType.DMA
+    vmem, anywhere = pl.BlockSpec(memory_space=pltpu.VMEM), pl.BlockSpec(memory_space=pl.ANY)
+    return pl.pallas_call(
+        functools.partial(backward_kernel, rows),
+        out_shape=(
+            jax.ShapeDtypeStruct((rows, width), f32),
+            jax.ShapeDtypeStruct((devices, rows, width), bf),
+        ),
+        in_specs=[anywhere] * 4 + [vmem] * 4,
+        out_specs=(vmem, anywhere),
+        scratch_shapes=scatter_scratch(rows, width) + [
+            pltpu.VMEM((2, 2, rows, width), bf),
+            pltpu.VMEM((2, 2, rows, hidden), f32),
+            pltpu.VMEM((2, 2, rows, hidden), f32),
+            pltpu.VMEM((2, 2, rows, width), bf),
+            dma((2, 3)), dma((2,)),
+        ],
+        compiler_params=pltpu.CompilerParams(has_side_effects=True, vmem_limit_bytes=60 << 20),
+        name="scatter_backward",
+    )(partial, upstream, a, b, gate_w, up_w, down_w, coeff)
+
 
 def own_columns(value, axis, groups):
     return lax.all_to_all(value, axis, split_axis=1, concat_axis=0, tiled=True, axis_index_groups=groups)
@@ -446,19 +874,19 @@
     slab_up = expert_up_weight[0]
     slab_down = expert_down_weight[0]
     upstream_all = lax.all_gather(output_gradient, "fsdp", axis=0, tiled=True)
-    inputs = lax.all_gather(normed_ffn, "fsdp", axis=0, tiled=True)
-    gate_part = matmul(inputs, slab_gate)
-    up_part = matmul(inputs, slab_up)
-    sigmoid = jax.nn.sigmoid(gate_part)
-    hidden = (gate_part * sigmoid * up_part).astype(bf)
-    part = (coeff_own * matmul(hidden, slab_down)).astype(bf)
-    grad_part = (coeff_own * upstream_all.astype(f32)).astype(bf)
-    grad_hidden = matmul(grad_part, slab_down.T)
-    grad_gate = (grad_hidden * up_part * sigmoid * (1.0 + gate_part * (1.0 - sigmoid))).astype(bf)
-    grad_up = (grad_hidden * gate_part * sigmoid).astype(bf)
-    grad_slab = (matmul(grad_gate, slab_gate.T) + matmul(grad_up, slab_up.T)).astype(bf)
-    grad_ffn = lax.psum_scatter(grad_slab, "fsdp", scatter_dimension=0, tiled=True).astype(f32)
-    moe = lax.psum_scatter(part, "fsdp", scatter_dimension=0, tiled=True).astype(f32)
+    coeff_own = coeff_own.reshape(devices, rows_dev, 1)
+    part, keep_gate, keep_up = experts_forward(normed_ffn, slab_gate, slab_up, slab_down, coeff_own)
+    moe, grad_slab = scatter_beside_backward(
+        part,
+        upstream_all.reshape(devices, rows_dev, width),
+        keep_gate,
+        keep_up,
+        slab_gate,
+        slab_up,
+        slab_down,
+        coeff_own,
+    )
+    grad_ffn = scatter_all(grad_slab)
     output = (middle + moe).astype(bf)
     upstream = output_gradient.astype(f32)
     grad_middle = upstream + rms_back(middle, ffn_scale, grad_ffn)
@@ -548,7 +976,7 @@
 
 
 def solution(mesh):
-    plan = heads_plan if mesh.shape["fsdp"] == 32 else shards
+    plan = heads_plan if mesh.shape["fsdp"] == LEVELS * 8 else shards
     in_specs = (
         P("fsdp", None),
         P(),

time: 1160 us -> 846 us (0.73)
  waiting for transfers between devices: 769 us -> 220 us
  Pallas kernels: 10.1 us -> 365 us
  matrix products: 224 us -> 109 us
    pallas_call x0 -> x3, Pallas kernels: none -> 355 us  [the longest x1 162 us: experts_forward(): pl.pallas_call(functools.partial(expert_kernel, rows), out_shape=(jax.Sha...]
    reduce_scatter x2 -> x0, waiting for transfers between devices: 348 us -> none  [the longest x1 185 us: heads_plan(): lax.psum_scatter(part, 'fsdp', scatter_dimension=0, tiled=True).astype(f32)]
    dot_general x35 -> x29, matrix products: 221 us -> 106 us  [matmul(): return jnp.dot(left, right, preferred_element_type=jnp.float32)]
    all_gather x1 -> x0, waiting for transfers between devices: 101 us -> none  [heads_plan(): inputs = lax.all_gather(normed_ffn, 'fsdp', axis=0, tiled=True)]
    all_gather x1, waiting for transfers between devices: 69.8 us -> 0.02 us  [heads_plan(): upstream_all = lax.all_gather(output_gradient, 'fsdp', axis=0, tiled=True)]
    all_to_all x1, waiting for transfers between devices: 18 us -> 0.01 us  [heads_plan(): lax.all_to_all(mixed_head.reshape(group, rows_dev, HEAD_DIM), 'fsdp', spl...]
    all_gather x1, waiting for transfers between devices: 17 us -> 0.01 us  [heads_plan(): output_matrix = lax.all_gather(output_weight, 'fsdp', axis=0, tiled=True)]
  transfers between devices with their start and end apart: 14 -> 11, of which waited for: 13 -> 7; matrix products, arithmetic and copies ran while one was open for 12% -> 13% of each run, Pallas kernels for 1% -> 21%
where the time goes in v2:
time: 846 us; the launch traced here: 834 us
  Pallas kernels  365 us (43%)
  waiting for transfers between devices  220 us (26%)
  matrix products  109 us (13%)
  other arithmetic  45.9 us (5%)
  blocking collectives  45.2 us (5%)
  starting transfers between devices  20.9 us (2%)
  between operations  15.6 us (2%)
  local copies, waits for them, and re-layouts  12.9 us (2%)
    pallas_call x1, Pallas kernels, experts_forward(): pl.pallas_call(functools.partial(expert_kernel, rows), out_shape=(jax.Sha...  162 us
    dot_general x29, matrix products, matmul(): return jnp.dot(left, right, preferred_element_type=jnp.float32)  106 us
    pallas_call x1, Pallas kernels, scatter_beside_backward(): pl.pallas_call(functools.partial(backward_kernel, rows), out_shape=(jax.S...  101 us
    pallas_call x1, Pallas kernels, scatter_all(): pl.pallas_call(functools.partial(scatter_kernel, rows, None), out_shape=j...  92.8 us
    reduce_scatter x1, waiting for transfers between devices, heads_plan(): lax.psum_scatter(grad_partial, 'fsdp', scatter_dimension=0, tiled=True, a...  64.2 us
    all_gather x1, waiting for transfers between devices, heads_plan(): lax.all_gather(normed, 'fsdp', axis=0, tiled=True, axis_index_groups=groups)  50.9 us
    all_gather x1, blocking collectives, heads_plan(): coeff_all = lax.all_gather(coeff.T, 'fsdp', axis=0, tiled=False)  45.2 us
    ppermute x1, waiting for transfers between devices, heads_plan(): lax.ppermute(stacked, 'fsdp', [(i, (i + other * group) % devices) for i i...  35.2 us
  transfers between devices with their start and end apart: 11, of which 7 were waited for; matrix products, arithmetic and copies ran while one was open for 13% of the time, Pallas kernels for 21%

profile of v2, /device:TPU:0, one launch (start us, length us, event | category | flops | bytes accessed | tf_op | source)
XLA Modules:
  0.0 834.2 jit_solution(1338029331222038121)
XLA Ops:
  9.2 1.5 gather_fusion.2
  13.6 2.0 fusion.13
  18.1 4.1 collective-permute-start
  22.2 35.2 %collective-permute-done = bf16[192,2048]{1,0:T(8,128)(2,1)S(1)} collective-permute-done((bf16[192,2048]{1,0:T(8,128)(2,1)S(1)}, bf16[192,2048]{1,0:T(8,128)(2,1)S(1)}, u32[]{:S(2)}, u32[]{:S(2)}) %collective-permute-start) | collective-permute-done | bytes 786464 | tf_op jit(solution)/shard_map/ppermute | solution.py:825
  57.3 2.7 copy_bitcast_fusion
  60.0 4.4 all-to-all-start
  64.6 25.0 %all-to-all-done = bf16[384,16,128]{2,0,1:T(8,128)(2,1)S(1)} async-done(((bf16[384,16,128]{2,0,1:T(8,128)(2,1)}), bf16[384,16,128]{2,0,1:T(8,128)(2,1)S(1)}, u32[]{:S(2)}, u32[]{:S(2)}) %all-to-all-start) | async-done | bytes 1572896 | tf_op jit(solution)/shard_map/all_to_all | solution.py:757
  91.0 50.9 %all-gather.6.cloned.1.call-done = bf16[2048,2048]{1,0:T(8,128)(2,1)} async-done(((bf16[128,2048]{1,0:T(8,128)(2,1)}), bf16[2048,2048]{1,0:T(8,128)(2,1)}) %all-gather.6.cloned.1.call-update) | async-done | bytes 8388624 | tf_op jit(solution)/shard_map/all_gather | solution.py:819
  141.9 6.3 convolution_convert_fusion
  148.2 2.9 fusion.98
  152.3 2.9 fusion.99
  156.3 2.4 fusion.100
  158.8 2.1 convolution_add_fusion.5
  161.2 2.4 fusion.37
  163.6 8.1 fusion.97
  171.8 10.1 %online-softmax = f32[2048,128]{1,0:T(8,128)} custom-call(f32[2048,2048]{1,0:T(8,128)} %get-tuple-element.40, f32[2048,128]{1,0:T(8,128)} %convolution_add_fusion.5), custom_call_target="tpu_custom_call" | custom-call | tf_op online-softmax
  184.1 3.8 all-to-all-start.1
  188.0 45.2 %all-gather = f32[512,128]{1,0:T(8,128)S(1)} all-gather(f32[16,128]{1,0:T(8,128)S(1)} %bitcast.124), channel_id=2, replica_groups=mesh['fsdp'=32] {'fsdp'}, dimensions={0}, use_global_device_ids=true | all-gather | bytes 270336 | tf_op jit(solution)/shard_map/all_gather | solution.py:871
  233.2 2.0 copy.89.coeff
  235.1 1.8 convolution_convert_fusion.2
  237.0 4.8 convolution_add_fusion.6
  243.4 161.8 %experts_forward.1 = (bf16[32,128,2048]{2,1,0:T(8,128)(2,1)}, f32[32,128,512]{2,1,0:T(8,128)}, f32[32,128,512]{2,1,0:T(8,128)}) custom-call(bf16[128,2048]{1,0:T(8,128)(2,1)} %multiply_convert_fusion.3.x_ref, bf16[2048,512]{1,0:T(8,128)(2,1)} %bitcast.102, bf16[2048,512]{1,0:T(8,128)(2,1)} %bitcast.104, bf16[512,2048]{1,0:T(8,128)(2,1)} %bitcast.106, ...), custom_call_target="tpu_custom_call" | custom-call | tf_op jit(solution)/shard_map/experts_forward/pallas_call | solution.py:656
  405.3 100.6 %scatter_backward.1 = (f32[128,2048]{1,0:T(8,128)}, bf16[32,128,2048]{2,1,0:T(8,128)(2,1)}) custom-call(bf16[32,128,2048]{2,1,0:T(8,128)(2,1)} %get-tuple-element.9.source, bf16[32,128,2048]{2,1,0:T(8,128)(2,1)} %bitcast.98, f32[32,128,512]{2,1,0:T(8,128)} %get-tuple-element.10.a_in, f32[32,128,512]{2,1,0:T(8,128)} %get-tuple-element.11.b_in, ...), custom_call_target="tpu_custom_call" | custom-call | tf_op jit(solution)/shard_map/scatter_backward/pallas_call | solution.py:736
  505.9 92.8 %scatter_all.1 = f32[128,2048]{1,0:T(8,128)S(1)} custom-call(bf16[32,128,2048]{2,1,0:T(8,128)(2,1)} %get-tuple-element.13.source), custom_call_target="tpu_custom_call" | custom-call | tf_op jit(solution)/shard_map/scatter_all/pallas_call | solution.py:512
  599.0 2.5 multiply_add_fusion
  601.5 2.9 fusion.93
  606.4 5.0 all-to-all-start.2
  611.5 8.1 fusion.1
  619.6 2.4 all-to-all-done.2
  622.0 15.9 %multiply_reduce_fusion = (f32[2048]{0:T(1024)S(1)}, f32[2048,2048]{1,0:T(8,128)}) fusion(f32[2048]{0:T(1024)S(1)} %fusion.1, f32[2048,2048]{1,0:T(8,128)} %get-tuple-element.40, f32[2048]{0:T(1024)S(1)} %get-tuple-element.39, bf16[2048,128]{1,0:T(8,128)(2,1)} %bitcast.24, f32[2048,128]{1,0:T(8,128)} %convolution_add_fusion.5), kind=kOutput, calls=%fused_computation.5 | convolution fusion | flops 1090779136 | bytes 35151872 | tf_op jit(solution)/shard_map/dot_general | solution.py:28
  638.9 8.1 multiply_convert_fusion
  647.1 2.9 convolution_multiply_fusion.1
  650.0 1.3 convolution_multiply_fusion
  651.3 5.7 fusion.6
  657.1 2.7 fusion.46
  665.4 9.4 %fusion.102 = f32[2048,2048]{1,0:T(8,128)} fusion(bf16[2048,128]{0,1:T(8,128)(2,1)} %copy-done.15, bf16[2048,128]{1,0:T(8,128)(2,1)} %bitcast.112), kind=kOutput, calls=%fused_computation.188 | convolution fusion | flops 1073741824 | bytes 17825792 | tf_op jit(solution)/shard_map/dot_general | solution.py:28
  674.8 8.1 fusion.101
  682.9 15.6 %add_convert_fusion = bf16[2048,2048]{1,0:T(8,128)(2,1)} fusion(f32[2048,2048]{1,0:T(8,128)} %fusion.101, f32[2048,2048]{1,0:T(8,128)} %fusion.102, bf16[2048,128]{1,0:T(8,128)(2,1)S(1)} %copy-done.17, bf16[2048,128]{1,0:T(8,128)(2,1)} %bitcast.117), kind=kOutput, calls=%fused_computation.3 | convolution fusion | flops 1086324736 | bytes 42991616 | tf_op jit(solution)/shard_map/dot_general | solution.py:28
  700.8 1.3 fusion.90
  702.4 1.4 fusion.59
  706.4 14.9 %reduce-scatter.5.cloned.1.call-done = f32[128,128]{0,1:T(8,128)} async-done(((f32[2048,128]{0,1:T(8,128)}), f32[128,128]{0,1:T(8,128)}) %reduce-scatter.5.cloned.1.call-update) | async-done | bytes 65552 | tf_op jit(solution)/shard_map/reduce_scatter | solution.py:929
  721.3 1.4 fusion.74
  722.8 3.7 maximum_bitcast_fusion.1
  726.5 3.4 all-to-all-start.3
  729.9 25.8 %all-to-all-done.3 = f32[32,128,64]{1,2,0:T(8,128)} async-done(((f32[32,128,64]{1,2,0:T(8,128)}), f32[32,128,64]{1,2,0:T(8,128)}, u32[]{:S(2)}, u32[]{:S(2)}) %all-to-all-start.3) | async-done | bytes 1048608 | tf_op jit(solution)/shard_map/all_to_all | solution.py:960
  758.1 1.9 slice_bitcast_fusion
  759.9 64.2 %reduce-scatter.3.cloned.1.call-done = bf16[128,2048]{1,0:T(8,128)(2,1)} async-done(((bf16[2048,2048]{1,0:T(8,128)(2,1)}), bf16[128,2048]{1,0:T(8,128)(2,1)}) %reduce-scatter.3.cloned.1.call-update) | async-done | bytes 524304 | tf_op jit(solution)/shard_map/reduce_scatter | solution.py:926
  824.1 1.6 fusion.14
  (187 shorter events, 32.8 us)
Async XLA Ops:
  7.2 57.3 %copy-start.43 = (bf16[128]{0:T(256)(128)(2,1)S(1)}, bf16[128]{0:T(256)(128)(2,1)}, u32[]{:S(2)}) copy-start(bf16[128]{0:T(256)(128)(2,1)} %param.25) | copy-start | bytes 772
  7.2 57.3 %copy-start.44 = (bf16[128]{0:T(256)(128)(2,1)S(1)}, bf16[128]{0:T(256)(128)(2,1)}, u32[]{:S(2)}) copy-start(bf16[128]{0:T(256)(128)(2,1)} %param.26) | copy-start | bytes 772
  7.2 57.4 %copy-start.39 = (s32[2,2048]{1,0:T(2,128)S(1)}, s32[2,2048]{1,0:T(2,128)}, u32[]{:S(2)}) copy-start(s32[2,2048]{1,0:T(2,128)} %param.20) | copy-start | bytes 49156
  7.2 83.7 %all-gather.8.cloned.1.call-start = ((), (), s32[]{:S(2)}) async-start(), calls=%async_computation.7 | async-start | bytes 1081344 | tf_op jit(solution)/shard_map/all_gather | solution.py:812
  11.6 130.3 %all-gather.6.cloned.1.call-start = ((), (), s32[]{:S(2)}) async-start(), calls=%async_computation.6 | async-start | bytes 8912896 | tf_op jit(solution)/shard_map/all_gather | solution.py:819
  12.3 78.4 %copy-start.32 = (f32[2048]{0:T(1024)}, f32[2048]{0:T(1024)S(1)}, u32[]{:S(2)}) copy-start(f32[2048]{0:T(1024)S(1)} %convert_element_type.130) | copy-start | bytes 24580
  13.5 51.0 %copy-start.36 = (f32[128]{0:T(128)}, f32[128]{0:T(128)S(1)}, u32[]{:S(2)}) copy-start(f32[128]{0:T(128)S(1)} %add_rsqrt_fusion.3) | copy-start | bytes 1540
  15.6 221.4 %all-gather.10.cloned.1.call-start = ((), (), s32[]{:S(2)}) async-start(), calls=%async_computation.8 | async-start | bytes 8650752 | tf_op jit(solution)/shard_map/all_gather | solution.py:833
  16.3 388.9 %all-gather.12.cloned.1.call-start = ((), (), s32[]{:S(2)}) async-start(), calls=%async_computation.9 | async-start | bytes 17301504 | tf_op jit(solution)/shard_map/all_gather | solution.py:876
  18.1 39.3 %collective-permute-start = (bf16[192,2048]{1,0:T(8,128)(2,1)S(1)}, bf16[192,2048]{1,0:T(8,128)(2,1)S(1)}, u32[]{:S(2)}, u32[]{:S(2)}) collective-permute-start(bf16[192,2048]{1,0:T(8,128)(2,1)S(1)} %pad_maximum_fusion), channel_id=1, source_target_pairs={{0,16},{1,17},{2,18},{3,19},{4,20},{5,21},{6,22},{7,23},{8,24},{9,... | collective-permute-start | bytes 2359304 | tf_op jit(solution)/shard_map/ppermute | solution.py:825
  60.0 29.7 %all-to-all-start = ((bf16[384,16,128]{2,0,1:T(8,128)(2,1)}), bf16[384,16,128]{2,0,1:T(8,128)(2,1)S(1)}, u32[]{:S(2)}, u32[]{:S(2)}) async-start(bf16[384,16,128]{2,0,1:T(8,128)(2,1)} %copy_bitcast_fusion), calls=%async_computation | async-start | bytes 3145728 | tf_op jit(solution)/shard_map/all_to_all | solution.py:757
  90.9 60.2 %copy-start.18 = (bf16[1,2,16,64,128]{4,3,0,2,1:T(8,128)(2,1)}, bf16[1,2,16,64,128]{4,3,0,2,1:T(8,128)(2,1)S(1)}, u32[]{:S(2)}) copy-start(bf16[1,2,16,64,128]{4,3,0,2,1:T(8,128)(2,1)S(1)} %get-tuple-element.16) | copy-start | bytes 1572868
  90.9 61.3 %copy-start.20 = (bf16[1,2,16,64,128]{4,3,0,2,1:T(8,128)(2,1)}, bf16[1,2,16,64,128]{4,3,0,2,1:T(8,128)(2,1)S(1)}, u32[]{:S(2)}) copy-start(bf16[1,2,16,64,128]{4,3,0,2,1:T(8,128)(2,1)S(1)} %get-tuple-element.15) | copy-start | bytes 1572868
  90.9 65.4 %copy-start.23 = (bf16[1,2,16,64,128]{4,3,0,2,1:T(8,128)(2,1)}, bf16[1,2,16,64,128]{4,3,0,2,1:T(8,128)(2,1)S(1)}, u32[]{:S(2)}) copy-start(bf16[1,2,16,64,128]{4,3,0,2,1:T(8,128)(2,1)S(1)} %get-tuple-element.14) | copy-start | bytes 1572868
  148.2 10.6 %copy-start.21 = (bf16[2048,64]{0,1:T(8,128)(2,1)}, bf16[2048,64]{0,1:T(8,128)(2,1)S(1)}, u32[]{:S(2)}) copy-start(bf16[2048,64]{0,1:T(8,128)(2,1)S(1)} %convolution_convert_fusion) | copy-start | bytes 786436
  152.2 8.7 %copy-start.3 = (f32[2048,128]{0,1:T(8,128)}, f32[2048,128]{0,1:T(8,128)S(1)}, u32[]{:S(2)}) copy-start(f32[2048,128]{0,1:T(8,128)S(1)} %get-tuple-element.34) | copy-start | bytes 3145732
  163.6 8.1 copy-start.25
  163.6 8.1 copy-start.28
  171.7 16.2 %copy-start.38 = (bf16[2048]{0:T(1024)(128)(2,1)S(1)}, bf16[2048]{0:T(1024)(128)(2,1)}, u32[]{:S(2)}) copy-start(bf16[2048]{0:T(1024)(128)(2,1)} %param.33) | copy-start | bytes 12292
  171.7 16.2 %copy-start.40 = (f32[128,8]{0,1:T(8,128)S(1)}, f32[128,8]{0,1:T(8,128)}, u32[]{:S(2)}) copy-start(f32[128,8]{0,1:T(8,128)} %param.22) | copy-start | bytes 12292
  171.7 16.2 %copy-start.41 = (s32[128,8]{0,1:T(8,128)S(1)}, s32[128,8]{0,1:T(8,128)}, u32[]{:S(2)}) copy-start(s32[128,8]{0,1:T(8,128)} %param.21) | copy-start | bytes 12292
  171.7 65.2 %copy-start.6 = (bf16[128,2048]{1,0:T(8,128)(2,1)S(1)}, bf16[128,2048]{1,0:T(8,128)(2,1)}, u32[]{:S(2)}) copy-start(bf16[128,2048]{1,0:T(8,128)(2,1)} %param.19) | copy-start | bytes 1572868
  184.1 51.0 %all-to-all-start.1 = ((bf16[16,128,128]{1,2,0:T(8,128)(2,1)}), bf16[16,128,128]{1,2,0:T(8,128)(2,1)S(1)}, u32[]{:S(2)}, u32[]{:S(2)}) async-start(bf16[16,128,128]{1,2,0:T(8,128)(2,1)} %copy.88), calls=%async_computation.1 | async-start | bytes 1048576 | tf_op jit(solution)/shard_map/all_to_all | solution.py:854
  242.3 356.3 %copy-start.5 = (f32[128,2048]{1,0:T(8,128)}, f32[128,2048]{1,0:T(8,128)S(1)}, u32[]{:S(2)}) copy-start(f32[128,2048]{1,0:T(8,128)S(1)} %get-tuple-element.38) | copy-start | bytes 3145732
  505.9 95.6 %slice-start.4 = ((s8[8388608]{0:T(1024)(128)(4,1)}), s8[4194304]{0:T(1024)(128)(4,1)S(1)}, s32[]{:S(2)}) async-start(s8[8388608]{0:T(1024)(128)(4,1)} %bitcast.96), calls=%async_computation.16 | async-start | bytes 8388608
  505.9 93.1 %copy-start.24 = (bf16[128,2048]{1,0:T(8,128)(2,1)S(1)}, bf16[128,2048]{1,0:T(8,128)(2,1)}, u32[]{:S(2)}) copy-start(bf16[128,2048]{1,0:T(8,128)(2,1)} %param.37) | copy-start | bytes 1572868
  505.9 93.1 %copy-start.27 = (f32[128,2048]{1,0:T(8,128)S(1)}, f32[128,2048]{1,0:T(8,128)}, u32[]{:S(2)}) copy-start(f32[128,2048]{1,0:T(8,128)} %get-tuple-element.12) | copy-start | bytes 3145732
  505.9 95.6 %slice-start.5 = ((s8[8388608]{0:T(1024)(128)(4,1)}), s8[4194304]{0:T(1024)(128)(4,1)S(1)}, s32[]{:S(2)}) async-start(s8[8388608]{0:T(1024)(128)(4,1)} %bitcast.96), calls=%async_computation.17 | async-start | bytes 8388608
  606.4 15.6 %all-to-all-start.2 = ((bf16[128,16,128]{2,0,1:T(8,128)(2,1)}), bf16[128,16,128]{2,0,1:T(8,128)(2,1)}, u32[]{:S(2)}, u32[]{:S(2)}) async-start(bf16[128,16,128]{2,0,1:T(8,128)(2,1)} %bitcast.93), calls=%async_computation.2 | async-start | bytes 1048576 | tf_op jit(solution)/shard_map/all_to_all | solution.py:757
  611.4 109.9 %reduce-scatter.5.cloned.1.call-start = ((), (), s32[]{:S(2)}) async-start(), calls=%async_computation.11 | async-start | bytes 1114112 | tf_op jit(solution)/shard_map/reduce_scatter | solution.py:929
  622.0 15.9 %slice-start = ((s8[16777216]{0:T(1024)(128)(4,1)}), s8[4194304]{0:T(1024)(128)(4,1)S(1)}, s32[]{:S(2)}) async-start(s8[16777216]{0:T(1024)(128)(4,1)} %bitcast.94), calls=%async_computation.12 | async-start | bytes 8388608
  622.0 15.9 %slice-start.1 = ((s8[16777216]{0:T(1024)(128)(4,1)}), s8[4194304]{0:T(1024)(128)(4,1)S(1)}, s32[]{:S(2)}) async-start(s8[16777216]{0:T(1024)(128)(4,1)} %bitcast.94), calls=%async_computation.13 | async-start | bytes 8388608
  622.0 15.9 %slice-start.2 = ((s8[16777216]{0:T(1024)(128)(4,1)}), s8[4194304]{0:T(1024)(128)(4,1)S(1)}, s32[]{:S(2)}) async-start(s8[16777216]{0:T(1024)(128)(4,1)} %bitcast.94), calls=%async_computation.14 | async-start | bytes 8388608
  622.0 16.9 %slice-start.3 = ((s8[16777216]{0:T(1024)(128)(4,1)}), s8[4194304]{0:T(1024)(128)(4,1)S(1)}, s32[]{:S(2)}) async-start(s8[16777216]{0:T(1024)(128)(4,1)} %bitcast.94), calls=%async_computation.15 | async-start | bytes 8388608
  638.9 8.2 copy-start.29
  638.9 8.2 copy-start.31
  651.3 8.4 %copy-start.4 = (f32[2048,128]{0,1:T(8,128)S(1)}, f32[2048,128]{0,1:T(8,128)}, u32[]{:S(2)}) copy-start(f32[2048,128]{0,1:T(8,128)} %copy-done.3) | copy-start | bytes 3145732
  660.3 14.5 %copy-start.13 = (bf16[2048,128]{0,1:T(8,128)(2,1)}, bf16[2048,128]{0,1:T(8,128)(2,1)S(1)}, u32[]{:S(2)}) copy-start(bf16[2048,128]{0,1:T(8,128)(2,1)S(1)} %multiply_convert_fusion.2) | copy-start | bytes 1572868
  665.3 9.4 %copy-start.19 = (bf16[1,2,16,64,128]{4,3,0,2,1:T(8,128)(2,1)S(1)}, bf16[1,2,16,64,128]{4,3,0,2,1:T(8,128)(2,1)}, u32[]{:S(2)}) copy-start(bf16[1,2,16,64,128]{4,3,0,2,1:T(8,128)(2,1)} %copy-done.18) | copy-start | bytes 1572868
  665.3 158.8 %reduce-scatter.3.cloned.1.call-start = ((), (), s32[]{:S(2)}) async-start(), calls=%async_computation.10 | async-start | bytes 8912896 | tf_op jit(solution)/shard_map/reduce_scatter | solution.py:926
  674.8 8.2 copy-start.17
  700.8 29.1 %copy-start.42 = (s32[2]{0:T(128)S(1)}, s32[2]{0:T(128)}, u32[]{:S(2)}) copy-start(s32[2]{0:T(128)} %param.23) | copy-start | bytes 28
  702.4 121.7 %copy-start.7 = (bf16[128,2048]{1,0:T(8,128)(2,1)S(1)}, bf16[128,2048]{1,0:T(8,128)(2,1)}, u32[]{:S(2)}) copy-start(bf16[128,2048]{1,0:T(8,128)(2,1)} %param.19) | copy-start | bytes 1572868
  702.4 121.7 %copy-start.12 = (bf16[2048,256]{1,0:T(8,128)(2,1)S(1)}, bf16[2048,256]{1,0:T(8,128)(2,1)}, u32[]{:S(2)}) copy-start(bf16[2048,256]{1,0:T(8,128)(2,1)} %all-gather.8.cloned.1.call-done) | copy-start | bytes 3145732
  702.4 121.7 %copy-start.33 = (f32[2048]{0:T(1024)S(1)}, f32[2048]{0:T(1024)}, u32[]{:S(2)}) copy-start(f32[2048]{0:T(1024)} %copy-done.32) | copy-start | bytes 24580
  702.4 121.7 %copy-start.37 = (f32[128]{0:T(128)S(1)}, f32[128]{0:T(128)}, u32[]{:S(2)}) copy-start(f32[128]{0:T(128)} %copy-done.36) | copy-start | bytes 1540
  721.3 105.7 %copy-start.1 = (bf16[8,4,64,16]{2,3,1,0:T(8,128)(2,1)S(1)}, bf16[8,4,64,16]{2,3,1,0:T(8,128)(2,1)}, u32[]{:S(2)}) copy-start(bf16[8,4,64,16]{2,3,1,0:T(8,128)(2,1)} %param.31) | copy-start | bytes 196612
  726.5 29.2 %all-to-all-start.3 = ((f32[32,128,64]{1,2,0:T(8,128)}), f32[32,128,64]{1,2,0:T(8,128)}, u32[]{:S(2)}, u32[]{:S(2)}) async-start(f32[32,128,64]{1,2,0:T(8,128)} %maximum_bitcast_fusion.1), calls=%async_computation.5 | async-start | bytes 2097152 | tf_op jit(solution)/shard_map/all_to_all | solution.py:960
  (14 other events, 53.5 us)
Sparse Core Ops, SparseCore 0:
  11.7 78.6 all-gather.7
  92.6 49.2 all-gather.5
  144.7 81.3 all-gather.9
  228.9 152.5 all-gather.11
  665.4 55.8 reduce-scatter.4
  723.6 100.5 reduce-scatter.2

commit v3 on v2

--- a/solution.py
+++ b/solution.py
@@ -753,8 +753,492 @@
     )(partial, upstream, a, b, gate_w, up_w, down_w, coeff)
 
 
-def own_columns(value, axis, groups):
-    return lax.all_to_all(value, axis, split_axis=1, concat_axis=0, tiled=True, axis_index_groups=groups)
+def front_kernel(rows, rank, normed, heads_w, pair, coeff, cosine, sine, query_gain, key_gain, q_seg, k_seg,
+                 mixed, weights, query_out, key_out, value_out, query_proj, key_proj, inner_out, coeff_out,
+                 held, mixed_buf,
+                 local_sem, send, recv, w_send, w_recv, pair_send, pair_recv, c_send, c_recv, m_send, m_recv, m_local):
+    place = Place()
+    f32, bf = jnp.float32, jnp.bfloat16
+    me, core = place.me, place.core
+    group = held.shape[0]
+    base, p = me // group * group, me % group
+    other = (me + group) % (2 * group)
+    other_base = group - base
+    half = rows // 2
+    depth = weights.shape[1]
+    wide = 3 * 128
+    z = place.z % 2
+    across_z = me + 8 - 16 * z
+    chip = p // 2
+
+    FIRST, ALONG, LAST, SIB = range(4)
+
+    def chip_at(h, k, far):
+        flip = place.chip(h, k, 0)
+        zz = z + far * (1 - 2 * z)
+        return zz * 4 + flip
+
+    def move(h, o, kind, target):
+        piece = held.at[2 * o + core, pl.ds(h * half, half)]
+        return pltpu.make_async_remote_copy(
+            src_ref=piece, dst_ref=piece, send_sem=send.at[kind, h, o],
+            recv_sem=recv.at[1 if kind == SIB else 0, h, o], device_id=(target,), device_id_type=MESH)
+
+    def arrived(h, o, sibling):
+        piece = held.at[2 * o + (1 - core if sibling else core), pl.ds(h * half, half)]
+        pltpu.make_async_remote_copy(
+            src_ref=piece, dst_ref=piece, send_sem=send.at[SIB, h, o],
+            recv_sem=recv.at[1 if sibling else 0, h, o], device_id=(place.sibling,), device_id_type=MESH).wait_recv()
+
+    def to_heads(q):
+        return pltpu.make_async_remote_copy(
+            src_ref=heads_w.at[q % group], dst_ref=weights.at[me, :, pl.ds(0, wide)], send_sem=w_send.at[q],
+            recv_sem=w_recv.at[me], device_id=(q,), device_id_type=MESH)
+
+    def to_expert(q):
+        return pltpu.make_async_remote_copy(
+            src_ref=coeff.at[q // 2], dst_ref=coeff_out.at[me], send_sem=c_send.at[q],
+            recv_sem=c_recv.at[me], device_id=(q,), device_id_type=MESH)
+
+    def pair_over(q, side):
+        row = (me + side * group) % (2 * group)
+        piece = weights.at[row, :, pl.ds(wide, 128)]
+        return pltpu.make_async_remote_copy(
+            src_ref=piece, dst_ref=piece, send_sem=pair_send.at[side, q],
+            recv_sem=pair_recv.at[row], device_id=(base + q,), device_id_type=MESH)
+
+    pair_other = pltpu.make_async_remote_copy(
+        src_ref=pair.at[other // group], dst_ref=weights.at[me, :, pl.ds(wide, 128)], send_sem=pair_send.at[2, 0],
+        recv_sem=pair_recv.at[me], device_id=(other,), device_id_type=MESH)
+    locals_ = [
+        pltpu.make_async_copy(normed, held.at[p], local_sem.at[0]),
+        pltpu.make_async_copy(pair.at[me // group], weights.at[me, :, pl.ds(wide, 128)], local_sem.at[1]),
+        pltpu.make_async_copy(heads_w.at[p], weights.at[me, :, pl.ds(0, wide)], local_sem.at[2]),
+        pltpu.make_async_copy(coeff.at[me // 2], coeff_out.at[me], local_sem.at[3]),
+    ]
+    for copy in locals_:
+        copy.start()
+    pair_other.start()
+
+    @pl.loop(0, group)
+    def _(i):
+        to_heads(other_base + (p + i) % group).start()
+
+    locals_[0].wait()
+    for h in range(2):
+        move(h, chip, FIRST, place.first(h)).start()
+        move(h, chip, ALONG, across_z).start()
+    for h in range(2):
+        move(h, chip, LAST, place.last(h)).start()
+        move(h, chip, SIB, place.sibling).start()
+    locals_[1].wait()
+
+    @pl.loop(1, group)
+    def _(i):
+        pair_over((p + i) % group, 0).start()
+        to_heads(base + (p + i) % group).start()
+
+    @pl.loop(1, 2 * group)
+    def _(i):
+        to_expert((me + i) % (2 * group)).start()
+
+    pltpu.make_async_remote_copy(
+        src_ref=pair.at[0], dst_ref=weights.at[other, :, pl.ds(wide, 128)], send_sem=pair_send.at[2, 0],
+        recv_sem=pair_recv.at[other], device_id=(other,), device_id_type=MESH).wait_recv()
+
+    @pl.loop(1, group)
+    def _(i):
+        pair_over((p + i) % group, 1).start()
+
+    for h in range(2):
+        o = chip_at(h, 1, 0)
+        arrived(h, o, False)
+        move(h, o, ALONG, across_z).start()
+        move(h, o, LAST, place.last(h)).start()
+        move(h, o, SIB, place.sibling).start()
+    for k in range(2):
+        for h in range(2):
+            o = chip_at(h, k, 1)
+            arrived(h, o, False)
+            move(h, o, LAST, place.last(h)).start()
+            move(h, o, SIB, place.sibling).start()
+    for far in range(2):
+        for k in range(2):
+            for h in range(2):
+                dx, dy = (1, k) if h == 0 else (k, 1)
+                o = (z + far * (1 - 2 * z)) * 4 + place.chip_at(dx, dy, 0)
+                arrived(h, o, False)
+                move(h, o, SIB, place.sibling).start()
+    for copy in locals_[2:]:
+        copy.wait()
+
+    @pl.loop(1, 2 * group)
+    def _(i):
+        q = (me + i) % (2 * group)
+        pltpu.make_async_remote_copy(
+            src_ref=heads_w.at[0], dst_ref=weights.at[q, :, pl.ds(0, wide)], send_sem=w_send.at[q],
+            recv_sem=w_recv.at[q], device_id=(q,), device_id_type=MESH).wait_recv()
+        pltpu.make_async_remote_copy(
+            src_ref=coeff.at[0], dst_ref=coeff_out.at[q], send_sem=c_send.at[q],
+            recv_sem=c_recv.at[q], device_id=(q,), device_id_type=MESH).wait_recv()
+
+        @pl.when(q != other)
+        def _():
+            pltpu.make_async_remote_copy(
+                src_ref=pair.at[0], dst_ref=weights.at[q, :, pl.ds(wide, 128)], send_sem=pair_send.at[2, 0],
+                recv_sem=pair_recv.at[q], device_id=(other,), device_id_type=MESH).wait_recv()
+
+    @pl.loop(0, group // 2)
+    def _(o):
+        for h in range(2):
+            arrived(h, o, True)
+
+    span = 2 * rows
+    seq = group * rows
+    up_own = weights[pl.ds(2 * p, 2), :, pl.ds(wide, 128)].reshape(2 * depth, 128)
+    up_own = pltpu.roll(up_own.astype(f32), 64, 1).astype(bf)
+    flip = (((1,), (1,)), ((), ()))
+    scale = 1.0 / math.sqrt(128)
+
+    @pl.loop(0, group // 2)
+    def _(b):
+        at = pl.ds(pl.multiple_of(b * span, span), span)
+        x = held[pl.ds(2 * b, 2)].reshape(span, -1)
+        acc = jnp.dot(x, weights[...].reshape(2 * group * depth, wide + 128), preferred_element_type=f32)
+        inner = acc[:, wide:].astype(bf)
+        inner_out[at] = inner
+        owner = lax.broadcasted_iota(jnp.int32, inner.shape, 1) // rank
+
+        def projected(j):
+            low = jnp.where(owner == j, inner.astype(f32), 0.0).astype(bf)
+            return acc[:, j * 128 : (j + 1) * 128] + lax.dot_general(low, up_own, flip, preferred_element_type=f32)
+
+        for j, (gain, raw, rot) in enumerate(((query_gain, query_proj, query_out), (key_gain, key_proj, key_out))):
+            value = projected(j)
+            raw[at] = value
+            unit = value * lax.rsqrt(jnp.mean(value * value, axis=-1, keepdims=True) + epsilon) * gain[...]
+            rot[at] = (unit * cosine[at] + pltpu.roll(unit, 64, 1) * sine[at]).astype(bf)
+        value_out[at] = projected(2).astype(bf)
+
+    def to_token(q):
+        return pltpu.make_async_remote_copy(
+            src_ref=mixed_buf.at[q], dst_ref=mixed.at[:, pl.ds(p * 128, 128)], send_sem=m_send.at[q],
+            recv_sem=m_recv.at[p], device_id=(base + q,), device_id_type=MESH)
+
+    keep = pltpu.make_async_copy(mixed_buf.at[p], mixed.at[:, pl.ds(p * 128, 128)], m_local)
+
+    @pl.loop(0, group // 2)
+    def _(b):
+        at = pl.ds(pl.multiple_of(b * span, span), span)
+        scores = lax.dot_general(query_out[at], key_out[...], flip, preferred_element_type=f32)
+        weight = jnp.where(q_seg[at] == k_seg[...], jnp.exp2(scores * (scale * math.log2(math.e))), 0.0)
+        total = jnp.sum(weight, axis=-1, keepdims=True)
+        value = jnp.dot(weight.astype(bf), value_out[...], preferred_element_type=f32) / total
+        mixed_buf[pl.ds(2 * b, 2)] = value.astype(bf).reshape(2, rows, 128)
+        for side in range(2):
+            q = 2 * b + side
+
+            @pl.when(q != p)
+            def _():
+                to_token(q).start()
+
+            @pl.when(q == p)
+            def _():
+                keep.start()
+
+    keep.wait()
+
+    @pl.loop(1, group)
+    def _(i):
+        q = (p + i) % group
+        pltpu.make_async_remote_copy(
+            src_ref=mixed_buf.at[q], dst_ref=mixed.at[:, pl.ds(q * 128, 128)], send_sem=m_send.at[q],
+            recv_sem=m_recv.at[q], device_id=(base + q,), device_id_type=MESH).wait_recv()
+
+    pair_other.wait_send()
+    for h in range(2):
+        move(h, chip, FIRST, place.first(h)).wait_send()
+        for far in range(2):
+            for k in range(2):
+                o = chip_at(h, k, far)
+                if far == 0:
+                    move(h, o, ALONG, across_z).wait_send()
+                move(h, o, LAST, place.last(h)).wait_send()
+                move(h, o, SIB, place.sibling).wait_send()
+                dx, dy = (1, k) if h == 0 else (k, 1)
+                o = (z + far * (1 - 2 * z)) * 4 + place.chip_at(dx, dy, 0)
+                move(h, o, SIB, place.sibling).wait_send()
+
+    @pl.loop(1, group)
+    def _(i):
+        q = (p + i) % group
+        pair_over(q, 0).wait_send()
+        pair_over(q, 1).wait_send()
+        to_token(q).wait_send()
+
+    @pl.loop(1, 2 * group)
+    def _(i):
+        q = (me + i) % (2 * group)
+        to_heads(q).wait_send()
+        to_expert(q).wait_send()
+
+
+def front(normed, heads_w, pair, coeff, cosine, sine, query_gain, key_gain, q_seg, k_seg, rank):
+    rows, width = normed.shape
+    group, depth = heads_w.shape[0], heads_w.shape[1]
+    devices, seq = 2 * group, rows * group
+    bf, f32 = jnp.bfloat16, jnp.float32
+    dma = pltpu.SemaphoreType.DMA
+    vmem, anywhere = pl.BlockSpec(memory_space=pltpu.VMEM), pl.BlockSpec(memory_space=pl.ANY)
+    head = jax.ShapeDtypeStruct((seq, 128), bf)
+    raw = jax.ShapeDtypeStruct((seq, 128), f32)
+    return pl.pallas_call(
+        functools.partial(front_kernel, rows, rank),
+        out_shape=(
+            jax.ShapeDtypeStruct((rows, width), bf),
+            jax.ShapeDtypeStruct((devices, depth, 512), bf),
+            head, head, head, raw, raw, head,
+            jax.ShapeDtypeStruct((devices, 1, rows), f32),
+        ),
+        in_specs=[anywhere] * 4 + [vmem] * 6,
+        out_specs=(vmem,) * 9,
+        scratch_shapes=[
+            pltpu.VMEM((group, rows, width), bf),
+            pltpu.VMEM((group, rows, 128), bf),
+            dma((4,)), dma((4, 2, group // 2)), dma((2, 2, group // 2)),
+            dma((devices,)), dma((devices,)), dma((3, group)), dma((devices,)),
+            dma((devices,)), dma((devices,)), dma((group,)), dma((group,)), dma,
+        ],
+        compiler_params=pltpu.CompilerParams(has_side_effects=True, vmem_limit_bytes=56 << 20),
+        name="front",
+    )(normed, heads_w, pair, coeff, cosine, sine, query_gain, key_gain, q_seg, k_seg)
+
+
+def back_kernel(rows, rank, grad_mixed, weights, query, key, value, query_proj, key_proj, inner, cosine, sine,
+                query_gain, key_gain, q_seg, k_seg, out, up_terms,
+                grads, key_t, grad_key, grad_value, heads, result, sib, cross_out, cross_in, z_out, z_in, first_out, first_in,
+                a_send, a_recv, a_local, sib_send, sib_recv, cross_send, cross_recv, z_send, z_recv, first_send, first_recv):
+    place = Place()
+    f32, bf = jnp.float32, jnp.bfloat16
+    me, core = place.me, place.core
+    group = grads.shape[0]
+    depth = weights.shape[1]
+    base, p = me // group * group, me % group
+    half, span, seq = rows // 2, 2 * rows, rows * group
+    width = out.shape[1] - 128
+    z = place.z % 2
+    across_z = me + 8 - 16 * z
+    flip = (((1,), (1,)), ((), ()))
+    tall = (((0,), (0,)), ((), ()))
+    scale = 1.0 / math.sqrt(128)
+
+    def to_head(q):
+        return pltpu.make_async_remote_copy(
+            src_ref=grad_mixed.at[:, pl.ds(q * 128, 128)], dst_ref=grads.at[p], send_sem=a_send.at[q],
+            recv_sem=a_recv.at[p], device_id=(base + q,), device_id_type=MESH)
+
+    def from_token(q):
+        return pltpu.make_async_remote_copy(
+            src_ref=grad_mixed.at[:, pl.ds(q * 128, 128)], dst_ref=grads.at[q], send_sem=a_send.at[q],
+            recv_sem=a_recv.at[q], device_id=(base + q,), device_id_type=MESH)
+
+    keep = pltpu.make_async_copy(grad_mixed.at[:, pl.ds(p * 128, 128)], grads.at[p], a_local)
+    keep.start()
+
+    @pl.loop(1, group)
+    def _(i):
+        to_head((p + i) % group).start()
+
+    key_t[...] = key[...].astype(f32).T.astype(bf)
+    grad_key[...] = jnp.zeros_like(grad_key)
+    grad_value[...] = jnp.zeros_like(grad_value)
+    keep.wait()
+
+    def raw_grad(raw, gain, turned, at):
+        back = turned * cosine[at] - pltpu.roll(turned, 64, 1) * sine[at]
+        rows_ = raw[at]
+        inverse = lax.rsqrt(jnp.mean(rows_ * rows_, axis=-1, keepdims=True) + epsilon)
+        unit = rows_ * inverse
+        scaled = back * gain[...]
+        return (inverse * (scaled - unit * jnp.mean(scaled * unit, axis=-1, keepdims=True))).astype(bf)
+
+    @pl.loop(0, group // 2)
+    def _(b):
+        at = pl.ds(pl.multiple_of(b * span, span), span)
+        for side in range(2):
+            q = 2 * b + side
+
+            @pl.when(q != p)
+            def _():
+                from_token(q).wait_recv()
+
+        ours = query[at]
+        grad = grads[pl.ds(2 * b, 2)].reshape(span, 128)
+        scores = lax.dot_general(key[...], ours, flip, preferred_element_type=f32)
+        weight = jnp.where(k_seg[...] == q_seg[:, at], jnp.exp2(scores * (scale * math.log2(math.e))), 0.0)
+        probs = weight * (1.0 / jnp.sum(weight, axis=0, keepdims=True))
+        grad_probs = lax.dot_general(value[...], grad, flip, preferred_element_type=f32)
+        mean = jnp.sum(probs * grad_probs, axis=0, keepdims=True)
+        grad_scores = (probs * (grad_probs - mean)).astype(bf)
+        grad_key[...] += jnp.dot(grad_scores, ours, preferred_element_type=f32)
+        grad_value[...] += jnp.dot(probs.astype(bf), grad, preferred_element_type=f32)
+        grad_query = jnp.dot(key_t[...], grad_scores, preferred_element_type=f32).T * scale
+        heads[at, 0:128] = raw_grad(query_proj, query_gain, grad_query, at)
+
+    up_own = weights[pl.ds(2 * p, 2), :, 384:512].reshape(2 * depth, 128)
+    up_own = pltpu.roll(up_own.astype(f32), 64, 1).astype(bf)
+
+    @pl.loop(0, group // 2)
+    def _(b):
+        at = pl.ds(pl.multiple_of(b * span, span), span)
+        heads[at, 128:256] = raw_grad(key_proj, key_gain, grad_key[at] * scale, at)
+        heads[at, 256:384] = grad_value[at].astype(bf)
+
+    def to_sibling(c):
+        return pltpu.make_async_remote_copy(
+            src_ref=result.at[c, 1 - core], dst_ref=sib.at[c], send_sem=sib_send.at[c],
+            recv_sem=sib_recv.at[c], device_id=(place.sibling,), device_id_type=MESH)
+
+    def across(h, k, far):
+        return pltpu.make_async_remote_copy(
+            src_ref=cross_out.at[h, k, far], dst_ref=cross_in.at[h, k, far], send_sem=cross_send.at[h, k, far],
+            recv_sem=cross_recv.at[h, k, far], device_id=(place.last(h),), device_id_type=MESH)
+
+    def along(h, k):
+        return pltpu.make_async_remote_copy(
+            src_ref=z_out.at[h, k], dst_ref=z_in.at[h, k], send_sem=z_send.at[h, k],
+            recv_sem=z_recv.at[h, k], device_id=(across_z,), device_id_type=MESH)
+
+    def first(h):
+        return pltpu.make_async_remote_copy(
+            src_ref=first_out.at[h], dst_ref=first_in.at[h], send_sem=first_send.at[h],
+            recv_sem=first_recv.at[h], device_id=(place.first(h),), device_id_type=MESH)
+
+    def both(c, h):
+        part = pl.ds(h * half, half)
+        return result[c, core, part].astype(f32) + sib[c, part].astype(f32)
+
+    def pair_sum(c):
+        far, dx, dy = 1 - c // 4, c % 2, c // 2 % 2
+        to_sibling(c).wait_recv()
+        for h, away, k in ((0, dx, dy), (1, dy, dx)):
+            @pl.when(away == 1)
+            def _():
+                cross_out[h, k, far] = both(c, h).astype(bf)
+                across(h, k, far).start()
+
+    @pl.loop(0, group // 2 + 1)
+    def _(c):
+        @pl.when(c < group // 2)
+        def _():
+            far, dx, dy = 1 - c // 4, c % 2, c // 2 % 2
+            o = (z + far * (1 - 2 * z)) * 4 + place.chip_at(dx, dy, 0)
+            mine = heads[pl.ds(pl.multiple_of(o * span, span), span), :]
+            matrix = weights[...].reshape(2 * group * depth, 512)[:, 0:384]
+            part = lax.dot_general(mine, matrix, flip, preferred_element_type=f32)
+            result[c, :, :, 0:width] = part.astype(bf).reshape(2, rows, width)
+            low = jnp.zeros((span, 128), f32)
+            owner = lax.broadcasted_iota(jnp.int32, low.shape, 1) // rank
+            for j in range(3):
+                term = jnp.dot(mine[:, j * 128 : (j + 1) * 128], up_own, preferred_element_type=f32)
+                low = jnp.where(owner == j, term, low)
+            result[c, :, :, width:] = low.astype(bf).reshape(2, rows, 128)
+            to_sibling(c).start()
+
+        @pl.when(c >= 1)
+        def _():
+            pair_sum(c - 1)
+
+    @pl.loop(0, group // 2)
+    def _(e):
+        far, k, h = 1 - e // 4, e // 2 % 2, e % 2
+        c = (1 - far) * 4 + k * (2 - h)
+        across(h, k, far).wait_recv()
+        total = both(c, h) + cross_in[h, k, far].astype(f32)
+
+        @pl.when(far == 1)
+        def _():
+            z_out[h, k] = total.astype(bf)
+            along(h, k).start()
+
+        @pl.when(far == 0)
+        def _():
+            along(h, k).wait_recv()
+            whole = total + z_in[h, k].astype(f32)
+
+            @pl.when(k == 1)
+            def _():
+                first_out[h] = whole.astype(bf)
+                first(h).start()
+
+            @pl.when(k == 0)
+            def _():
+                out[pl.ds(h * half, half)] = whole
+
+    owner = lax.broadcasted_iota(jnp.int32, (128, 128), 0) // rank
+    up = jnp.zeros((128, 128), f32)
+    for j in range(3):
+        term = lax.dot_general(inner[...], heads[:, j * 128 : (j + 1) * 128], tall, preferred_element_type=f32)
+        up = jnp.where(owner == j, term, up)
+    up_terms[...] = up
+    for h in range(2):
+        first(h).wait_recv()
+        out[pl.ds(h * half, half)] += first_in[h].astype(f32)
+
+    @pl.loop(1, group)
+    def _(i):
+        to_head((p + i) % group).wait_send()
+
+    @pl.loop(0, group // 2)
+    def _(c):
+        to_sibling(c).wait_send()
+        across(c % 2, c // 2 % 2, c // 4).wait_send()
+
+        @pl.when(c < 4)
+        def _():
+            along(c % 2, c // 2).wait_send()
+
+        @pl.when(c < 2)
+        def _():
+            first(c).wait_send()
+
+
+def back(grad_mixed, weights, query, key, value, query_proj, key_proj, inner, cosine, sine,
+         query_gain, key_gain, q_seg, k_seg, rank):
+    rows, width = grad_mixed.shape
+    seq = query.shape[0]
+    group = seq // rows
+    bf, f32 = jnp.bfloat16, jnp.float32
+    dma = pltpu.SemaphoreType.DMA
+    vmem = pl.BlockSpec(memory_space=pltpu.VMEM)
+    wide = width + 128
+    piece = (rows // 2, wide)
+    return pl.pallas_call(
+        functools.partial(back_kernel, rows, rank),
+        out_shape=(jax.ShapeDtypeStruct((rows, wide), f32), jax.ShapeDtypeStruct((128, 128), f32)),
+        in_specs=[vmem] * 14,
+        out_specs=(vmem, vmem),
+        scratch_shapes=[
+            pltpu.VMEM((group, rows, 128), bf),
+            pltpu.VMEM((128, seq), bf),
+            pltpu.VMEM((seq, 128), f32),
+            pltpu.VMEM((seq, 128), f32),
+            pltpu.VMEM((seq, 384), bf),
+            pltpu.VMEM((group // 2, 2, rows, wide), bf),
+            pltpu.VMEM((group // 2, rows, wide), bf),
+            pltpu.VMEM((2, 2, 2) + piece, bf),
+            pltpu.VMEM((2, 2, 2) + piece, bf),
+            pltpu.VMEM((2, 2) + piece, bf),
+            pltpu.VMEM((2, 2) + piece, bf),
+            pltpu.VMEM((2,) + piece, bf),
+            pltpu.VMEM((2,) + piece, bf),
+            dma((group,)), dma((group,)), dma, dma((group // 2,)), dma((group // 2,)),
+            dma((2, 2, 2)), dma((2, 2, 2)), dma((2, 2)), dma((2, 2)), dma((2,)), dma((2,)),
+        ],
+        compiler_params=pltpu.CompilerParams(has_side_effects=True, vmem_limit_bytes=60 << 20),
+        name="back",
+    )(grad_mixed, weights, query, key, value, query_proj, key_proj, inner, cosine, sine,
+      query_gain, key_gain, q_seg, k_seg)
 
 
 def heads_plan(
@@ -804,72 +1288,38 @@
     ups = jnp.take(adapter_up_factors, sequence_adapter_index, axis=0)
     pair = jnp.concatenate(
         [
-            downs.transpose(2, 0, 1, 3).reshape(own_rows, seqs * slots),
-            ups.transpose(3, 0, 1, 2).reshape(own_rows, seqs * slots),
+            downs.transpose(0, 2, 1, 3).reshape(seqs, own_rows, slots),
+            ups.transpose(0, 3, 1, 2).reshape(seqs, own_rows, slots),
         ],
-        axis=1,
-    )
-    factors = lax.all_gather(pair, "fsdp", axis=0, tiled=True)
-    down_own = lax.dynamic_slice_in_dim(factors, sequence * slots, slots, 1)
-    up_own = lax.dynamic_slice_in_dim(factors, (seqs + sequence) * slots, slots, 1)
-    up_head = lax.dynamic_slice_in_dim(up_own, place * HEAD_DIM, HEAD_DIM, 0)
-
+        axis=2,
+    )
+    heads_w = jnp.concatenate(
+        [
+            weight.reshape(own_rows, group, HEAD_DIM)
+            for weight in (query_weight, key_weight, value_weight)
+        ],
+        axis=2,
+    ).transpose(1, 0, 2)
+    chosen = (routes[:, :, None] == jnp.arange(experts, dtype=jnp.int32)).astype(f32)
+    coeff = jnp.sum(gates[:, :, None] * chosen, axis=1)
     rows = tokens.astype(f32)
     normed = rms_scale(rows, attn_scale).astype(bf)
-    normed_all = lax.all_gather(normed, "fsdp", axis=0, tiled=True, axis_index_groups=groups)
-
-    stacked = jnp.concatenate([query_weight, key_weight, value_weight], axis=0)
-    copies = [stacked]
-    for other in range(1, seqs):
-        copies.append(
-            lax.ppermute(
-                stacked, "fsdp", [(i, (i + other * group) % devices) for i in range(devices)]
-            )
-        )
-    mine = own_columns(jnp.concatenate(copies, axis=0), "fsdp", groups)
-    mine = mine.reshape(group, seqs, 3, own_rows, HEAD_DIM)
-    order = (sequence - jnp.arange(seqs)) % seqs
-    mine = jnp.take(mine, order, axis=1).transpose(2, 1, 0, 3, 4).reshape(3, width, HEAD_DIM)
     output_matrix = lax.all_gather(output_weight, "fsdp", axis=0, tiled=True)
-
-    inner_all = matmul(normed_all, down_own).astype(bf)
-
-    def project(index):
-        inner = inner_all[:, index * rank : (index + 1) * rank]
-        up = up_head[:, index * rank : (index + 1) * rank]
-        return matmul(normed_all, mine[index]) + matmul(inner, up.T)
-
-    query_proj, key_proj, value_proj = project(0), project(1), project(2)
-    query = rotate(rms_scale(query_proj, query_scale), cosine, sine).astype(bf)
-    key = rotate(rms_scale(key_proj, key_scale), cosine, sine).astype(bf)
-    value = value_proj.astype(bf)
-    allowed = segment_row[:, None] == segment_row[None, :]
-    scores = jnp.where(allowed, matmul(query, key.T) * scale, -1e30)
-    maximum = jnp.max(scores, axis=-1, keepdims=True)
-    weights = jnp.exp(scores - maximum)
-    total = jnp.sum(weights, axis=-1, keepdims=True)
-    probs = weights / total
-    probs_low = probs.astype(bf)
-    mixed_head = matmul(probs_low, value).astype(bf)
-    mixed = lax.all_to_all(
-        mixed_head.reshape(group, rows_dev, HEAD_DIM),
-        "fsdp",
-        split_axis=0,
-        concat_axis=0,
-        axis_index_groups=groups,
-        tiled=True,
-    )
-    mixed = mixed.transpose(1, 0, 2).reshape(rows_dev, width)
+    turns = (jnp.concatenate([cosine, cosine], axis=1), jnp.concatenate([-sine, sine], axis=1))
+    head_gains = (query_scale.reshape(1, HEAD_DIM), key_scale.reshape(1, HEAD_DIM))
+    tall, flat = segment_row.reshape(SEQ_LEN, 1), segment_row.reshape(1, SEQ_LEN)
+    mixed, head_weights, query, key, value, query_proj, key_proj, inner_all, coeff_own = front(
+        normed, heads_w, pair, coeff.T.reshape(experts, 1, rows_dev), *turns, *head_gains, tall, flat, rank
+    )
+    weights = head_weights.reshape(width, 4 * HEAD_DIM)
+    down_own = weights[:, 3 * HEAD_DIM : 3 * HEAD_DIM + slots]
+    up_own = weights[:, 3 * HEAD_DIM + slots :]
     down_out = down_own[:, 3 * rank :]
     up_out = up_own[:, 3 * rank :]
     out_inner = matmul(mixed, down_out).astype(bf)
     middle = rows + matmul(mixed, output_matrix) + matmul(out_inner, up_out.T)
     normed_ffn = rms_scale(middle, ffn_scale).astype(bf)
 
-    chosen = (routes[:, :, None] == jnp.arange(experts, dtype=jnp.int32)).astype(f32)
-    coeff = jnp.sum(gates[:, :, None] * chosen, axis=1)
-    coeff_all = lax.all_gather(coeff.T, "fsdp", axis=0, tiled=False)
-    coeff_own = lax.dynamic_index_in_dim(coeff_all, device // 2, 1, keepdims=False).reshape(-1, 1)
     slab_gate = expert_gate_weight[0]
     slab_up = expert_up_weight[0]
     slab_down = expert_down_weight[0]
@@ -894,59 +1344,19 @@
 
     grad_inner_out = matmul(grad_attn, up_out).astype(bf)
     grad_mixed = matmul(grad_attn, output_matrix.T) + matmul(grad_inner_out, down_out.T)
-    grad_mixed = own_columns(grad_mixed.astype(bf), "fsdp", groups)
+    grad_mixed = grad_mixed.astype(bf)
     up_out_terms = matmul(out_inner.T, grad_attn)
     down_out_terms = matmul(grad_inner_out.T, mixed)
 
-    grad_probs = matmul(grad_mixed, value.T)
-    grad_scores = (
-        probs * (grad_probs - jnp.sum(probs * grad_probs, axis=-1, keepdims=True))
-    ).astype(bf)
-    grad_query = matmul(grad_scores, key) * scale
-    grad_key = matmul(grad_scores.T, query) * scale
-    grad_value = matmul(probs_low.T, grad_mixed)
-    back = jnp.concatenate(
-        [
-            rms_back(query_proj, query_scale, rotate_back(grad_query, cosine, sine)).astype(bf),
-            rms_back(key_proj, key_scale, rotate_back(grad_key, cosine, sine)).astype(bf),
-            grad_value.astype(bf),
-        ],
-        axis=1,
-    )
-    grad_partial = sum(
-        matmul(back[:, j * HEAD_DIM : (j + 1) * HEAD_DIM], mine[j].T) for j in range(3)
-    ).astype(bf)
-    inner_partial = jnp.concatenate(
-        [
-            matmul(back[:, j * HEAD_DIM : (j + 1) * HEAD_DIM], up_head[:, j * rank : (j + 1) * rank])
-            for j in range(3)
-        ],
-        axis=1,
-    )
-    grad_sum = lax.psum_scatter(
-        grad_partial, "fsdp", scatter_dimension=0, tiled=True, axis_index_groups=groups
-    ).astype(f32)
-    inner_sum = lax.psum_scatter(
-        jnp.pad(inner_partial, ((0, 0), (0, 128 - 3 * rank))),
-        "fsdp",
-        scatter_dimension=0,
-        tiled=True,
-        axis_index_groups=groups,
-    )
-    grad_inner = inner_sum[:, : 3 * rank].astype(bf)
+    sums, up_head_terms = back(
+        grad_mixed, head_weights, query, key, value, query_proj, key_proj, inner_all,
+        *turns, *head_gains, flat, tall, rank,
+    )
+    up_head_terms = up_head_terms[: 3 * rank]
+    grad_sum, grad_inner = sums[:, :width], sums[:, width : width + 3 * rank].astype(bf)
     grad_normed = grad_sum + matmul(grad_inner, down_own[:, : 3 * rank].T)
     grad_tokens = (grad_middle + rms_back(rows, attn_scale, grad_normed)).astype(bf)
 
-    up_head_terms = jnp.concatenate(
-        [
-            matmul(
-                inner_all[:, j * rank : (j + 1) * rank].T,
-                back[:, j * HEAD_DIM : (j + 1) * HEAD_DIM],
-            )
-            for j in range(3)
-        ],
-        axis=0,
-    )
     down_terms = jnp.concatenate([matmul(grad_inner.T, normed), down_out_terms], axis=0)
     head_slot = (jnp.arange(group) == place).astype(f32)
     up_terms = jnp.concatenate(

time: 846 us -> 663 us (0.78); the launches traced: 834 us -> 662 us
  Pallas kernels: 365 us -> 564 us
  waiting for transfers between devices: 220 us -> 24.5 us
  matrix products: 109 us -> 22 us
  blocking collectives: 45.2 us -> 0 us
  other arithmetic: 45.9 us -> 17.2 us
  starting transfers between devices: 20.9 us -> 7.81 us
    pallas_call x0 -> x2, Pallas kernels: none -> 225 us  [the longest x1 140 us: front(): pl.pallas_call(functools.partial(front_kernel, rows, rank), out_shape=(ja...]
    dot_general x29 -> x7, matrix products: 106 us -> 18 us  [matmul(): return jnp.dot(left, right, preferred_element_type=jnp.float32)]
    reduce_scatter x2 -> x0, waiting for transfers between devices: 79.1 us -> none  [the longest x1 64.2 us: heads_plan(): lax.psum_scatter(grad_partial, 'fsdp', scatter_dimension=0, tiled=True, a...]
    all_gather x2 -> x0, waiting for transfers between devices: 50.9 us -> none  [the longest x1 50.9 us: heads_plan(): lax.all_gather(normed, 'fsdp', axis=0, tiled=True, axis_index_groups=groups)]
    all_gather x1 -> x0, blocking collectives: 45.2 us -> none  [heads_plan(): coeff_all = lax.all_gather(coeff.T, 'fsdp', axis=0, tiled=False)]
    ppermute x1 -> x0, waiting for transfers between devices: 35.2 us -> none  [heads_plan(): lax.ppermute(stacked, 'fsdp', [(i, (i + other * group) % devices) for i i...]
    all_to_all x3 -> x0, waiting for transfers between devices: 27.5 us -> none  [the longest x2 27.5 us: own_columns(): lax.all_to_all(value, axis, split_axis=1, concat_axis=0, tiled=True, axis...]
    pallas_call x1, Pallas kernels: 162 us -> 146 us  [experts_forward(): pl.pallas_call(functools.partial(expert_kernel, rows), out_shape=(jax.Sha...]
  transfers between devices with their start and end apart: 11 -> 3, of which waited for: 7 -> 1; matrix products, arithmetic and copies ran while one was open for 13% -> 5% of each run, Pallas kernels for 21% -> 43%
where the time goes in v3:
time: 663 us; the launch traced here: 662 us
  Pallas kernels  564 us (85%)
  waiting for transfers between devices  24.5 us (4%)
  matrix products  22 us (3%)
  other arithmetic  17.2 us (3%)
  between operations  14.5 us (2%)
  local copies, waits for them, and re-layouts  12.7 us (2%)
  starting transfers between devices  7.81 us (1%)
    pallas_call x1, Pallas kernels, experts_forward(): pl.pallas_call(functools.partial(expert_kernel, rows), out_shape=(jax.Sha...  146 us
    pallas_call x1, Pallas kernels, front(): pl.pallas_call(functools.partial(front_kernel, rows, rank), out_shape=(ja...  140 us
    pallas_call x1, Pallas kernels, scatter_beside_backward(): pl.pallas_call(functools.partial(backward_kernel, rows), out_shape=(jax.S...  101 us
    pallas_call x1, Pallas kernels, scatter_all(): pl.pallas_call(functools.partial(scatter_kernel, rows, None), out_shape=j...  92.6 us
    pallas_call x1, Pallas kernels, back(): pl.pallas_call(functools.partial(back_kernel, rows, rank), out_shape=(jax...  84.7 us
    all_to_all x1, waiting for transfers between devices, heads_plan(): lax.all_to_all(terms.reshape(2 * slots, devices, own_rows).transpose(1, 0...  23.2 us
    dot_general x7, matrix products, matmul(): return jnp.dot(left, right, preferred_element_type=jnp.float32)  18 us
  transfers between devices with their start and end apart: 3, of which 1 were waited for; matrix products, arithmetic and copies ran while one was open for 5% of the time, Pallas kernels for 43%

profile of v3, /device:TPU:0, one launch (start us, length us, event | category | flops | bytes accessed | tf_op | source)
XLA Modules:
  0.0 662.4 jit_solution(10777625427804863807)
XLA Ops:
  7.3 0.7 all-gather.3.cloned.1.call-update
  8.0 0.7 all-gather.5.cloned.1.call-update
  8.8 0.7 fusion.36
  9.5 1.4 copy.60.q_seg.k_seg
  10.9 0.7 convert_element_type.68
  11.7 0.7 compare_select_fusion
  12.3 1.5 gather_fusion
  14.0 1.5 gather_fusion.1
  15.7 0.7 pad_maximum_fusion.2.pair
  16.4 0.6 select_reduce_fusion
  17.1 0.1 copy_bitcast_fusion
  17.3 1.0 maximum_bitcast_fusion.1.heads_w
  18.3 0.2 fusion.11
  18.5 0.5 bitcast_convert_fusion
  19.1 0.6 constant_dynamic-slice_fusion.k_seg.q_seg
  19.7 3.7 fusion.17
  23.4 1.9 pad_maximum_fusion
  25.3 1.0 fusion.5.normed
  26.3 140.1 %front.1 = (bf16[128,2048]{1,0:T(8,128)(2,1)}, bf16[32,64,512]{2,1,0:T(8,128)(2,1)}, bf16[2048,128]{1,0:T(8,128)(2,1)}, bf16[2048,128]{1,0:T(8,128)(2,1)}, bf16[...) custom-call(bf16[128,2048]{1,0:T(8,128)(2,1)} %fusion.5.normed, ...), custom_call_target="tpu_custom_call" | custom-call | tf_op jit(solution)/shard_map/front/pallas_call | solution.py:995
  166.4 2.8 copy.61.coeff
  169.4 1.6 convolution_convert_fusion.1
  171.0 4.7 convolution_add_fusion.3
  175.8 1.6 multiply_reduce_fusion.1
  177.3 1.0 multiply_convert_fusion.x_ref
  178.3 145.5 %experts_forward.1 = (bf16[32,128,2048]{2,1,0:T(8,128)(2,1)}, f32[32,128,512]{2,1,0:T(8,128)}, f32[32,128,512]{2,1,0:T(8,128)}) custom-call(bf16[128,2048]{1,0:T(8,128)(2,1)} %multiply_convert_fusion.x_ref, bf16[2048,512]{1,0:T(8,128)(2,1)} %bitcast.66, bf16[2048,512]{1,0:T(8,128)(2,1)} %bitcast.68, bf16[512,2048]{1,0:T(8,128)(2,1)} %bitcast.70, ...), custom_call_target="tpu_custom_call" | custom-call | tf_op jit(solution)/shard_map/experts_forward/pallas_call | solution.py:656
  323.9 100.7 %scatter_backward.1 = (f32[128,2048]{1,0:T(8,128)}, bf16[32,128,2048]{2,1,0:T(8,128)(2,1)}) custom-call(bf16[32,128,2048]{2,1,0:T(8,128)(2,1)} %get-tuple-element.23.source, bf16[32,128,2048]{2,1,0:T(8,128)(2,1)} %bitcast.65, f32[32,128,512]{2,1,0:T(8,128)} %get-tuple-element.24.a_in, f32[32,128,512]{2,1,0:T(8,128)} %get-tuple-element.25.b_in, ...), custom_call_target="tpu_custom_call" | custom-call | tf_op jit(solution)/shard_map/scatter_backward/pallas_call | solution.py:736
  424.6 92.6 %scatter_all.1 = f32[128,2048]{1,0:T(8,128)S(1)} custom-call(bf16[32,128,2048]{2,1,0:T(8,128)(2,1)} %get-tuple-element.27.source), custom_call_target="tpu_custom_call" | custom-call | tf_op jit(solution)/shard_map/scatter_all/pallas_call | solution.py:512
  517.2 0.3 multiply_reduce_fusion
  517.6 0.7 copy-done.8
  518.3 0.3 copy-done.9
  518.6 1.2 multiply_add_fusion
  519.8 0.6 copy-done.3
  520.4 0.6 convolution_convert_fusion
  521.0 1.4 fusion.20
  522.4 1.4 fusion.25
  523.7 6.3 fusion.23
  530.0 1.3 fusion.1.grad_mixed
  531.3 84.7 %back.1 = (f32[128,2176]{1,0:T(8,128)}, f32[128,128]{1,0:T(8,128)}) custom-call(bf16[128,2048]{1,0:T(8,128)(2,1)} %fusion.1.grad_mixed, bf16[32,64,512]{2,1,0:T(8,128)(2,1)} %get-tuple-element.21.weights, bf16[2048,128]{1,0:T(8,128)(2,1)} %get-tuple-element.28.query, bf16[2048,128]{1,0:T(8,128)(2,1)} %get-tuple-element.29.key, ...), custom_call_target="tpu_custom_call" | custom-call | tf_op jit(solution)/shard_map/back/pallas_call | solution.py:1216
  616.0 0.7 slice.35
  616.9 1.3 fusion.18
  618.3 0.1 broadcast_multiply_fusion
  618.5 1.9 maximum_bitcast_fusion
  620.4 7.7 %all-to-all-start = ((f32[32,128,64]{1,2,0:T(8,128)}), f32[32,128,64]{1,2,0:T(8,128)S(1)}, u32[]{:S(2)}, u32[]{:S(2)}) async-start(f32[32,128,64]{1,2,0:T(8,128)} %maximum_bitcast_fusion), calls=%async_computation | async-start | bytes 2097152 | tf_op jit(solution)/shard_map/all_to_all | solution.py:1370
  628.1 1.9 fusion.6
  630.0 1.2 fusion.10
  631.2 23.2 %all-to-all-done = f32[32,128,64]{1,2,0:T(8,128)S(1)} async-done(((f32[32,128,64]{1,2,0:T(8,128)}), f32[32,128,64]{1,2,0:T(8,128)S(1)}, u32[]{:S(2)}, u32[]{:S(2)}) %all-to-all-start) | async-done | bytes 1048608 | tf_op jit(solution)/shard_map/all_to_all | solution.py:1370
  654.5 0.2 copy.70
  654.7 0.8 slice_bitcast_fusion
  (61 shorter events, 1.2 us)
Async XLA Ops:
  7.2 9.9 %copy-start = (bf16[64,2048]{1,0:T(8,128)(2,1)S(1)}, bf16[64,2048]{1,0:T(8,128)(2,1)}, u32[]{:S(2)}) copy-start(bf16[64,2048]{1,0:T(8,128)(2,1)} %param.28) | copy-start | bytes 786436
  7.2 6.6 copy-start.16
  7.2 8.5 %copy-start.13 = (bf16[2048]{0:T(1024)(128)(2,1)S(1)}, bf16[2048]{0:T(1024)(128)(2,1)}, u32[]{:S(2)}) copy-start(bf16[2048]{0:T(1024)(128)(2,1)} %param.33) | copy-start | bytes 12292
  7.2 9.2 %copy-start.15 = (s32[128,8]{0,1:T(8,128)S(1)}, s32[128,8]{0,1:T(8,128)}, u32[]{:S(2)}) copy-start(s32[128,8]{0,1:T(8,128)} %param.21) | copy-start | bytes 12292
  7.2 9.2 %copy-start.14 = (f32[128,8]{0,1:T(8,128)S(1)}, f32[128,8]{0,1:T(8,128)}, u32[]{:S(2)}) copy-start(f32[128,8]{0,1:T(8,128)} %param.22) | copy-start | bytes 12292
  7.2 9.8 %copy-start.10 = (bf16[64,2048]{1,0:T(8,128)(2,1)S(1)}, bf16[64,2048]{1,0:T(8,128)(2,1)}, u32[]{:S(2)}) copy-start(bf16[64,2048]{1,0:T(8,128)(2,1)} %param.27) | copy-start | bytes 786436
  7.2 9.9 %copy-start.11 = (bf16[64,2048]{1,0:T(8,128)(2,1)S(1)}, bf16[64,2048]{1,0:T(8,128)(2,1)}, u32[]{:S(2)}) copy-start(bf16[64,2048]{1,0:T(8,128)(2,1)} %param.29) | copy-start | bytes 786436
  7.2 163.8 %all-gather.3.cloned.1.call-start = ((), (), s32[]{:S(2)}) async-start(), calls=%async_computation.1 | async-start | bytes 8650752 | tf_op jit(solution)/shard_map/all_gather | solution.py:1307
  8.0 315.9 %all-gather.5.cloned.1.call-start = ((), (), s32[]{:S(2)}) async-start(), calls=%async_computation.2 | async-start | bytes 17301504 | tf_op jit(solution)/shard_map/all_gather | solution.py:1326
  10.9 7.4 %copy-start.2 = (bf16[128,2048]{1,0:T(8,128)(2,1)S(1)}, bf16[128,2048]{1,0:T(8,128)(2,1)}, u32[]{:S(2)}) copy-start(bf16[128,2048]{1,0:T(8,128)(2,1)} %param.19) | copy-start | bytes 1572868
  13.8 4.7 copy-start.17
  13.8 4.7 copy-start.18
  13.8 5.2 copy-start.12
  166.4 3.0 copy-start.4
  517.2 1.0 copy-start.8
  517.2 1.4 copy-start.9
  518.6 1.8 copy-start.3
  531.3 85.6 %copy-start.5 = (bf16[128,2048]{1,0:T(8,128)(2,1)S(1)}, bf16[128,2048]{1,0:T(8,128)(2,1)}, u32[]{:S(2)}) copy-start(bf16[128,2048]{1,0:T(8,128)(2,1)} %fusion.5.normed) | copy-start | bytes 1572868
  616.9 1.6 copy-start.6
  616.9 1.6 copy-start.7
  620.4 34.0 %all-to-all-start = ((f32[32,128,64]{1,2,0:T(8,128)}), f32[32,128,64]{1,2,0:T(8,128)S(1)}, u32[]{:S(2)}, u32[]{:S(2)}) async-start(f32[32,128,64]{1,2,0:T(8,128)} %maximum_bitcast_fusion), calls=%async_computation | async-start | bytes 2097152 | tf_op jit(solution)/shard_map/all_to_all | solution.py:1370
  630.0 25.6 %copy-start.1 = (bf16[64,2048]{1,0:T(8,128)(2,1)S(1)}, bf16[64,2048]{1,0:T(8,128)(2,1)}, u32[]{:S(2)}) copy-start(bf16[64,2048]{1,0:T(8,128)(2,1)} %param.28) | copy-start | bytes 786436
Sparse Core Ops, SparseCore 0:
  10.9 113.5 all-gather.2
  127.4 166.6 all-gather.4

commit v4 on v3

--- a/solution.py
+++ b/solution.py
@@ -3,6 +3,7 @@
 
 import jax
 import jax.numpy as jnp
+import numpy as np
 from jax import lax
 from jax.experimental import pallas as pl
 from jax.experimental.pallas import tpu as pltpu
@@ -329,6 +330,7 @@
     return (output, grad_tokens, grad_down, grad_up)
 
 
+epsilon = 1e-06
 MESH = pl.DeviceIdType.MESH
 LEVELS = 4
 CHIPS = 16
@@ -520,243 +522,357 @@
     )(partial)
 
 
-def expert_kernel(rows, x_ref, gate_w, up_w, down_w, coeff, part_out, a_out, b_out,
-                  held, part_buf, a_buf, b_buf, own_sem, send, recv, out_sem):
+def experts_kernel(rows, x_ref, up_ref, gate_w, up_w, down_w, coeff, out, part_out, gathered,
+                   block, part_buf, result, sib, cross_out, cross_in, hold, z_in, first_out, first_in, total,
+                   local_sem, load_sem, part_sem, send, recv, sib_send, sib_recv, cross_send, cross_recv,
+                   z_send, z_recv, first_send, first_recv):
     place = Place()
-    half_rows = rows // 2
+    half = rows // 2
     f32, bf = jnp.float32, jnp.bfloat16
-    me = place.me
+    flip = (((1,), (1,)), ((), ()))
+    me, core = place.me, place.core
+    upper = place.z // 2
+    inner = place.z * (1 - upper) + (3 - place.z) * upper
     UP, DOWN, LAST, SIB, FIRST = range(5)
 
-    def move(h, o, kind, target):
-        d = 2 * o + place.core
-        part = pl.ds(h * half_rows, half_rows)
-        return pltpu.make_async_remote_copy(
-            src_ref=held.at[d, part], dst_ref=held.at[d, part], send_sem=send.at[kind, h, o],
-            recv_sem=recv.at[1 if kind == SIB else 0, h, o], device_id=(target,), device_id_type=MESH)
-
-    def arrived(h, o, sib):
-        d = 2 * o + (1 - place.core if sib else place.core)
-        part = pl.ds(h * half_rows, half_rows)
+    def move(n, h, o, kind, target):
+        piece = gathered.at[2 * o + core, h, n]
+        return pltpu.make_async_remote_copy(
+            src_ref=piece, dst_ref=piece, send_sem=send.at[kind, n, h, o],
+            recv_sem=recv.at[1 if kind == SIB else 0, n, h, o], device_id=(target,), device_id_type=MESH)
+
+    def arrived(n, h, o, sibling):
+        piece = gathered.at[2 * o + (1 - core if sibling else core), h, n]
         pltpu.make_async_remote_copy(
-            src_ref=held.at[d, part], dst_ref=held.at[d, part], send_sem=send.at[SIB, h, o],
-            recv_sem=recv.at[1 if sib else 0, h, o], device_id=(place.sibling,), device_id_type=MESH).wait_recv()
-
-    def spread(h, o, level, act):
+            src_ref=piece, dst_ref=piece, send_sem=send.at[SIB, n, h, o],
+            recv_sem=recv.at[1 if sibling else 0, n, h, o], device_id=(place.sibling,), device_id_type=MESH).wait_recv()
+
+    def column(n, h, o, level, act):
         @pl.when((level <= place.z) & (place.z < LEVELS - 1))
         def _():
-            act(move(h, o, UP, me + 8))
+            act(move(n, h, o, UP, me + 8))
 
         @pl.when((level >= place.z) & (place.z > 0))
         def _():
-            act(move(h, o, DOWN, me - 8))
-
-        act(move(h, o, LAST, place.last(h)))
-        act(move(h, o, SIB, place.sibling))
+            act(move(n, h, o, DOWN, me - 8))
+
+    def spread(n, h, o, level, act):
+        column(n, h, o, level, act)
+        act(move(n, h, o, LAST, place.last(h)))
+        act(move(n, h, o, SIB, place.sibling))
+
+    def to_sibling(u):
+        slot = u % 2
+        return pltpu.make_async_remote_copy(
+            src_ref=result.at[slot, 1 - core], dst_ref=sib.at[slot], send_sem=sib_send.at[slot],
+            recv_sem=sib_recv.at[slot], device_id=(place.sibling,), device_id_type=MESH)
+
+    def across(h, k, i):
+        return pltpu.make_async_remote_copy(
+            src_ref=cross_out.at[h, k, i % 2], dst_ref=cross_in.at[h, k, i], send_sem=cross_send.at[h, k, i],
+            recv_sem=cross_recv.at[h, k, i], device_id=(place.last(h),), device_id_type=MESH)
+
+    def along(h, k, level, up, slot):
+        return pltpu.make_async_remote_copy(
+            src_ref=hold.at[h, k, level], dst_ref=z_in.at[h, k, slot], send_sem=z_send.at[h, k, level],
+            recv_sem=z_recv.at[h, k, slot], device_id=(me - 8 + 16 * up,), device_id_type=MESH)
+
+    def first(h):
+        return pltpu.make_async_remote_copy(
+            src_ref=first_out.at[h], dst_ref=first_in.at[h], send_sem=first_send.at[h],
+            recv_sem=first_recv.at[h], device_id=(place.first(h),), device_id_type=MESH)
+
+    def down_slot(level):
+        ends = 1 - jnp.minimum(jnp.abs(level - (place.z - 1)), 1)
+        return level + ends * (LEVELS - level)
+
+    def order(u):
+        return u % 2, u // 2 % 2, place.level(u // 4)
 
     start = lambda copy: copy.start()
     done = lambda copy: copy.wait_send()
-    own = pltpu.make_async_copy(x_ref, held.at[me], own_sem)
-    own.start()
-    own.wait()
     mine = me // 2
-    for h in range(2):
-        move(h, mine, FIRST, place.first(h)).start()
-        spread(h, mine, place.z, start)
-    for h in range(2):
+    own = [
+        pltpu.make_async_copy(ref.at[pl.ds(h * half, half)], gathered.at[me, h, n], local_sem.at[n, h])
+        for n, ref in enumerate((x_ref, up_ref)) for h in range(2)
+    ]
+    for copy in own:
+        copy.start()
+    for copy in own:
+        copy.wait()
+    pieces = [(n, h) for n in range(2) for h in range(2)]
+    for n, h in pieces:
+        column(n, h, mine, place.z, start)
+        move(n, h, mine, FIRST, place.first(h)).start()
+    for n, h in pieces:
+        move(n, h, mine, LAST, place.last(h)).start()
+        move(n, h, mine, SIB, place.sibling).start()
+    for n, h in pieces:
         o = place.chip(h, 1, place.z)
-        arrived(h, o, False)
-        spread(h, o, place.z, start)
-
-    def cross(q):
-        level, dx, dy = place.level(q // 4), q % 2, q // 2 % 2
+        arrived(n, h, o, False)
+        spread(n, h, o, place.z, start)
+
+    def cross_arrivals(q):
+        dx, dy, level = order(q)
         o = place.chip_at(dx, dy, level)
         for h, away in ((0, dx), (1, dy)):
             @pl.when(away == 1)
             def _():
-                arrived(h, o, False)
-                move(h, o, SIB, place.sibling).start()
-
-    def outputs(t, slot):
-        o = place.chip_at(t % 2, t // 2 % 2, place.level(t // 4))
-        two = pl.ds(2 * o, 2)
-        return (
-            pltpu.make_async_copy(part_buf.at[slot], part_out.at[two], out_sem.at[slot, 0]),
-            pltpu.make_async_copy(a_buf.at[slot], a_out.at[two], out_sem.at[slot, 1]),
-            pltpu.make_async_copy(b_buf.at[slot], b_out.at[two], out_sem.at[slot, 2]),
-        )
-
-    @pl.loop(0, CHIPS)
-    def _(t):
-        @pl.when(t < CHIPS - 4)
-        def _():
-            level, h, k = place.level(1 + t // 4), t % 2, t // 2 % 2
-            o = place.chip(h, k, level)
-            arrived(h, o, False)
-            spread(h, o, level, start)
-
-        @pl.when(t + 1 < CHIPS)
-        def _():
-            cross(t + 1)
-
-        o = place.chip_at(t % 2, t // 2 % 2, place.level(t // 4))
-        for h in range(2):
-            arrived(h, o, True)
-        slot = t % 2
-
-        @pl.when(t >= 2)
-        def _():
-            for copy in outputs(t - 2, slot):
-                copy.wait()
-
-        x = held[pl.ds(2 * o, 2)].reshape(2 * rows, -1)
+                for n in range(2):
+                    arrived(n, h, o, False)
+                    move(n, h, o, SIB, place.sibling).start()
+
+    def keep_part(u):
+        dx, dy, level = order(u)
+        o = place.chip_at(dx, dy, level)
+        return pltpu.make_async_copy(part_buf.at[u % 2], part_out.at[o], part_sem.at[u % 2])
+
+    def compute(u):
+        dx, dy, level = order(u)
+        o = place.chip_at(dx, dy, level)
+        for n, h in pieces:
+            arrived(n, h, o, True)
+        load = pltpu.make_async_copy(gathered.at[pl.ds(2 * o, 2)], block, load_sem)
+        load.start()
+
+        @pl.when(u >= 2)
+        def _():
+            to_sibling(u - 2).wait_send()
+
+        load.wait()
+        slot = u % 2
+        c = coeff[pl.ds(2 * o, 2)].reshape(2 * rows, 1)
+        x = block[:, :, 0].reshape(2 * rows, -1)
         gate = jnp.dot(x, gate_w[...], preferred_element_type=f32)
         up = jnp.dot(x, up_w[...], preferred_element_type=f32)
         sig = jax.nn.sigmoid(gate)
         silu = gate * sig
         hidden = (silu * up).astype(bf)
-        a_buf[slot] = (up * sig * (1.0 + gate * (1.0 - sig))).reshape(2, rows, -1)
-        b_buf[slot] = silu.reshape(2, rows, -1)
-        c = coeff[pl.ds(2 * o, 2)].reshape(2 * rows, 1)
-        part = jnp.dot(hidden, down_w[...], preferred_element_type=f32)
-        part_buf[slot] = (c * part).astype(bf).reshape(2, rows, -1)
-        for copy in outputs(t, slot):
-            copy.start()
-
-    for t in (CHIPS - 2, CHIPS - 1):
-        for copy in outputs(t, t % 2):
-            copy.wait()
+        part = (c * jnp.dot(hidden, down_w[...], preferred_element_type=f32)).astype(bf)
+        part = part.reshape(2, 2, half, -1)
+        result[slot, 0, 1] = part[0]
+        result[slot, 1, 1] = part[1]
+        upstream = (c * block[:, :, 1].reshape(2 * rows, -1).astype(f32)).astype(bf)
+        grad_hidden = lax.dot_general(upstream, down_w[...], flip, preferred_element_type=f32)
+        grad_gate = (grad_hidden * up * sig * (1.0 + gate * (1.0 - sig))).astype(bf)
+        grad_up = (grad_hidden * silu).astype(bf)
+        grad = lax.dot_general(grad_gate, gate_w[...], flip, preferred_element_type=f32)
+        grad += lax.dot_general(grad_up, up_w[...], flip, preferred_element_type=f32)
+        grad = grad.astype(bf).reshape(2, 2, half, -1)
+        result[slot, 0, 0] = grad[0]
+        result[slot, 1, 0] = grad[1]
+
+    def pair_sum(u):
+        dx, dy, level = order(u)
+        i, slot = u // 4, u % 2
+        to_sibling(u).wait_recv()
+
+        def pair(n, h):
+            return (result[slot, core, n, h].astype(f32) + sib[slot, n, h].astype(f32)).astype(bf)
+
+        for h, away, k in ((0, dx, dy), (1, dy, dx)):
+            @pl.when(away == 1)
+            def _():
+                @pl.when(i >= 2)
+                def _():
+                    across(h, k, i - 2).wait_send()
+
+                cross_out[h, k, i % 2] = pair(0, h)
+                across(h, k, i).start()
+
+            @pl.when(away == 0)
+            def _():
+                hold[h, k, level] = pair(0, h)
+
+        @pl.when(u >= 2)
+        def _():
+            keep_part(u - 2).wait()
+
+        for h in range(2):
+            part_buf[slot, h] = pair(1, h)
+        keep_part(u).start()
+
+    def column_event(e):
+        late = e // 8
+        i_end = e // 4
+        j_end = e % 4
+        i_mid = (e // 4) * (1 - late) + (2 + e % 2) * late
+        j_mid = (e % 4) * (1 - late) + ((e - 8) // 2) * late
+        turn_end = i_end + 1 - 4 * (i_end // 3)
+        level_end = turn_end + upper * (3 - 2 * turn_end)
+        turn_mid = 2 - i_mid + (i_mid // 2) * 3 - (i_mid // 3) * 2
+        level_mid = turn_mid + upper * (3 - 2 * turn_mid)
+        j = j_end + inner * (j_mid - j_end)
+        level = level_end + inner * (level_mid - level_end)
+        return j % 2, j // 2, level
+
+    def column_sum(e):
+        h, k, level = column_event(e)
+        turn = level + upper * (3 - 2 * level)
+        i = turn + inner * (1 - 2 * turn) * (1 - jnp.minimum(turn // 2, 1))
+        across(h, k, i).wait_recv()
+        total[...] = hold[h, k, level].astype(f32) + cross_in[h, k, i].astype(f32)
+
+        @pl.when((level >= place.z) & (place.z > 0))
+        def _():
+            along(h, k, level, 1, level).wait_recv()
+            total[...] += z_in[h, k, level].astype(f32)
+
+        @pl.when((level < place.z) & (place.z < LEVELS - 1))
+        def _():
+            along(h, k, level, 0, level).wait_recv()
+            total[...] += z_in[h, k, level].astype(f32)
+
+        @pl.when((level == place.z) & (place.z < LEVELS - 1))
+        def _():
+            along(h, k, level, 0, LEVELS).wait_recv()
+            total[...] += z_in[h, k, LEVELS].astype(f32)
+
+        @pl.when(level > place.z)
+        def _():
+            hold[h, k, level] = total[...].astype(bf)
+            along(h, k, level, 1, level).start()
+
+        @pl.when(level < place.z)
+        def _():
+            hold[h, k, level] = total[...].astype(bf)
+            along(h, k, level, 0, down_slot(level)).start()
+
+        @pl.when((level == place.z) & (k == 1))
+        def _():
+            first_out[h] = total[...].astype(bf)
+            first(h).start()
+
+        @pl.when((level == place.z) & (k == 0))
+        def _():
+            out[h] = total[...]
+
+    @pl.loop(0, 2 * CHIPS - 1)
+    def _(u):
+        @pl.when((u >= 1) & (u < CHIPS - 3))
+        def _():
+            t = u - 1
+            level, h, k = place.level(1 + t // 4), t % 2, t // 2 % 2
+            o = place.chip(h, k, level)
+            for n in range(2):
+                arrived(n, h, o, False)
+                spread(n, h, o, level, start)
+
+        @pl.when(u + 1 < CHIPS)
+        def _():
+            cross_arrivals(u + 1)
+
+        @pl.when(u < CHIPS)
+        def _():
+            compute(u)
+
+        @pl.when((u >= 1) & (u <= CHIPS))
+        def _():
+            pair_sum(u - 1)
+
+        @pl.when(u < CHIPS)
+        def _():
+            to_sibling(u).start()
+
+        e = u - 7 - 8 * inner
+
+        @pl.when((e >= 0) & (e < CHIPS))
+        def _():
+            column_sum(e)
 
     for h in range(2):
-        move(h, mine, FIRST, place.first(h)).wait_send()
-        spread(h, mine, place.z, done)
-        spread(h, place.chip(h, 1, place.z), place.z, done)
+        first(h).wait_recv()
+        out[h] += first_in[h].astype(f32)
+
+    for n, h in pieces:
+        move(n, h, mine, FIRST, place.first(h)).wait_send()
+        spread(n, h, mine, place.z, done)
+        spread(n, h, place.chip(h, 1, place.z), place.z, done)
+    for h in range(2):
+        first(h).wait_send()
+    for u in (CHIPS - 2, CHIPS - 1):
+        to_sibling(u).wait_send()
+        keep_part(u).wait()
 
     @pl.loop(0, CHIPS)
     def _(t):
+        h, k = t % 2, t // 2 % 2
+
         @pl.when(t < CHIPS - 4)
         def _():
-            level, h, k = place.level(1 + t // 4), t % 2, t // 2 % 2
-            spread(h, place.chip(h, k, level), level, done)
-
-        dx, dy = t % 2, t // 2 % 2
-        o = place.chip_at(dx, dy, place.level(t // 4))
-        for h, away in ((0, dx), (1, dy)):
+            level = place.level(1 + t // 4)
+            for n in range(2):
+                spread(n, h, place.chip(h, k, level), level, done)
+
+        dx, dy, level = order(t)
+        o = place.chip_at(dx, dy, level)
+        for side, away in ((0, dx), (1, dy)):
             @pl.when(away == 1)
             def _():
-                move(h, o, SIB, place.sibling).wait_send()
-
-
-def experts_forward(x, gate_w, up_w, down_w, coeff):
+                for n in range(2):
+                    move(n, side, o, SIB, place.sibling).wait_send()
+
+        @pl.when(t >= 8)
+        def _():
+            across(h, k, t // 4).wait_send()
+
+        level = t // 4
+
+        @pl.when(level > place.z)
+        def _():
+            along(h, k, level, 1, level).wait_send()
+
+        @pl.when(level < place.z)
+        def _():
+            along(h, k, level, 0, down_slot(level)).wait_send()
+
+
+def experts_pass(x, upstream, gate_w, up_w, down_w, coeff):
     rows, width = x.shape
-    devices, hidden = coeff.shape[0], gate_w.shape[1]
+    devices = coeff.shape[0]
+    half = rows // 2
     bf, f32 = jnp.bfloat16, jnp.float32
     dma = pltpu.SemaphoreType.DMA
     vmem, anywhere = pl.BlockSpec(memory_space=pltpu.VMEM), pl.BlockSpec(memory_space=pl.ANY)
-    return pl.pallas_call(
-        functools.partial(expert_kernel, rows),
+    piece = (half, width)
+    grad, part, _ = pl.pallas_call(
+        functools.partial(experts_kernel, rows),
         out_shape=(
-            jax.ShapeDtypeStruct((devices, rows, width), bf),
-            jax.ShapeDtypeStruct((devices, rows, hidden), f32),
-            jax.ShapeDtypeStruct((devices, rows, hidden), f32),
+            jax.ShapeDtypeStruct((2,) + piece, f32),
+            jax.ShapeDtypeStruct((CHIPS, 2) + piece, bf),
+            jax.ShapeDtypeStruct((devices, 2, 2) + piece, bf),
         ),
-        in_specs=[anywhere, vmem, vmem, vmem, vmem],
-        out_specs=(anywhere, anywhere, anywhere),
+        in_specs=[anywhere, anywhere, vmem, vmem, vmem, vmem],
+        out_specs=(vmem, anywhere, anywhere),
         scratch_shapes=[
-            pltpu.VMEM((devices, rows, width), bf),
-            pltpu.VMEM((2, 2, rows, width), bf),
-            pltpu.VMEM((2, 2, rows, hidden), f32),
-            pltpu.VMEM((2, 2, rows, hidden), f32),
-            dma, dma((5, 2, CHIPS)), dma((2, 2, CHIPS)), dma((2, 3)),
+            pltpu.VMEM((2, 2, 2) + piece, bf),
+            pltpu.VMEM((2, 2) + piece, bf),
+            pltpu.VMEM((2, 2, 2, 2) + piece, bf),
+            pltpu.VMEM((2, 2, 2) + piece, bf),
+            pltpu.VMEM((2, 2, 2) + piece, bf),
+            pltpu.VMEM((2, 2, LEVELS) + piece, bf),
+            pltpu.VMEM((2, 2, LEVELS) + piece, bf),
+            pltpu.VMEM((2, 2, LEVELS + 1) + piece, bf),
+            pltpu.VMEM((2,) + piece, bf),
+            pltpu.VMEM((2,) + piece, bf),
+            pltpu.VMEM(piece, f32),
+            dma((2, 2)), dma, dma((2,)), dma((5, 2, 2, CHIPS)), dma((2, 2, 2, CHIPS)), dma((2,)), dma((2,)),
+            dma((2, 2, LEVELS)), dma((2, 2, LEVELS)),
+            dma((2, 2, LEVELS)), dma((2, 2, LEVELS + 1)), dma((2,)), dma((2,)),
         ],
         compiler_params=pltpu.CompilerParams(has_side_effects=True, vmem_limit_bytes=56 << 20),
-        name="experts_forward",
-    )(x, gate_w, up_w, down_w, coeff)
-
-
-def backward_kernel(rows, source, upstream, a_in, b_in, gate_w, up_w, down_w, coeff, out, grad_out, *scratch):
-    scatter, (u_buf, a_buf, b_buf, g_buf, in_sem, out_sem) = scratch[:-6], scratch[-6:]
-    f32, bf = jnp.float32, jnp.bfloat16
-    flip = (((1,), (1,)), ((), ()))
-
-    def inputs(t, slot):
-        two = pl.ds(2 * t, 2)
-        return (
-            pltpu.make_async_copy(upstream.at[two], u_buf.at[slot], in_sem.at[slot, 0]),
-            pltpu.make_async_copy(a_in.at[two], a_buf.at[slot], in_sem.at[slot, 1]),
-            pltpu.make_async_copy(b_in.at[two], b_buf.at[slot], in_sem.at[slot, 2]),
-        )
-
-    def output(t, slot):
-        return pltpu.make_async_copy(g_buf.at[slot], grad_out.at[pl.ds(2 * t, 2)], out_sem.at[slot])
-
-    def work(t):
-        @pl.when(t == 0)
-        def _():
-            for copy in inputs(0, 0):
-                copy.start()
-
-        @pl.when(t < CHIPS)
-        def _():
-            slot = t % 2
-
-            @pl.when(t + 1 < CHIPS)
-            def _():
-                for copy in inputs(t + 1, 1 - slot):
-                    copy.start()
-
-            for copy in inputs(t, slot):
-                copy.wait()
-
-            @pl.when(t >= 2)
-            def _():
-                output(t - 2, slot).wait()
-
-            c = coeff[pl.ds(2 * t, 2)].reshape(2 * rows, 1)
-            part = (c * u_buf[slot].reshape(2 * rows, -1).astype(f32)).astype(bf)
-            grad_hidden = lax.dot_general(part, down_w[...], flip, preferred_element_type=f32)
-            grad_gate = (grad_hidden * a_buf[slot].reshape(2 * rows, -1)).astype(bf)
-            grad_up = (grad_hidden * b_buf[slot].reshape(2 * rows, -1)).astype(bf)
-            grad = lax.dot_general(grad_gate, gate_w[...], flip, preferred_element_type=f32)
-            grad += lax.dot_general(grad_up, up_w[...], flip, preferred_element_type=f32)
-            g_buf[slot] = grad.astype(bf).reshape(2, rows, -1)
-            output(t, slot).start()
-
-    scatter_kernel(rows, work, source, out, *scatter)
-    for t in (CHIPS - 2, CHIPS - 1):
-        output(t, t % 2).wait()
-
-
-def scatter_beside_backward(partial, upstream, a, b, gate_w, up_w, down_w, coeff):
-    devices, rows, width = partial.shape
-    hidden = gate_w.shape[1]
-    bf, f32 = jnp.bfloat16, jnp.float32
-    dma = pltpu.SemaphoreType.DMA
-    vmem, anywhere = pl.BlockSpec(memory_space=pltpu.VMEM), pl.BlockSpec(memory_space=pl.ANY)
-    return pl.pallas_call(
-        functools.partial(backward_kernel, rows),
-        out_shape=(
-            jax.ShapeDtypeStruct((rows, width), f32),
-            jax.ShapeDtypeStruct((devices, rows, width), bf),
-        ),
-        in_specs=[anywhere] * 4 + [vmem] * 4,
-        out_specs=(vmem, anywhere),
-        scratch_shapes=scatter_scratch(rows, width) + [
-            pltpu.VMEM((2, 2, rows, width), bf),
-            pltpu.VMEM((2, 2, rows, hidden), f32),
-            pltpu.VMEM((2, 2, rows, hidden), f32),
-            pltpu.VMEM((2, 2, rows, width), bf),
-            dma((2, 3)), dma((2,)),
-        ],
-        compiler_params=pltpu.CompilerParams(has_side_effects=True, vmem_limit_bytes=60 << 20),
-        name="scatter_backward",
-    )(partial, upstream, a, b, gate_w, up_w, down_w, coeff)
-
-
-def front_kernel(rows, rank, normed, heads_w, pair, coeff, cosine, sine, query_gain, key_gain, q_seg, k_seg,
-                 mixed, weights, query_out, key_out, value_out, query_proj, key_proj, inner_out, coeff_out,
-                 held, mixed_buf,
-                 local_sem, send, recv, w_send, w_recv, pair_send, pair_recv, c_send, c_recv, m_send, m_recv, m_local):
+        name="experts",
+    )(x, upstream, gate_w, up_w, down_w, coeff)
+    return grad.reshape(rows, width), part
+
+
+def front_kernel(rows, rank, picked, tokens, rows_gain, heads_w, downs, ups, routes, gates, out_w, near, far_turn,
+                 query_gain, key_gain, ffn_gain, q_seg, k_seg,
+                 middle, normed_ffn, normed, mixed, out_inner, weights, query_out, key_out, value_out,
+                 query_proj, key_proj, inner_out, coeff_out, cosine, sine, out_all,
+                 held, mixed_buf, pair, coeff, wo,
+                 local_sem, send, recv, w_send, w_recv, pair_send, pair_recv, c_send, c_recv, m_send, m_recv, m_local,
+                 g_send, g_recv, keep_sem):
     place = Place()
     f32, bf = jnp.float32, jnp.bfloat16
     me, core = place.me, place.core
@@ -810,28 +926,90 @@
     pair_other = pltpu.make_async_remote_copy(
         src_ref=pair.at[other // group], dst_ref=weights.at[me, :, pl.ds(wide, 128)], send_sem=pair_send.at[2, 0],
         recv_sem=pair_recv.at[me], device_id=(other,), device_id_type=MESH)
-    locals_ = [
-        pltpu.make_async_copy(normed, held.at[p], local_sem.at[0]),
-        pltpu.make_async_copy(pair.at[me // group], weights.at[me, :, pl.ds(wide, 128)], local_sem.at[1]),
-        pltpu.make_async_copy(heads_w.at[p], weights.at[me, :, pl.ds(0, wide)], local_sem.at[2]),
-        pltpu.make_async_copy(coeff.at[me // 2], coeff_out.at[me], local_sem.at[3]),
+    UP, DOWN, G_LAST, G_SIB, G_FIRST = range(5)
+
+    def g_move(h, o, kind, target):
+        piece = wo.at[2 * o + core, h]
+        return pltpu.make_async_remote_copy(
+            src_ref=piece, dst_ref=piece, send_sem=g_send.at[kind, h, o],
+            recv_sem=g_recv.at[1 if kind == G_SIB else 0, h, o], device_id=(target,), device_id_type=MESH)
+
+    def g_arrived(h, o, sibling):
+        piece = wo.at[2 * o + (1 - core if sibling else core), h]
+        pltpu.make_async_remote_copy(
+            src_ref=piece, dst_ref=piece, send_sem=g_send.at[G_SIB, h, o],
+            recv_sem=g_recv.at[1 if sibling else 0, h, o], device_id=(place.sibling,), device_id_type=MESH).wait_recv()
+
+    def g_column(h, o, level, act):
+        @pl.when((level <= place.z) & (place.z < LEVELS - 1))
+        def _():
+            act(g_move(h, o, UP, me + 8))
+
+        @pl.when((level >= place.z) & (place.z > 0))
+        def _():
+            act(g_move(h, o, DOWN, me - 8))
+
+    def g_spread(h, o, level, act):
+        g_column(h, o, level, act)
+        act(g_move(h, o, G_LAST, place.last(h)))
+        act(g_move(h, o, G_SIB, place.sibling))
+
+    def g_level(t):
+        level, h, k = place.level(1 + t // 4), t % 2, t // 2 % 2
+        o = place.chip(h, k, level)
+        g_arrived(h, o, False)
+        g_spread(h, o, level, start)
+
+    def g_cross(q):
+        dx, dy = q % 2, q // 2 % 2
+        o = place.chip_at(dx, dy, place.level(q // 4))
+        for h, away in ((0, dx), (1, dy)):
+            @pl.when(away == 1)
+            def _():
+                g_arrived(h, o, False)
+                g_move(h, o, G_SIB, place.sibling).start()
+
+    start = lambda copy: copy.start()
+    done = lambda copy: copy.wait_send()
+    own_chip = me // 2
+    own_copies = [
+        pltpu.make_async_copy(heads_w.at[p], weights.at[me, :, pl.ds(0, wide)], local_sem.at[0]),
+        pltpu.make_async_copy(out_w.at[pl.ds(0, depth // 2)], wo.at[me, 0], local_sem.at[1]),
+        pltpu.make_async_copy(out_w.at[pl.ds(depth // 2, depth // 2)], wo.at[me, 1], local_sem.at[2]),
     ]
-    for copy in locals_:
+    for copy in own_copies:
         copy.start()
-    pair_other.start()
-
-    @pl.loop(0, group)
-    def _(i):
-        to_heads(other_base + (p + i) % group).start()
-
-    locals_[0].wait()
+    ours = tokens[...].astype(f32)
+    low = (ours * lax.rsqrt(jnp.mean(ours * ours, axis=-1, keepdims=True) + epsilon) * rows_gain[...]).astype(bf)
+    held[p] = low
+    normed[...] = low
     for h in range(2):
         move(h, chip, FIRST, place.first(h)).start()
         move(h, chip, ALONG, across_z).start()
     for h in range(2):
         move(h, chip, LAST, place.last(h)).start()
         move(h, chip, SIB, place.sibling).start()
-    locals_[1].wait()
+
+    for s in range(2):
+        down, up = downs[picked[s]].astype(f32), ups[picked[s]].astype(f32)
+        down = jnp.concatenate([down[j] for j in range(4)], axis=1)
+        up = jnp.concatenate([up[j] for j in range(4)], axis=0).T
+        pair[s] = jnp.concatenate([down, up], axis=1).astype(bf)
+    weights[me, :, wide:] = pair[me // group]
+    pair_other.start()
+
+    @pl.loop(0, group)
+    def _(i):
+        to_heads(other_base + (p + i) % group).start()
+
+    lane = lax.broadcasted_iota(jnp.int32, (rows, 128), 1)
+    gate = jnp.zeros((rows, 128), f32)
+    for k in range(routes.shape[1]):
+        gate += jnp.where(lane == routes[:, k : k + 1], gates[:, k : k + 1], 0.0)
+    gate = gate.T
+    for e in range(coeff.shape[0]):
+        coeff[e] = gate[e : e + 1]
+    coeff_out[me] = coeff[me // 2]
 
     @pl.loop(1, group)
     def _(i):
@@ -841,6 +1019,15 @@
     @pl.loop(1, 2 * group)
     def _(i):
         to_expert((me + i) % (2 * group)).start()
+
+    for copy in own_copies[1:]:
+        copy.wait()
+    for h in range(2):
+        g_column(h, own_chip, place.z, start)
+        g_move(h, own_chip, G_FIRST, place.first(h)).start()
+    for h in range(2):
+        g_move(h, own_chip, G_LAST, place.last(h)).start()
+        g_move(h, own_chip, G_SIB, place.sibling).start()
 
     pltpu.make_async_remote_copy(
         src_ref=pair.at[0], dst_ref=weights.at[other, :, pl.ds(wide, 128)], send_sem=pair_send.at[2, 0],
@@ -862,6 +1049,19 @@
             arrived(h, o, False)
             move(h, o, LAST, place.last(h)).start()
             move(h, o, SIB, place.sibling).start()
+    for h in range(2):
+        o = place.chip(h, 1, place.z)
+        g_arrived(h, o, False)
+        g_spread(h, o, place.z, start)
+
+    @pl.loop(0, group)
+    def _(i):
+        at = pl.ds(pl.multiple_of(i * rows, rows), rows)
+        c, s = far_turn[0, pl.ds(i, 1)], far_turn[1, pl.ds(i, 1)]
+        cosine[at] = c * near[0] - s * near[1]
+        turn = s * near[0] + c * near[1]
+        sine[at] = jnp.where(lane < 64, -turn, turn)
+
     for far in range(2):
         for k in range(2):
             for h in range(2):
@@ -869,8 +1069,12 @@
                 o = (z + far * (1 - 2 * z)) * 4 + place.chip_at(dx, dy, 0)
                 arrived(h, o, False)
                 move(h, o, SIB, place.sibling).start()
-    for copy in locals_[2:]:
-        copy.wait()
+    own_copies[0].wait()
+
+    @pl.loop(0, 4)
+    def _(t):
+        g_level(t)
+
 
     @pl.loop(1, 2 * group)
     def _(i):
@@ -893,6 +1097,10 @@
         for h in range(2):
             arrived(h, o, True)
 
+    @pl.loop(4, 8)
+    def _(t):
+        g_level(t)
+
     span = 2 * rows
     seq = group * rows
     up_own = weights[pl.ds(2 * p, 2), :, pl.ds(wide, 128)].reshape(2 * depth, 128)
@@ -919,6 +1127,10 @@
             unit = value * lax.rsqrt(jnp.mean(value * value, axis=-1, keepdims=True) + epsilon) * gain[...]
             rot[at] = (unit * cosine[at] + pltpu.roll(unit, 64, 1) * sine[at]).astype(bf)
         value_out[at] = projected(2).astype(bf)
+
+        @pl.when(b % 2 == 0)
+        def _():
+            g_level(8 + b // 2)
 
     def to_token(q):
         return pltpu.make_async_remote_copy(
@@ -946,6 +1158,9 @@
             def _():
                 keep.start()
 
+        g_cross(2 * b)
+        g_cross(2 * b + 1)
+
     keep.wait()
 
     @pl.loop(1, group)
@@ -954,6 +1169,46 @@
         pltpu.make_async_remote_copy(
             src_ref=mixed_buf.at[q], dst_ref=mixed.at[:, pl.ds(q * 128, 128)], send_sem=m_send.at[q],
             recv_sem=m_recv.at[q], device_id=(base + q,), device_id_type=MESH).wait_recv()
+
+    @pl.loop(0, CHIPS)
+    def _(o):
+        for h in range(2):
+            g_arrived(h, o, True)
+
+    keep_out = pltpu.make_async_copy(wo, out_all, keep_sem)
+    keep_out.start()
+    ours = mixed[...]
+    matrix = weights[:, :, wide:].reshape(2 * group * depth, 128)
+    lane = lax.broadcasted_iota(jnp.int32, (rows, 128), 1)
+    inner = jnp.dot(ours, matrix, preferred_element_type=f32)
+    inner = jnp.where(lane // rank == 3, inner, 0.0).astype(bf)
+    out_inner[...] = inner
+    shifted = pltpu.roll(inner.astype(f32), 64, 1).astype(bf)
+    total = tokens[...].astype(f32) + jnp.dot(ours, wo[...].reshape(2 * group * depth, -1), preferred_element_type=f32)
+    total = total + lax.dot_general(shifted, matrix, flip, preferred_element_type=f32)
+    middle[...] = total
+    unit = total * lax.rsqrt(jnp.mean(total * total, axis=-1, keepdims=True) + epsilon)
+    normed_ffn[...] = (unit * ffn_gain[...]).astype(bf)
+
+    keep_out.wait()
+    for h in range(2):
+        g_move(h, own_chip, G_FIRST, place.first(h)).wait_send()
+        g_spread(h, own_chip, place.z, done)
+        g_spread(h, place.chip(h, 1, place.z), place.z, done)
+
+    @pl.loop(0, CHIPS)
+    def _(t):
+        @pl.when(t < CHIPS - 4)
+        def _():
+            level, h, k = place.level(1 + t // 4), t % 2, t // 2 % 2
+            g_spread(h, place.chip(h, k, level), level, done)
+
+        dx, dy = t % 2, t // 2 % 2
+        o = place.chip_at(dx, dy, place.level(t // 4))
+        for h, away in ((0, dx), (1, dy)):
+            @pl.when(away == 1)
+            def _():
+                g_move(h, o, G_SIB, place.sibling).wait_send()
 
     pair_other.wait_send()
     for h in range(2):
@@ -983,40 +1238,66 @@
         to_expert(q).wait_send()
 
 
-def front(normed, heads_w, pair, coeff, cosine, sine, query_gain, key_gain, q_seg, k_seg, rank):
-    rows, width = normed.shape
+def turn_tables(rows, group):
+    frequency = rope_base ** (-(np.arange(64, dtype=np.float32) * np.float32(2.0 / 128)))
+    frequency = np.concatenate([frequency, frequency]).astype(np.float64)
+    tables = []
+    for positions in (np.arange(rows), np.arange(group) * rows):
+        angle = positions[:, None] * frequency[None, :]
+        tables.append(np.stack([np.cos(angle), np.sin(angle)]).astype(np.float32))
+    return tables
+
+
+def front(picked, tokens, rows_gain, heads_w, downs, ups, routes, gates, out_w, query_gain, key_gain, ffn_gain, q_seg, k_seg):
+    rows, width = tokens.shape
     group, depth = heads_w.shape[0], heads_w.shape[1]
+    rank = downs.shape[3]
     devices, seq = 2 * group, rows * group
     bf, f32 = jnp.bfloat16, jnp.float32
     dma = pltpu.SemaphoreType.DMA
     vmem, anywhere = pl.BlockSpec(memory_space=pltpu.VMEM), pl.BlockSpec(memory_space=pl.ANY)
     head = jax.ShapeDtypeStruct((seq, 128), bf)
     raw = jax.ShapeDtypeStruct((seq, 128), f32)
+    mine = jax.ShapeDtypeStruct((rows, width), bf)
+    near, far_turn = turn_tables(rows, group)
     return pl.pallas_call(
         functools.partial(front_kernel, rows, rank),
         out_shape=(
-            jax.ShapeDtypeStruct((rows, width), bf),
+            jax.ShapeDtypeStruct((rows, width), f32), mine, mine, mine,
+            jax.ShapeDtypeStruct((rows, 128), bf),
             jax.ShapeDtypeStruct((devices, depth, 512), bf),
             head, head, head, raw, raw, head,
             jax.ShapeDtypeStruct((devices, 1, rows), f32),
+            raw, raw,
+            jax.ShapeDtypeStruct((devices, 2, depth // 2, width), bf),
         ),
-        in_specs=[anywhere] * 4 + [vmem] * 6,
-        out_specs=(vmem,) * 9,
+        in_specs=[pl.BlockSpec(memory_space=pltpu.SMEM), vmem, vmem, anywhere, vmem, vmem, vmem, vmem, anywhere]
+        + [vmem] * 7,
+        out_specs=(vmem,) * 15 + (anywhere,),
         scratch_shapes=[
             pltpu.VMEM((group, rows, width), bf),
             pltpu.VMEM((group, rows, 128), bf),
-            dma((4,)), dma((4, 2, group // 2)), dma((2, 2, group // 2)),
+            pltpu.VMEM((2, depth, 128), bf),
+            pltpu.VMEM((group, 1, rows), f32),
+            pltpu.VMEM((devices, 2, depth // 2, width), bf),
+            dma((3,)), dma((4, 2, group // 2)), dma((2, 2, group // 2)),
             dma((devices,)), dma((devices,)), dma((3, group)), dma((devices,)),
             dma((devices,)), dma((devices,)), dma((group,)), dma((group,)), dma,
+            dma((5, 2, CHIPS)), dma((2, 2, CHIPS)), dma,
         ],
-        compiler_params=pltpu.CompilerParams(has_side_effects=True, vmem_limit_bytes=56 << 20),
+        compiler_params=pltpu.CompilerParams(has_side_effects=True, vmem_limit_bytes=60 << 20),
         name="front",
-    )(normed, heads_w, pair, coeff, cosine, sine, query_gain, key_gain, q_seg, k_seg)
-
-
-def back_kernel(rows, rank, grad_mixed, weights, query, key, value, query_proj, key_proj, inner, cosine, sine,
-                query_gain, key_gain, q_seg, k_seg, out, up_terms,
+    )(picked, tokens, rows_gain, heads_w, downs, ups, routes, gates, out_w, jnp.asarray(near), jnp.asarray(far_turn),
+      query_gain, key_gain, ffn_gain, q_seg, k_seg)
+
+
+def back_kernel(rows, rank, grad_mixed, part, weights, query, key, value, query_proj, key_proj, inner, cosine, sine,
+                query_gain, key_gain, q_seg, k_seg, rows_in, normed, rows_gain, grad_middle, middle, early,
+                grad_rows, output, factors, out, up_terms, part_sum, late, early_in, late_in, owned,
+                e_send, e_recv, l_send, l_recv, f_send, f_recv, t_local,
                 grads, key_t, grad_key, grad_value, heads, result, sib, cross_out, cross_in, z_out, z_in, first_out, first_in,
+                held, part_in, part_z, part_total, part_first_out, part_first_in,
+                held_sem, pc_send, pc_recv, pz_send, pz_recv, pf_send, pf_recv,
                 a_send, a_recv, a_local, sib_send, sib_recv, cross_send, cross_recv, z_send, z_recv, first_send, first_recv):
     place = Place()
     f32, bf = jnp.float32, jnp.bfloat16
@@ -1032,6 +1313,76 @@
     tall = (((0,), (0,)), ((), ()))
     scale = 1.0 / math.sqrt(128)
 
+    def keep_piece(h, k, level):
+        return pltpu.make_async_copy(part.at[place.chip(h, k, level), h], held.at[h, k, level], held_sem.at[h, k, level])
+
+    def part_across(h, k, level):
+        dx, dy = (1, k) if h == 0 else (k, 1)
+        return pltpu.make_async_remote_copy(
+            src_ref=part.at[place.chip_at(dx, dy, level), h], dst_ref=part_in.at[h, k, level],
+            send_sem=pc_send.at[h, k, level], recv_sem=pc_recv.at[h, k, level],
+            device_id=(place.last(h),), device_id_type=MESH)
+
+    def crossed(h, k, level):
+        return pltpu.make_async_remote_copy(
+            src_ref=held.at[h, k, level], dst_ref=part_in.at[h, k, level], send_sem=pc_send.at[h, k, level],
+            recv_sem=pc_recv.at[h, k, level], device_id=(place.last(h),), device_id_type=MESH)
+
+    def part_along(h, k, level, up, slot):
+        return pltpu.make_async_remote_copy(
+            src_ref=held.at[h, k, level], dst_ref=part_z.at[h, k, slot], send_sem=pz_send.at[h, k, level],
+            recv_sem=pz_recv.at[h, k, slot], device_id=(me - 8 + 16 * up,), device_id_type=MESH)
+
+    def part_first(h):
+        return pltpu.make_async_remote_copy(
+            src_ref=part_first_out.at[h], dst_ref=part_first_in.at[h], send_sem=pf_send.at[h],
+            recv_sem=pf_recv.at[h], device_id=(place.first(h),), device_id_type=MESH)
+
+    def down_slot(level):
+        ends = 1 - jnp.minimum(jnp.abs(level - (place.z - 1)), 1)
+        return level + ends * (LEVELS - level)
+
+    def part_event(e):
+        h, k, level = e % 2, e // 2 % 2, place.level(3 - e // 4)
+        keep_piece(h, k, level).wait()
+        crossed(h, k, level).wait_recv()
+        total = held[h, k, level].astype(f32) + part_in[h, k, level].astype(f32)
+        part_total[...] = total
+
+        @pl.when((level >= place.z) & (place.z > 0))
+        def _():
+            part_along(h, k, level, 1, level).wait_recv()
+            part_total[...] += part_z[h, k, level].astype(f32)
+
+        @pl.when((level < place.z) & (place.z < LEVELS - 1))
+        def _():
+            part_along(h, k, level, 0, level).wait_recv()
+            part_total[...] += part_z[h, k, level].astype(f32)
+
+        @pl.when((level == place.z) & (place.z < LEVELS - 1))
+        def _():
+            part_along(h, k, level, 0, LEVELS).wait_recv()
+            part_total[...] += part_z[h, k, LEVELS].astype(f32)
+
+        @pl.when(level > place.z)
+        def _():
+            held[h, k, level] = part_total[...].astype(bf)
+            part_along(h, k, level, 1, level).start()
+
+        @pl.when(level < place.z)
+        def _():
+            held[h, k, level] = part_total[...].astype(bf)
+            part_along(h, k, level, 0, down_slot(level)).start()
+
+        @pl.when((level == place.z) & (k == 1))
+        def _():
+            part_first_out[h] = part_total[...].astype(bf)
+            part_first(h).start()
+
+        @pl.when((level == place.z) & (k == 0))
+        def _():
+            part_sum[h] = part_total[...]
+
     def to_head(q):
         return pltpu.make_async_remote_copy(
             src_ref=grad_mixed.at[:, pl.ds(q * 128, 128)], dst_ref=grads.at[p], send_sem=a_send.at[q],
@@ -1044,10 +1395,42 @@
 
     keep = pltpu.make_async_copy(grad_mixed.at[:, pl.ds(p * 128, 128)], grads.at[p], a_local)
     keep.start()
+
+    def early_to(q, frm):
+        return pltpu.make_async_remote_copy(
+            src_ref=early.at[:, pl.ds(q * 128, 128)], dst_ref=early_in.at[frm], send_sem=e_send.at[q],
+            recv_sem=e_recv.at[frm], device_id=(base + q,), device_id_type=MESH)
+
+    def late_to(q, frm):
+        return pltpu.make_async_remote_copy(
+            src_ref=late.at[:, pl.ds(q * 128, 128)], dst_ref=late_in.at[frm], send_sem=l_send.at[q],
+            recv_sem=l_recv.at[frm], device_id=(base + q,), device_id_type=MESH)
+
+    def to_owner(side, q, frm):
+        return pltpu.make_async_remote_copy(
+            src_ref=owned, dst_ref=factors.at[frm], send_sem=f_send.at[side],
+            recv_sem=f_recv.at[frm], device_id=(q,), device_id_type=MESH)
+
+    early_keep = pltpu.make_async_copy(early.at[:, pl.ds(p * 128, 128)], early_in.at[p], t_local.at[0])
+    late_keep = pltpu.make_async_copy(late.at[:, pl.ds(p * 128, 128)], late_in.at[p], t_local.at[1])
+    owned_keep = pltpu.make_async_copy(owned, factors.at[me // group], t_local.at[2])
+    early_keep.start()
 
     @pl.loop(1, group)
     def _(i):
         to_head((p + i) % group).start()
+
+    @pl.loop(1, group)
+    def _(i):
+        early_to((p + i) % group, p).start()
+
+    @pl.loop(0, 4)
+    def _(i):
+        level = place.level(3 - i)
+        for k in range(2):
+            for h in range(2):
+                part_across(h, k, level).start()
+                keep_piece(h, k, level).start()
 
     key_t[...] = key[...].astype(f32).T.astype(bf)
     grad_key[...] = jnp.zeros_like(grad_key)
@@ -1084,6 +1467,7 @@
         grad_value[...] += jnp.dot(probs.astype(bf), grad, preferred_element_type=f32)
         grad_query = jnp.dot(key_t[...], grad_scores, preferred_element_type=f32).T * scale
         heads[at, 0:128] = raw_grad(query_proj, query_gain, grad_query, at)
+        part_event(b)
 
     up_own = weights[pl.ds(2 * p, 2), :, 384:512].reshape(2 * depth, 128)
     up_own = pltpu.roll(up_own.astype(f32), 64, 1).astype(bf)
@@ -1148,6 +1532,7 @@
         @pl.when(c >= 1)
         def _():
             pair_sum(c - 1)
+            part_event(group // 2 + c - 1)
 
     @pl.loop(0, group // 2)
     def _(e):
@@ -1184,10 +1569,90 @@
     for h in range(2):
         first(h).wait_recv()
         out[pl.ds(h * half, half)] += first_in[h].astype(f32)
+    lane = lax.broadcasted_iota(jnp.int32, (rows, 128), 1)
+    grad_inner = jnp.where(lane < 3 * rank, out[:, width:], 0.0).astype(bf)
+    late[...] = lax.dot_general(grad_inner, normed[...], tall, preferred_element_type=f32)[: 3 * rank]
+    late_keep.start()
+
+    @pl.loop(1, group)
+    def _(i):
+        late_to((p + i) % group, p).start()
+
+    downs = weights[:, :, 384:512].reshape(2 * group * depth, 128)
+    grad_normed = out[:, 0:width] + lax.dot_general(grad_inner, downs, flip, preferred_element_type=f32)
+    ours = rows_in[...].astype(f32)
+    inverse = lax.rsqrt(jnp.mean(ours * ours, axis=-1, keepdims=True) + epsilon)
+    unit = ours * inverse
+    scaled = grad_normed * rows_gain[...]
+    grad = inverse * (scaled - unit * jnp.mean(scaled * unit, axis=-1, keepdims=True))
+    grad_rows[...] = (grad_middle[...] + grad).astype(bf)
+    early_keep.wait()
+    late_keep.wait()
+
+    @pl.loop(1, group)
+    def _(i):
+        q = (p + i) % group
+        early_to(q, q).wait_recv()
+        late_to(q, q).wait_recv()
+
+    sums = jnp.sum(early_in[...], axis=0)
+    owned[0 : 3 * rank] = jnp.sum(late_in[...], axis=0)
+    owned[3 * rank : 4 * rank] = sums[:rank]
+    owned[4 * rank : 7 * rank] = up_terms[0 : 3 * rank]
+    owned[7 * rank : 8 * rank] = sums[rank:]
+    for side in range(2):
+        q = 2 * p + side
+
+        @pl.when(q != me)
+        def _():
+            to_owner(side, q, me // group).start()
+
+        @pl.when(q == me)
+        def _():
+            owned_keep.start()
+
+    for h in range(2):
+        part_first(h).wait_recv()
+        side = pl.ds(h * half, half)
+        output[side] = (middle[side] + part_sum[h] + part_first_in[h].astype(f32)).astype(bf)
+    for s in range(2):
+        source = s * group + me // 2
+
+        @pl.when(source != me)
+        def _():
+            to_owner(0, source, s).wait_recv()
+
+        @pl.when(source == me)
+        def _():
+            owned_keep.wait()
 
     @pl.loop(1, group)
     def _(i):
         to_head((p + i) % group).wait_send()
+        early_to((p + i) % group, p).wait_send()
+        late_to((p + i) % group, p).wait_send()
+
+    for side in range(2):
+        @pl.when(2 * p + side != me)
+        def _():
+            to_owner(side, 2 * p + side, me // group).wait_send()
+
+    for h in range(2):
+        part_first(h).wait_send()
+
+    @pl.loop(0, 4)
+    def _(level):
+        for k in range(2):
+            for h in range(2):
+                part_across(h, k, level).wait_send()
+
+                @pl.when(level > place.z)
+                def _():
+                    part_along(h, k, level, 1, level).wait_send()
+
+                @pl.when(level < place.z)
+                def _():
+                    part_along(h, k, level, 0, down_slot(level)).wait_send()
 
     @pl.loop(0, group // 2)
     def _(c):
@@ -1203,8 +1668,8 @@
             first(c).wait_send()
 
 
-def back(grad_mixed, weights, query, key, value, query_proj, key_proj, inner, cosine, sine,
-         query_gain, key_gain, q_seg, k_seg, rank):
+def back(grad_mixed, part, weights, query, key, value, query_proj, key_proj, inner, cosine, sine,
+         query_gain, key_gain, q_seg, k_seg, rows_in, normed, rows_gain, grad_middle, middle, early, rank):
     rows, width = grad_mixed.shape
     seq = query.shape[0]
     group = seq // rows
@@ -1213,12 +1678,25 @@
     vmem = pl.BlockSpec(memory_space=pltpu.VMEM)
     wide = width + 128
     piece = (rows // 2, wide)
+    own = part.shape[2:]
     return pl.pallas_call(
         functools.partial(back_kernel, rows, rank),
-        out_shape=(jax.ShapeDtypeStruct((rows, wide), f32), jax.ShapeDtypeStruct((128, 128), f32)),
-        in_specs=[vmem] * 14,
-        out_specs=(vmem, vmem),
+        out_shape=(
+            jax.ShapeDtypeStruct((rows, width), bf),
+            jax.ShapeDtypeStruct((rows, width), bf),
+            jax.ShapeDtypeStruct((2, 8 * rank, 128), f32),
+        ),
+        in_specs=[vmem, pl.BlockSpec(memory_space=pl.ANY)] + [vmem] * 19,
+        out_specs=(vmem, vmem, vmem),
         scratch_shapes=[
+            pltpu.VMEM((rows, wide), f32),
+            pltpu.VMEM((128, 128), f32),
+            pltpu.VMEM((2,) + own, f32),
+            pltpu.VMEM((3 * rank, width), f32),
+            pltpu.VMEM((group, 2 * rank, 128), f32),
+            pltpu.VMEM((group, 3 * rank, 128), f32),
+            pltpu.VMEM((8 * rank, 128), f32),
+            dma((group,)), dma((group,)), dma((group,)), dma((group,)), dma((2,)), dma((2,)), dma((3,)),
             pltpu.VMEM((group, rows, 128), bf),
             pltpu.VMEM((128, seq), bf),
             pltpu.VMEM((seq, 128), f32),
@@ -1232,13 +1710,21 @@
             pltpu.VMEM((2, 2) + piece, bf),
             pltpu.VMEM((2,) + piece, bf),
             pltpu.VMEM((2,) + piece, bf),
+            pltpu.VMEM((2, 2, LEVELS) + own, bf),
+            pltpu.VMEM((2, 2, LEVELS) + own, bf),
+            pltpu.VMEM((2, 2, LEVELS + 1) + own, bf),
+            pltpu.VMEM(own, f32),
+            pltpu.VMEM((2,) + own, bf),
+            pltpu.VMEM((2,) + own, bf),
+            dma((2, 2, LEVELS)), dma((2, 2, LEVELS)), dma((2, 2, LEVELS)), dma((2, 2, LEVELS)), dma((2, 2, LEVELS + 1)),
+            dma((2,)), dma((2,)),
             dma((group,)), dma((group,)), dma, dma((group // 2,)), dma((group // 2,)),
             dma((2, 2, 2)), dma((2, 2, 2)), dma((2, 2)), dma((2, 2)), dma((2,)), dma((2,)),
         ],
-        compiler_params=pltpu.CompilerParams(has_side_effects=True, vmem_limit_bytes=60 << 20),
+        compiler_params=pltpu.CompilerParams(has_side_effects=True, vmem_limit_bytes=63 << 20),
         name="back",
-    )(grad_mixed, weights, query, key, value, query_proj, key_proj, inner, cosine, sine,
-      query_gain, key_gain, q_seg, k_seg)
+    )(grad_mixed, part, weights, query, key, value, query_proj, key_proj, inner, cosine, sine,
+      query_gain, key_gain, q_seg, k_seg, rows_in, normed, rows_gain, grad_middle, middle, early)
 
 
 def heads_plan(
@@ -1267,32 +1753,17 @@
     rows_dev, width = tokens.shape
     group = SEQ_LEN // rows_dev
     seqs = segments.shape[0]
-    experts = devices // 2
     rank = adapter_down_factors.shape[3]
     slots = 4 * rank
     own_rows = query_weight.shape[0]
     device = lax.axis_index("fsdp")
-    place = device % group
     sequence = device // group
-    groups = [list(range(s * group, (s + 1) * group)) for s in range(seqs)]
-    scale = 1.0 / math.sqrt(HEAD_DIM)
     segment_row = pick(segments, sequence)
-    cosine, sine = rope_tables(jnp.arange(SEQ_LEN, dtype=jnp.int32).astype(f32))
-    cosine, sine = cosine[:, 0], sine[:, 0]
     attn_scale = attention_norm_gain.astype(f32)
     query_scale = query_norm_gain.astype(f32)
     key_scale = key_norm_gain.astype(f32)
     ffn_scale = expert_norm_gain.astype(f32)
 
-    downs = jnp.take(adapter_down_factors, sequence_adapter_index, axis=0)
-    ups = jnp.take(adapter_up_factors, sequence_adapter_index, axis=0)
-    pair = jnp.concatenate(
-        [
-            downs.transpose(0, 2, 1, 3).reshape(seqs, own_rows, slots),
-            ups.transpose(0, 3, 1, 2).reshape(seqs, own_rows, slots),
-        ],
-        axis=2,
-    )
     heads_w = jnp.concatenate(
         [
             weight.reshape(own_rows, group, HEAD_DIM)
@@ -1300,44 +1771,24 @@
         ],
         axis=2,
     ).transpose(1, 0, 2)
-    chosen = (routes[:, :, None] == jnp.arange(experts, dtype=jnp.int32)).astype(f32)
-    coeff = jnp.sum(gates[:, :, None] * chosen, axis=1)
-    rows = tokens.astype(f32)
-    normed = rms_scale(rows, attn_scale).astype(bf)
-    output_matrix = lax.all_gather(output_weight, "fsdp", axis=0, tiled=True)
-    turns = (jnp.concatenate([cosine, cosine], axis=1), jnp.concatenate([-sine, sine], axis=1))
     head_gains = (query_scale.reshape(1, HEAD_DIM), key_scale.reshape(1, HEAD_DIM))
     tall, flat = segment_row.reshape(SEQ_LEN, 1), segment_row.reshape(1, SEQ_LEN)
-    mixed, head_weights, query, key, value, query_proj, key_proj, inner_all, coeff_own = front(
-        normed, heads_w, pair, coeff.T.reshape(experts, 1, rows_dev), *turns, *head_gains, tall, flat, rank
-    )
+    (middle, normed_ffn, normed, mixed, out_inner, head_weights, query, key, value, query_proj, key_proj, inner_all,
+     coeff_own, *turns, output_matrix) = front(
+        sequence_adapter_index, tokens, attn_scale.reshape(1, width), heads_w, adapter_down_factors,
+        adapter_up_factors, routes, gates, output_weight, *head_gains, ffn_scale.reshape(1, width), tall, flat,
+    )
+    output_matrix = output_matrix.reshape(width, width)
+    out_inner = out_inner[:, 3 * rank : slots]
     weights = head_weights.reshape(width, 4 * HEAD_DIM)
-    down_own = weights[:, 3 * HEAD_DIM : 3 * HEAD_DIM + slots]
-    up_own = weights[:, 3 * HEAD_DIM + slots :]
-    down_out = down_own[:, 3 * rank :]
-    up_out = up_own[:, 3 * rank :]
-    out_inner = matmul(mixed, down_out).astype(bf)
-    middle = rows + matmul(mixed, output_matrix) + matmul(out_inner, up_out.T)
-    normed_ffn = rms_scale(middle, ffn_scale).astype(bf)
+    down_out = weights[:, 3 * HEAD_DIM + 3 * rank : 3 * HEAD_DIM + slots]
+    up_out = weights[:, 3 * HEAD_DIM + slots + 3 * rank :]
 
     slab_gate = expert_gate_weight[0]
     slab_up = expert_up_weight[0]
     slab_down = expert_down_weight[0]
-    upstream_all = lax.all_gather(output_gradient, "fsdp", axis=0, tiled=True)
     coeff_own = coeff_own.reshape(devices, rows_dev, 1)
-    part, keep_gate, keep_up = experts_forward(normed_ffn, slab_gate, slab_up, slab_down, coeff_own)
-    moe, grad_slab = scatter_beside_backward(
-        part,
-        upstream_all.reshape(devices, rows_dev, width),
-        keep_gate,
-        keep_up,
-        slab_gate,
-        slab_up,
-        slab_down,
-        coeff_own,
-    )
-    grad_ffn = scatter_all(grad_slab)
-    output = (middle + moe).astype(bf)
+    grad_ffn, part = experts_pass(normed_ffn, output_gradient, slab_gate, slab_up, slab_down, coeff_own)
     upstream = output_gradient.astype(f32)
     grad_middle = upstream + rms_back(middle, ffn_scale, grad_ffn)
     grad_attn = grad_middle.astype(bf)
@@ -1348,33 +1799,13 @@
     up_out_terms = matmul(out_inner.T, grad_attn)
     down_out_terms = matmul(grad_inner_out.T, mixed)
 
-    sums, up_head_terms = back(
-        grad_mixed, head_weights, query, key, value, query_proj, key_proj, inner_all,
-        *turns, *head_gains, flat, tall, rank,
-    )
-    up_head_terms = up_head_terms[: 3 * rank]
-    grad_sum, grad_inner = sums[:, :width], sums[:, width : width + 3 * rank].astype(bf)
-    grad_normed = grad_sum + matmul(grad_inner, down_own[:, : 3 * rank].T)
-    grad_tokens = (grad_middle + rms_back(rows, attn_scale, grad_normed)).astype(bf)
-
-    down_terms = jnp.concatenate([matmul(grad_inner.T, normed), down_out_terms], axis=0)
-    head_slot = (jnp.arange(group) == place).astype(f32)
-    up_terms = jnp.concatenate(
-        [
-            (up_head_terms[:, None, :] * head_slot[None, :, None]).reshape(3 * rank, width),
-            up_out_terms,
-        ],
-        axis=0,
-    )
-    terms = jnp.concatenate([down_terms, up_terms], axis=0)
-    terms = lax.all_to_all(
-        terms.reshape(2 * slots, devices, own_rows).transpose(1, 0, 2),
-        "fsdp",
-        split_axis=0,
-        concat_axis=0,
-        tiled=True,
-    )
-    terms = jnp.sum(terms.reshape(seqs, group, 2 * slots, own_rows), axis=1)
+    grad_tokens, output, terms = back(
+        grad_mixed, part, head_weights, query, key, value, query_proj, key_proj, inner_all,
+        *turns, *head_gains, flat, tall,
+        tokens, normed, attn_scale.reshape(1, width), grad_middle, middle,
+        jnp.concatenate([down_out_terms, up_out_terms], axis=0), rank,
+    )
+    terms = lax.dynamic_slice_in_dim(terms, device % 2 * own_rows, own_rows, 2)
     selected = (
         jnp.arange(ADAPTER_COUNT, dtype=jnp.int32)[:, None] == sequence_adapter_index[None, :]
     ).astype(f32)

time: 663 us -> 586 us (0.88)
  waiting for transfers between devices: 24.5 us -> 0 us
  between operations: 14.5 us -> 0.96 us
  matrix products: 22 us -> 8.62 us
  other arithmetic: 17.2 us -> 5.67 us
  Pallas kernels: 564 us -> 553 us
  starting transfers between devices: 7.81 us -> 0 us
    pallas_call x3 -> x1, Pallas kernels: 339 us -> 270 us  [experts_pass(): pl.pallas_call(functools.partial(experts_kernel, rows), out_shape=(jax.Sh...]
    pallas_call x1, Pallas kernels: 84.7 us -> 153 us  [back(): pl.pallas_call(functools.partial(back_kernel, rows, rank), out_shape=(jax...]
    all_to_all x1 -> x0, waiting for transfers between devices: 23.2 us -> none  [heads_plan(): lax.all_to_all(terms.reshape(2 * slots, devices, own_rows).transpose(1, 0...]
    pallas_call x1, Pallas kernels: 140 us -> 131 us  [front(): pl.pallas_call(functools.partial(front_kernel, rows, rank), out_shape=(ja...]
    dot_general x7 -> x5, matrix products: 18 us -> 8.62 us  [matmul(): return jnp.dot(left, right, preferred_element_type=jnp.float32)]
    all_to_all x1 -> x0, starting transfers between devices: 7.73 us -> none  [heads_plan(): lax.all_to_all(terms.reshape(2 * slots, devices, own_rows).transpose(1, 0...]
  transfers between devices with their start and end apart: 3 -> 0, of which waited for: 1 -> 0; matrix products, arithmetic and copies ran while one was open for 5% -> 0% of each run, Pallas kernels for 43% -> 0%
where the time goes in v4:
time: 586 us; the launch traced here: 584 us
  Pallas kernels  553 us (94%)
  local copies, waits for them, and re-layouts  15.3 us (3%)
  matrix products  8.62 us (1%)
    pallas_call x1, Pallas kernels, experts_pass(): pl.pallas_call(functools.partial(experts_kernel, rows), out_shape=(jax.Sh...  270 us
    pallas_call x1, Pallas kernels, back(): pl.pallas_call(functools.partial(back_kernel, rows, rank), out_shape=(jax...  153 us
    pallas_call x1, Pallas kernels, front(): pl.pallas_call(functools.partial(front_kernel, rows, rank), out_shape=(ja...  131 us

profile of v4, /device:TPU:0, one launch (start us, length us, event | category | flops | bytes accessed | tf_op | source)
XLA Modules:
  0.0 583.9 jit_solution(17830474898473093472)
XLA Ops:
  0.6 0.0 copy-start
  0.7 0.8 fusion.15
  1.5 0.0 copy-start.19
  1.5 0.0 copy-start.20
  1.5 0.0 copy-start.15
  1.5 0.0 copy-start.12
  1.5 1.4 copy.43.q_seg.k_seg
  2.9 1.3 constant_dynamic-slice_fusion.1.k_seg.q_seg
  4.2 1.1 copy_bitcast_fusion
  5.3 0.0 copy-done.10
  5.3 0.1 copy_bitcast_fusion.2
  5.4 1.0 maximum_bitcast_fusion.heads_w
  6.4 0.6 convert_element_type.26
  7.0 0.0 copy-done.19
  7.0 0.5 bitcast_convert_fusion
  7.6 0.6 reshape.105
  8.2 1.0 copy.40.downs
  9.2 0.7 copy.41.routes
  9.9 0.7 copy.42.gates
  10.6 130.5 %front.1 = (f32[128,2048]{1,0:T(8,128)}, bf16[128,2048]{1,0:T(8,128)(2,1)}, bf16[128,2048]{1,0:T(8,128)(2,1)}, bf16[128,2048]{1,0:T(8,128)(2,1)}, bf16[128,128]{...) custom-call(s32[2]{0:T(128)} %picked.1, ...), custom_call_target="tpu_custom_call" | custom-call | tf_op jit(solution)/shard_map/front/pallas_call | solution.py:1263
  141.2 2.8 copy.44.coeff
  144.0 269.7 %experts.1 = (f32[2,64,2048]{2,1,0:T(8,128)}, bf16[16,2,64,2048]{3,2,1,0:T(8,128)(2,1)}, bf16[32,2,2,64,2048]{4,3,2,1,0:T(8,128)(2,1)}) custom-call(bf16[128,2048]{1,0:T(8,128)(2,1)} %get-tuple-element.26.x_ref, bf16[128,2048]{1,0:T(8,128)(2,1)} %up_ref.1, bf16[2048,512]{1,0:T(8,128)(2,1)} %bitcast.54, bf16[2048,512]{1,0:T(8,128)(2,1)} %bitcast.55, ...), custom_call_target="tpu_custom_call" | custom-call | tf_op jit(solution)/shard_map/experts/pallas_call | solution.py:838
  413.7 0.0 copy-start.6
  413.7 0.2 multiply_reduce_fusion.1
  413.9 0.0 copy-done.11
  413.9 1.6 multiply_reduce_fusion
  415.5 0.0 copy-done.5
  415.5 0.0 copy-done.6
  415.5 0.0 copy-start.7
  415.6 0.0 copy-start.13
  415.6 0.3 multiply_add_fusion.grad_middle
  415.9 0.0 copy-start.2
  415.9 1.6 copy-done.4
  417.5 0.6 convolution_convert_fusion
  418.1 0.2 fusion.10
  418.3 0.3 fusion.3
  418.6 0.7 pad_maximum_fusion.early
  419.3 6.3 %fusion.8 = f32[128,2048]{1,0:T(8,128)S(1)} fusion(bf16[2048,2048]{1,0:T(8,128)(2,1)} %bitcast.50, f32[128,2048]{1,0:T(8,128)S(1)} %multiply_add_fusion.grad_middle), kind=kOutput, calls=%fused_computation.29 | convolution fusion | flops 1074003968 | bytes 10485760 | tf_op jit(solution)/shard_map/dot_general | solution.py:29
  425.6 1.3 fusion.grad_mixed
  426.9 153.0 %back.1 = (bf16[128,2048]{1,0:T(8,128)(2,1)}, bf16[128,2048]{1,0:T(8,128)(2,1)}, f32[2,128,128]{2,1,0:T(8,128)}) custom-call(bf16[128,2048]{1,0:T(8,128)(2,1)} %fusion.grad_mixed, bf16[16,2,64,2048]{3,2,1,0:T(8,128)(2,1)} %get-tuple-element.31.part, bf16[32,64,512]{2,1,0:T(8,128)(2,1)} %get-tuple-element.30.weights, ...), custom_call_target="tpu_custom_call" | custom-call | tf_op jit(solution)/shard_map/back/pallas_call | solution.py:1682
  579.9 1.1 constant_dynamic-slice_fusion
  581.0 0.1 copy.46
  581.1 0.0 copy-start.1
  581.1 0.1 multiply_reduce_fusion.2
  581.2 0.2 copy.47
  581.4 0.8 slice_bitcast_fusion
  582.3 0.8 copy.56
  583.1 0.8 copy.57
  (29 shorter events, 0.1 us)
Async XLA Ops:
  0.6 3.6 copy-start
  0.6 4.7 copy-start.10
  1.5 4.9 copy-start.14
  1.5 5.5 copy-start.19
  1.5 5.5 copy-start.20
  1.5 6.1 %copy-start.15 = (bf16[2048]{0:T(1024)(128)(2,1)S(1)}, bf16[2048]{0:T(1024)(128)(2,1)}, u32[]{:S(2)}) copy-start(bf16[2048]{0:T(1024)(128)(2,1)} %param.26) | copy-start | bytes 12292
  1.5 6.7 %copy-start.12 = (bf16[8,4,64,16]{2,3,1,0:T(8,128)(2,1)S(1)}, bf16[8,4,64,16]{2,3,1,0:T(8,128)(2,1)}, u32[]{:S(2)}) copy-start(bf16[8,4,64,16]{2,3,1,0:T(8,128)(2,1)} %param.33) | copy-start | bytes 196612
  2.9 6.3 %copy-start.16 = (s32[128,8]{0,1:T(8,128)S(1)}, s32[128,8]{0,1:T(8,128)}, u32[]{:S(2)}) copy-start(s32[128,8]{0,1:T(8,128)} %param.23) | copy-start | bytes 12292
  2.9 7.0 %copy-start.17 = (f32[128,8]{0,1:T(8,128)S(1)}, f32[128,8]{0,1:T(8,128)}, u32[]{:S(2)}) copy-start(f32[128,8]{0,1:T(8,128)} %param.24) | copy-start | bytes 12292
  144.0 269.8 %copy-start.3 = (f32[128,2048]{1,0:T(8,128)S(1)}, f32[128,2048]{1,0:T(8,128)}, u32[]{:S(2)}) copy-start(f32[128,2048]{1,0:T(8,128)} %get-tuple-element.25.middle) | copy-start | bytes 3145732
  144.0 270.0 %copy-start.11 = (f32[2048]{0:T(1024)S(1)}, f32[2048]{0:T(1024)}, u32[]{:S(2)}) copy-start(f32[2048]{0:T(1024)} %convert_element_type.26) | copy-start | bytes 24580
  413.7 1.8 copy-start.5
  413.7 1.8 copy-start.6
  415.5 2.0 copy-start.4
  415.5 2.5 copy-start.7
  415.6 2.7 copy-start.13
  415.9 9.7 %copy-start.2 = (f32[128,2048]{1,0:T(8,128)}, f32[128,2048]{1,0:T(8,128)S(1)}, u32[]{:S(2)}) copy-start(f32[128,2048]{1,0:T(8,128)S(1)} %multiply_add_fusion.grad_middle) | copy-start | bytes 3145732
  426.9 154.2 %copy-start.18 = (s32[2]{0:T(128)S(1)}, s32[2]{0:T(128)}, u32[]{:S(2)}) copy-start(s32[2]{0:T(128)} %picked.1) | copy-start | bytes 28
  579.9 2.4 copy-start.9
  579.9 3.2 copy-start.8
  581.1 2.8 copy-start.1

commit v5 on v4

--- a/solution.py
+++ b/solution.py
@@ -522,6 +522,22 @@
     )(partial)
 
 
+OUTER_STEPS = (
+    278531, 8684081, 548864, 50372672, 13396561, 21889169, 33882149, 17581620, 9471010, 55600272, 39080084, 42346578,
+    38601784, 34932793, 11887841, 63513731, 35729961, 39868579, 48350861, 36731452, 45215881, 61890111, 49625245,
+    16334382, 37575933, 62463018, 50150443, 79059002, 44584191, 15537291, 48616602, 79246902, 35155759, 39409401,
+    39735847, 35482347, 64378152, 78529191, 47859943, 77196578, 76957479, 126075168, 126075360, 126075360, 126075360,
+    126075360, 126075360, 126075360, 126075360, 126075360, 126075360, 126075360,
+)
+INNER_STEPS = (
+    51829, 9699843, 13936708, 551028, 51423780, 9996900, 10502711, 17092868, 8408709, 16838712, 12658837, 21033529,
+    12912694, 11906089, 13410925, 27593879, 41985814, 35706924, 33850915, 8978567, 47562812, 39879804, 40139314,
+    38052989, 45162741, 16585263, 39357567, 18733167, 12130482, 22616686, 16319635, 33115890, 22886442, 11390570,
+    28079293, 38353539, 45742714, 15539854, 41500262, 32339182, 65596554, 40431279, 27123339, 78722744, 44953901,
+    75851499, 63856430, 76173993, 78209769, 76435697, 76693803, 76959526,
+)
+
+
 def experts_kernel(rows, x_ref, up_ref, gate_w, up_w, down_w, coeff, out, part_out, gathered,
                    block, part_buf, result, sib, cross_out, cross_in, hold, z_in, first_out, first_in, total,
                    local_sem, load_sem, part_sem, send, recv, sib_send, sib_recv, cross_send, cross_recv,
@@ -561,16 +577,15 @@
         act(move(n, h, o, LAST, place.last(h)))
         act(move(n, h, o, SIB, place.sibling))
 
-    def to_sibling(u):
-        slot = u % 2
+    def to_sibling(slot):
         return pltpu.make_async_remote_copy(
             src_ref=result.at[slot, 1 - core], dst_ref=sib.at[slot], send_sem=sib_send.at[slot],
             recv_sem=sib_recv.at[slot], device_id=(place.sibling,), device_id_type=MESH)
 
-    def across(h, k, i):
-        return pltpu.make_async_remote_copy(
-            src_ref=cross_out.at[h, k, i % 2], dst_ref=cross_in.at[h, k, i], send_sem=cross_send.at[h, k, i],
-            recv_sem=cross_recv.at[h, k, i], device_id=(place.last(h),), device_id_type=MESH)
+    def across(h, k, level):
+        return pltpu.make_async_remote_copy(
+            src_ref=cross_out.at[h, k, level], dst_ref=cross_in.at[h, k, level], send_sem=cross_send.at[h, k, level],
+            recv_sem=cross_recv.at[h, k, level], device_id=(place.last(h),), device_id_type=MESH)
 
     def along(h, k, level, up, slot):
         return pltpu.make_async_remote_copy(
@@ -585,9 +600,6 @@
     def down_slot(level):
         ends = 1 - jnp.minimum(jnp.abs(level - (place.z - 1)), 1)
         return level + ends * (LEVELS - level)
-
-    def order(u):
-        return u % 2, u // 2 % 2, place.level(u // 4)
 
     start = lambda copy: copy.start()
     done = lambda copy: copy.wait_send()
@@ -601,46 +613,20 @@
     for copy in own:
         copy.wait()
     pieces = [(n, h) for n in range(2) for h in range(2)]
-    for n, h in pieces:
-        column(n, h, mine, place.z, start)
-        move(n, h, mine, FIRST, place.first(h)).start()
-    for n, h in pieces:
-        move(n, h, mine, LAST, place.last(h)).start()
-        move(n, h, mine, SIB, place.sibling).start()
-    for n, h in pieces:
-        o = place.chip(h, 1, place.z)
-        arrived(n, h, o, False)
-        spread(n, h, o, place.z, start)
-
-    def cross_arrivals(q):
-        dx, dy, level = order(q)
-        o = place.chip_at(dx, dy, level)
-        for h, away in ((0, dx), (1, dy)):
-            @pl.when(away == 1)
-            def _():
-                for n in range(2):
-                    arrived(n, h, o, False)
-                    move(n, h, o, SIB, place.sibling).start()
-
-    def keep_part(u):
-        dx, dy, level = order(u)
-        o = place.chip_at(dx, dy, level)
-        return pltpu.make_async_copy(part_buf.at[u % 2], part_out.at[o], part_sem.at[u % 2])
-
-    def compute(u):
-        dx, dy, level = order(u)
-        o = place.chip_at(dx, dy, level)
+    def keep_part(o, slot):
+        return pltpu.make_async_copy(part_buf.at[slot], part_out.at[o], part_sem.at[slot])
+
+    def compute(o, slot, again):
         for n, h in pieces:
             arrived(n, h, o, True)
         load = pltpu.make_async_copy(gathered.at[pl.ds(2 * o, 2)], block, load_sem)
         load.start()
 
-        @pl.when(u >= 2)
-        def _():
-            to_sibling(u - 2).wait_send()
+        @pl.when(again)
+        def _():
+            to_sibling(slot).wait_send()
 
         load.wait()
-        slot = u % 2
         c = coeff[pl.ds(2 * o, 2)].reshape(2 * rows, 1)
         x = block[:, :, 0].reshape(2 * rows, -1)
         gate = jnp.dot(x, gate_w[...], preferred_element_type=f32)
@@ -661,11 +647,10 @@
         grad = grad.astype(bf).reshape(2, 2, half, -1)
         result[slot, 0, 0] = grad[0]
         result[slot, 1, 0] = grad[1]
-
-    def pair_sum(u):
-        dx, dy, level = order(u)
-        i, slot = u // 4, u % 2
-        to_sibling(u).wait_recv()
+        to_sibling(slot).start()
+
+    def pair_sum(dx, dy, level, slot, again):
+        to_sibling(slot).wait_recv()
 
         def pair(n, h):
             return (result[slot, core, n, h].astype(f32) + sib[slot, n, h].astype(f32)).astype(bf)
@@ -673,45 +658,26 @@
         for h, away, k in ((0, dx, dy), (1, dy, dx)):
             @pl.when(away == 1)
             def _():
-                @pl.when(i >= 2)
-                def _():
-                    across(h, k, i - 2).wait_send()
-
-                cross_out[h, k, i % 2] = pair(0, h)
-                across(h, k, i).start()
+                cross_out[h, k, level] = pair(0, h)
+                across(h, k, level).start()
 
             @pl.when(away == 0)
             def _():
                 hold[h, k, level] = pair(0, h)
 
-        @pl.when(u >= 2)
-        def _():
-            keep_part(u - 2).wait()
+        o = place.chip_at(dx, dy, level)
+
+        @pl.when(again)
+        def _():
+            keep_part(o, slot).wait()
 
         for h in range(2):
             part_buf[slot, h] = pair(1, h)
-        keep_part(u).start()
-
-    def column_event(e):
-        late = e // 8
-        i_end = e // 4
-        j_end = e % 4
-        i_mid = (e // 4) * (1 - late) + (2 + e % 2) * late
-        j_mid = (e % 4) * (1 - late) + ((e - 8) // 2) * late
-        turn_end = i_end + 1 - 4 * (i_end // 3)
-        level_end = turn_end + upper * (3 - 2 * turn_end)
-        turn_mid = 2 - i_mid + (i_mid // 2) * 3 - (i_mid // 3) * 2
-        level_mid = turn_mid + upper * (3 - 2 * turn_mid)
-        j = j_end + inner * (j_mid - j_end)
-        level = level_end + inner * (level_mid - level_end)
-        return j % 2, j // 2, level
-
-    def column_sum(e):
-        h, k, level = column_event(e)
-        turn = level + upper * (3 - 2 * level)
-        i = turn + inner * (1 - 2 * turn) * (1 - jnp.minimum(turn // 2, 1))
-        across(h, k, i).wait_recv()
-        total[...] = hold[h, k, level].astype(f32) + cross_in[h, k, i].astype(f32)
+        keep_part(o, slot).start()
+
+    def column_sum(h, k, level):
+        across(h, k, level).wait_recv()
+        total[...] = hold[h, k, level].astype(f32) + cross_in[h, k, level].astype(f32)
 
         @pl.when((level >= place.z) & (place.z > 0))
         def _():
@@ -747,38 +713,65 @@
         def _():
             out[h] = total[...]
 
-    @pl.loop(0, 2 * CHIPS - 1)
-    def _(u):
-        @pl.when((u >= 1) & (u < CHIPS - 3))
-        def _():
-            t = u - 1
-            level, h, k = place.level(1 + t // 4), t % 2, t // 2 % 2
-            o = place.chip(h, k, level)
-            for n in range(2):
+    def step(code):
+        kind, which = code // 32, code % 32
+        h, k, n = which % 2, which // 2 % 2, which // 16
+        turn = which // 4 % 4
+        level = turn + upper * (3 - 2 * turn)
+        o = place.chip(h, k, level)
+
+        @pl.when(kind == 0)
+        def _():
+            move(which // 2 % 2, h, mine, FIRST, place.first(h)).start()
+
+        @pl.when(kind == 1)
+        def _():
+            @pl.when((k == 1) | (level != place.z))
+            def _():
                 arrived(n, h, o, False)
-                spread(n, h, o, level, start)
-
-        @pl.when(u + 1 < CHIPS)
-        def _():
-            cross_arrivals(u + 1)
-
-        @pl.when(u < CHIPS)
-        def _():
-            compute(u)
-
-        @pl.when((u >= 1) & (u <= CHIPS))
-        def _():
-            pair_sum(u - 1)
-
-        @pl.when(u < CHIPS)
-        def _():
-            to_sibling(u).start()
-
-        e = u - 7 - 8 * inner
-
-        @pl.when((e >= 0) & (e < CHIPS))
-        def _():
-            column_sum(e)
+
+            move(n, h, o, LAST, place.last(h)).start()
+            move(n, h, o, SIB, place.sibling).start()
+
+        @pl.when((kind == 2) | (kind == 3))
+        def _():
+            down = (kind + upper) % 2
+            piece = gathered.at[2 * o + core, h, n]
+            pltpu.make_async_remote_copy(
+                src_ref=piece, dst_ref=piece, send_sem=send.at[down, n, h, o], recv_sem=recv.at[0, n, h, o],
+                device_id=(me + 8 - 16 * down,), device_id_type=MESH).start()
+
+        @pl.when(kind == 4)
+        def _():
+            away = place.chip_at(1 - h + h * k, k + h - h * k, level)
+            arrived(n, h, away, False)
+            move(n, h, away, SIB, place.sibling).start()
+
+        dx, dy = which % 2, which // 2 % 2
+
+        @pl.when((kind == 5) | (kind == 6))
+        def _():
+            compute(place.chip_at(dx, dy, level), which // 16, kind == 5)
+
+        @pl.when((kind == 7) | (kind == 8))
+        def _():
+            pair_sum(dx, dy, level, which // 16, kind == 7)
+
+        @pl.when(kind == 9)
+        def _():
+            column_sum(h, k, level)
+
+    @pl.loop(0, len(OUTER_STEPS))
+    def _(i):
+        word = 0
+        for at, (outer_word, inner_word) in enumerate(zip(OUTER_STEPS, INNER_STEPS)):
+            word = jnp.where(i == at, jnp.where(inner == 0, outer_word, inner_word), word)
+
+        def one(_, rest):
+            step(rest % 512)
+            return rest // 512
+
+        lax.fori_loop(0, 3, one, word)
 
     for h in range(2):
         first(h).wait_recv()
@@ -790,9 +783,9 @@
         spread(n, h, place.chip(h, 1, place.z), place.z, done)
     for h in range(2):
         first(h).wait_send()
-    for u in (CHIPS - 2, CHIPS - 1):
-        to_sibling(u).wait_send()
-        keep_part(u).wait()
+    for slot in range(2):
+        to_sibling(slot).wait_send()
+        keep_part(0, slot).wait()
 
     @pl.loop(0, CHIPS)
     def _(t):
@@ -804,19 +797,16 @@
             for n in range(2):
                 spread(n, h, place.chip(h, k, level), level, done)
 
-        dx, dy, level = order(t)
-        o = place.chip_at(dx, dy, level)
+        dx, dy = t % 2, t // 2 % 2
+        o = place.chip_at(dx, dy, t // 4)
         for side, away in ((0, dx), (1, dy)):
             @pl.when(away == 1)
             def _():
                 for n in range(2):
                     move(n, side, o, SIB, place.sibling).wait_send()
 
-        @pl.when(t >= 8)
-        def _():
-            across(h, k, t // 4).wait_send()
-
         level = t // 4
+        across(h, k, level).wait_send()
 
         @pl.when(level > place.z)
         def _():
@@ -849,7 +839,7 @@
             pltpu.VMEM((2, 2) + piece, bf),
             pltpu.VMEM((2, 2, 2, 2) + piece, bf),
             pltpu.VMEM((2, 2, 2) + piece, bf),
-            pltpu.VMEM((2, 2, 2) + piece, bf),
+            pltpu.VMEM((2, 2, LEVELS) + piece, bf),
             pltpu.VMEM((2, 2, LEVELS) + piece, bf),
             pltpu.VMEM((2, 2, LEVELS) + piece, bf),
             pltpu.VMEM((2, 2, LEVELS + 1) + piece, bf),
@@ -1467,7 +1457,10 @@
         grad_value[...] += jnp.dot(probs.astype(bf), grad, preferred_element_type=f32)
         grad_query = jnp.dot(key_t[...], grad_scores, preferred_element_type=f32).T * scale
         heads[at, 0:128] = raw_grad(query_proj, query_gain, grad_query, at)
-        part_event(b)
+
+        @pl.when((b >= 2) & (b % 2 == 0))
+        def _():
+            part_event(b // 2 - 1)
 
     up_own = weights[pl.ds(2 * p, 2), :, 384:512].reshape(2 * depth, 128)
     up_own = pltpu.roll(up_own.astype(f32), 64, 1).astype(bf)
@@ -1532,7 +1525,10 @@
         @pl.when(c >= 1)
         def _():
             pair_sum(c - 1)
-            part_event(group // 2 + c - 1)
+
+        @pl.when(c % 2 == 0)
+        def _():
+            part_event(3 + c // 2)
 
     @pl.loop(0, group // 2)
     def _(e):
@@ -1559,6 +1555,10 @@
             @pl.when(k == 0)
             def _():
                 out[pl.ds(h * half, half)] = whole
+
+        @pl.when(e % 2 == 1)
+        def _():
+            part_event(8 + e // 2)
 
     owner = lax.broadcasted_iota(jnp.int32, (128, 128), 0) // rank
     up = jnp.zeros((128, 128), f32)
@@ -1610,6 +1610,10 @@
         @pl.when(q == me)
         def _():
             owned_keep.start()
+
+    @pl.loop(12, CHIPS)
+    def _(e):
+        part_event(e)
 
     for h in range(2):
         part_first(h).wait_recv()

time: 586 us -> 545 us (0.930)
  Pallas kernels: 553 us -> 513 us
    pallas_call x1, Pallas kernels: 270 us -> 239 us  [experts_pass(): pl.pallas_call(functools.partial(experts_kernel, rows), out_shape=(jax.Sh...]
    pallas_call x1, Pallas kernels: 153 us -> 144 us  [back(): pl.pallas_call(functools.partial(back_kernel, rows, rank), out_shape=(jax...]
where the time goes in v5:
time: 545 us; the launch traced here: 544 us
  Pallas kernels  513 us (94%)
  local copies, waits for them, and re-layouts  15.3 us (3%)
  matrix products  8.63 us (2%)
  other arithmetic  5.67 us (1%)
    pallas_call x1, Pallas kernels, experts_pass(): pl.pallas_call(functools.partial(experts_kernel, rows), out_shape=(jax.Sh...  239 us
    pallas_call x1, Pallas kernels, back(): pl.pallas_call(functools.partial(back_kernel, rows, rank), out_shape=(jax...  144 us
    pallas_call x1, Pallas kernels, front(): pl.pallas_call(functools.partial(front_kernel, rows, rank), out_shape=(ja...  131 us

profile of v5, /device:TPU:0, one launch (start us, length us, event | category | flops | bytes accessed | tf_op | source)
XLA Modules:
  0.0 543.8 jit_solution(9857079189081142037)
XLA Ops:
  0.6 0.0 copy-start
  0.6 0.0 copy-start.10
  0.7 0.8 fusion.15
  1.5 0.0 copy-start.19
  1.5 0.0 copy-start.20
  1.5 0.0 copy-start.15
  1.5 0.0 copy-start.12
  1.5 1.4 copy.43.q_seg.k_seg
  2.9 1.3 constant_dynamic-slice_fusion.1.k_seg.q_seg
  4.2 0.0 copy-done
  4.2 1.1 copy_bitcast_fusion
  5.3 0.0 copy-done.10
  5.3 0.1 copy_bitcast_fusion.2
  5.4 1.0 maximum_bitcast_fusion.heads_w
  6.4 0.6 convert_element_type.26
  7.0 0.0 copy-done.19
  7.0 0.5 bitcast_convert_fusion
  7.6 0.6 reshape.105
  8.2 1.0 copy.40.downs
  9.2 0.7 copy.41.routes
  9.9 0.7 copy.42.gates
  10.6 130.5 %front.1 = (f32[128,2048]{1,0:T(8,128)}, bf16[128,2048]{1,0:T(8,128)(2,1)}, bf16[128,2048]{1,0:T(8,128)(2,1)}, bf16[128,2048]{1,0:T(8,128)(2,1)}, bf16[128,128]{...) custom-call(s32[2]{0:T(128)} %picked.1, ...), custom_call_target="tpu_custom_call" | custom-call | tf_op jit(solution)/shard_map/front/pallas_call | solution.py:1253
  141.2 2.8 copy.44.coeff
  144.0 238.8 %experts.1 = (f32[2,64,2048]{2,1,0:T(8,128)}, bf16[16,2,64,2048]{3,2,1,0:T(8,128)(2,1)}, bf16[32,2,2,64,2048]{4,3,2,1,0:T(8,128)(2,1)}) custom-call(bf16[128,2048]{1,0:T(8,128)(2,1)} %get-tuple-element.26.x_ref, bf16[128,2048]{1,0:T(8,128)(2,1)} %up_ref.1, bf16[2048,512]{1,0:T(8,128)(2,1)} %bitcast.54, bf16[2048,512]{1,0:T(8,128)(2,1)} %bitcast.55, ...), custom_call_target="tpu_custom_call" | custom-call | tf_op jit(solution)/shard_map/experts/pallas_call | solution.py:828
  382.8 0.0 copy-start.6
  382.8 0.2 multiply_reduce_fusion.1
  383.0 0.0 copy-done.11
  383.0 1.6 multiply_reduce_fusion
  384.7 0.3 multiply_add_fusion.grad_middle
  385.0 0.0 copy-start.2
  385.0 1.6 copy-done.4
  386.6 0.6 convolution_convert_fusion
  387.2 0.2 fusion.10
  387.4 0.0 copy-done.13
  387.4 0.3 fusion.3
  387.7 0.7 pad_maximum_fusion.early
  388.4 6.3 %fusion.8 = f32[128,2048]{1,0:T(8,128)S(1)} fusion(bf16[2048,2048]{1,0:T(8,128)(2,1)} %bitcast.50, f32[128,2048]{1,0:T(8,128)S(1)} %multiply_add_fusion.grad_middle), kind=kOutput, calls=%fused_computation.29 | convolution fusion | flops 1074003968 | bytes 10485760 | tf_op jit(solution)/shard_map/dot_general | solution.py:29
  394.7 0.0 copy-done.2
  394.7 1.3 fusion.grad_mixed
  396.0 143.8 %back.1 = (bf16[128,2048]{1,0:T(8,128)(2,1)}, bf16[128,2048]{1,0:T(8,128)(2,1)}, f32[2,128,128]{2,1,0:T(8,128)}) custom-call(bf16[128,2048]{1,0:T(8,128)(2,1)} %fusion.grad_mixed, bf16[16,2,64,2048]{3,2,1,0:T(8,128)(2,1)} %get-tuple-element.31.part, bf16[32,64,512]{2,1,0:T(8,128)(2,1)} %get-tuple-element.30.weights, ...), custom_call_target="tpu_custom_call" | custom-call | tf_op jit(solution)/shard_map/back/pallas_call | solution.py:1686
  539.8 1.1 constant_dynamic-slice_fusion
  540.9 0.1 copy.46
  541.0 0.0 copy-start.1
  541.0 0.1 multiply_reduce_fusion.2
  541.2 0.2 copy.47
  541.4 0.8 slice_bitcast_fusion
  542.2 0.8 copy.56
  543.0 0.8 copy.57
  (29 shorter events, 0.1 us)
Async XLA Ops:
  0.6 3.6 copy-start
  0.6 4.7 copy-start.10
  1.5 4.9 copy-start.14
  1.5 5.5 %copy-start.19 = (bf16[128]{0:T(256)(128)(2,1)S(1)}, bf16[128]{0:T(256)(128)(2,1)}, u32[]{:S(2)}) copy-start(bf16[128]{0:T(256)(128)(2,1)} %param.28) | copy-start | bytes 772
  1.5 5.5 %copy-start.20 = (bf16[128]{0:T(256)(128)(2,1)S(1)}, bf16[128]{0:T(256)(128)(2,1)}, u32[]{:S(2)}) copy-start(bf16[128]{0:T(256)(128)(2,1)} %param.27) | copy-start | bytes 772
  1.5 6.1 %copy-start.15 = (bf16[2048]{0:T(1024)(128)(2,1)S(1)}, bf16[2048]{0:T(1024)(128)(2,1)}, u32[]{:S(2)}) copy-start(bf16[2048]{0:T(1024)(128)(2,1)} %param.26) | copy-start | bytes 12292
  1.5 6.7 %copy-start.12 = (bf16[8,4,64,16]{2,3,1,0:T(8,128)(2,1)S(1)}, bf16[8,4,64,16]{2,3,1,0:T(8,128)(2,1)}, u32[]{:S(2)}) copy-start(bf16[8,4,64,16]{2,3,1,0:T(8,128)(2,1)} %param.33) | copy-start | bytes 196612
  2.9 6.3 %copy-start.16 = (s32[128,8]{0,1:T(8,128)S(1)}, s32[128,8]{0,1:T(8,128)}, u32[]{:S(2)}) copy-start(s32[128,8]{0,1:T(8,128)} %param.23) | copy-start | bytes 12292
  2.9 7.0 %copy-start.17 = (f32[128,8]{0,1:T(8,128)S(1)}, f32[128,8]{0,1:T(8,128)}, u32[]{:S(2)}) copy-start(f32[128,8]{0,1:T(8,128)} %param.24) | copy-start | bytes 12292
  144.0 238.9 %copy-start.3 = (f32[128,2048]{1,0:T(8,128)S(1)}, f32[128,2048]{1,0:T(8,128)}, u32[]{:S(2)}) copy-start(f32[128,2048]{1,0:T(8,128)} %get-tuple-element.25.middle) | copy-start | bytes 3145732
  144.0 239.0 %copy-start.11 = (f32[2048]{0:T(1024)S(1)}, f32[2048]{0:T(1024)}, u32[]{:S(2)}) copy-start(f32[2048]{0:T(1024)} %convert_element_type.26) | copy-start | bytes 24580
  382.8 1.8 copy-start.5
  382.8 1.8 copy-start.6
  384.6 2.0 copy-start.4
  384.6 2.5 copy-start.7
  384.6 2.7 copy-start.13
  385.0 9.7 %copy-start.2 = (f32[128,2048]{1,0:T(8,128)}, f32[128,2048]{1,0:T(8,128)S(1)}, u32[]{:S(2)}) copy-start(f32[128,2048]{1,0:T(8,128)S(1)} %multiply_add_fusion.grad_middle) | copy-start | bytes 3145732
  396.0 145.1 %copy-start.18 = (s32[2]{0:T(128)S(1)}, s32[2]{0:T(128)}, u32[]{:S(2)}) copy-start(s32[2]{0:T(128)} %picked.1) | copy-start | bytes 28
  539.8 2.4 copy-start.9
  539.8 3.2 copy-start.8
  541.0 2.8 copy-start.1

commit v6 on v5

--- a/solution.py
+++ b/solution.py
@@ -336,6 +336,21 @@
 CHIPS = 16
 
 
+def greet_all(me, devices):
+    barrier = pltpu.get_barrier_semaphore()
+
+    @pl.loop(1, devices)
+    def _(i):
+        pl.semaphore_signal(barrier, inc=1, device_id=((me + i) % devices,), device_id_type=MESH)
+
+
+def segments_at(segs, sequence, at):
+    row = segs[0:1, at]
+    for s in range(1, segs.shape[0]):
+        row = jnp.where(sequence == s, segs[s : s + 1, at], row)
+    return row.astype(jnp.float32)
+
+
 class Place:
     def __init__(self):
         self.me = me = lax.axis_index("fsdp")
@@ -371,174 +386,25 @@
         return self.across_x * (1 - half) + self.across_y * half
 
 
-def scatter_kernel(rows, work, source, out, own, sib, cross_out, cross_in, z_out, z_in, first_out, first_in, total,
-                   own_sem, sib_send, sib_recv, cross_send, cross_recv, z_send, z_recv, first_send, first_recv):
-    place = Place()
-    half_rows = rows // 2
-    f32, bf = jnp.float32, jnp.bfloat16
-
-    def local(o):
-        return pltpu.make_async_copy(source.at[2 * o + place.core], own.at[o], own_sem.at[o])
-
-    def to_sibling(o):
-        return pltpu.make_async_remote_copy(
-            src_ref=source.at[2 * o + 1 - place.core], dst_ref=sib.at[o], send_sem=sib_send.at[o],
-            recv_sem=sib_recv.at[o], device_id=(place.sibling,), device_id_type=MESH)
-
-    def across(h, k, level):
-        return pltpu.make_async_remote_copy(
-            src_ref=cross_out.at[h, k, level], dst_ref=cross_in.at[h, k, level], send_sem=cross_send.at[h, k, level],
-            recv_sem=cross_recv.at[h, k, level], device_id=(place.last(h),), device_id_type=MESH)
-
-    def along(h, k, level, up):
-        return pltpu.make_async_remote_copy(
-            src_ref=z_out.at[h, k, level], dst_ref=z_in.at[up, h, k, level], send_sem=z_send.at[h, k, level],
-            recv_sem=z_recv.at[up, h, k, level], device_id=(place.me - 8 + 16 * up,), device_id_type=MESH)
-
-    def first(h):
-        return pltpu.make_async_remote_copy(
-            src_ref=first_out.at[h], dst_ref=first_in.at[h], send_sem=first_send.at[h],
-            recv_sem=first_recv.at[h], device_id=(place.first(h),), device_id_type=MESH)
-
-    def both(o, h):
-        part = pl.ds(h * half_rows, half_rows)
-        return own[o, part].astype(f32) + sib[o, part].astype(f32)
-
-    @pl.loop(0, CHIPS)
-    def _(q):
-        o = place.chip_at(q % 2, q // 2 % 2, place.level(3 - q // 4))
-        local(o).start()
-        to_sibling(o).start()
-
-    @pl.loop(0, CHIPS + 4)
-    def _(t):
-        @pl.when(t < CHIPS)
-        def _():
-            level = place.level(3 - t // 4)
-            dx, dy = t % 2, t // 2 % 2
-            o = place.chip_at(dx, dy, level)
-            local(o).wait()
-            to_sibling(o).wait_recv()
-            for h, away, k in ((0, dx, dy), (1, dy, dx)):
-                @pl.when(away == 1)
-                def _():
-                    cross_out[h, k, level] = both(o, h).astype(bf)
-                    across(h, k, level).start()
-
-        @pl.when(t >= 4)
-        def _():
-            i, h, k = (t - 4) // 4, t % 2, t // 2 % 2
-            level = place.level(3 - i)
-            o = place.chip(h, k, level)
-            across(h, k, level).wait_recv()
-            total[...] = both(o, h) + cross_in[h, k, level].astype(f32)
-
-            @pl.when((level >= place.z) & (place.z > 0))
-            def _():
-                along(h, k, level, 1).wait_recv()
-                total[...] += z_in[1, h, k, level].astype(f32)
-
-            @pl.when((level <= place.z) & (place.z < LEVELS - 1))
-            def _():
-                along(h, k, level, 0).wait_recv()
-                total[...] += z_in[0, h, k, level].astype(f32)
-
-            @pl.when(level > place.z)
-            def _():
-                z_out[h, k, level] = total[...].astype(bf)
-                along(h, k, level, 1).start()
-
-            @pl.when(level < place.z)
-            def _():
-                z_out[h, k, level] = total[...].astype(bf)
-                along(h, k, level, 0).start()
-
-            @pl.when((level == place.z) & (k == 1))
-            def _():
-                first_out[h] = total[...].astype(bf)
-                first(h).start()
-
-            @pl.when((level == place.z) & (k == 0))
-            def _():
-                out[pl.ds(h * half_rows, half_rows)] = total[...]
-
-        if work is not None:
-            work(t)
-
-    for h in range(2):
-        first(h).wait_recv()
-        out[pl.ds(h * half_rows, half_rows)] += first_in[h].astype(f32)
-
-    @pl.loop(0, CHIPS)
-    def _(q):
-        o = place.chip_at(q % 2, q // 2 % 2, place.level(3 - q // 4))
-        to_sibling(o).wait_send()
-        h, k, level = q % 2, q // 2 % 2, q // 4
-        across(h, k, level).wait_send()
-
-        @pl.when(level > place.z)
-        def _():
-            along(h, k, level, 1).wait_send()
-
-        @pl.when(level < place.z)
-        def _():
-            along(h, k, level, 0).wait_send()
-
-    for h in range(2):
-        first(h).wait_send()
-
-
-def scatter_scratch(rows, width):
-    bf = jnp.bfloat16
-    dma = pltpu.SemaphoreType.DMA
-    piece = (rows // 2, width)
-    return [
-        pltpu.VMEM((CHIPS, rows, width), bf),
-        pltpu.VMEM((CHIPS, rows, width), bf),
-        pltpu.VMEM((2, 2, LEVELS) + piece, bf),
-        pltpu.VMEM((2, 2, LEVELS) + piece, bf),
-        pltpu.VMEM((2, 2, LEVELS) + piece, bf),
-        pltpu.VMEM((2, 2, 2, LEVELS) + piece, bf),
-        pltpu.VMEM((2,) + piece, bf),
-        pltpu.VMEM((2,) + piece, bf),
-        pltpu.VMEM(piece, jnp.float32),
-        dma((CHIPS,)), dma((CHIPS,)), dma((CHIPS,)),
-        dma((2, 2, LEVELS)), dma((2, 2, LEVELS)),
-        dma((2, 2, LEVELS)), dma((2, 2, 2, LEVELS)),
-        dma((2,)), dma((2,)),
-    ]
-
-
-def scatter_all(partial):
-    devices, rows, width = partial.shape
-    return pl.pallas_call(
-        functools.partial(scatter_kernel, rows, None),
-        out_shape=jax.ShapeDtypeStruct((rows, width), jnp.float32),
-        in_specs=[pl.BlockSpec(memory_space=pl.ANY)],
-        out_specs=pl.BlockSpec(memory_space=pltpu.VMEM),
-        scratch_shapes=scatter_scratch(rows, width),
-        compiler_params=pltpu.CompilerParams(has_side_effects=True, vmem_limit_bytes=48 << 20),
-        name="scatter_all",
-    )(partial)
-
-
 OUTER_STEPS = (
-    278531, 8684081, 548864, 50372672, 13396561, 21889169, 33882149, 17581620, 9471010, 55600272, 39080084, 42346578,
-    38601784, 34932793, 11887841, 63513731, 35729961, 39868579, 48350861, 36731452, 45215881, 61890111, 49625245,
-    16334382, 37575933, 62463018, 50150443, 79059002, 44584191, 15537291, 48616602, 79246902, 35155759, 39409401,
-    39735847, 35482347, 64378152, 78529191, 47859943, 77196578, 76957479, 126075168, 126075360, 126075360, 126075360,
-    126075360, 126075360, 126075360, 126075360, 126075360, 126075360, 126075360,
+    819265, 8651264, 12861442, 50372656, 8931409, 17432627, 13697571, 13172803, 37790773, 54809233, 34645544,
+    42607251, 15008899, 14756500, 11890914, 65086601, 16013475, 59585160, 15800984, 41180860, 12187788, 16326300,
+    37256878, 49626350, 11353642, 15294205, 36592266, 15561967, 40523830, 79254266, 10041135, 49140263, 35279415,
+    65867414, 77672101, 60178981, 78533815, 43118213, 76663074, 64638646, 75646758, 126075173, 126075360, 126075360,
+    126075360, 126075360, 126075360, 126075360, 126075360, 126075360, 126075360, 126075360,
 )
 INNER_STEPS = (
-    51829, 9699843, 13936708, 551028, 51423780, 9996900, 10502711, 17092868, 8408709, 16838712, 12658837, 21033529,
-    12912694, 11906089, 13410925, 27593879, 41985814, 35706924, 33850915, 8978567, 47562812, 39879804, 40139314,
-    38052989, 45162741, 16585263, 39357567, 18733167, 12130482, 22616686, 16319635, 33115890, 22886442, 11390570,
-    28079293, 38353539, 45742714, 15539854, 41500262, 32339182, 65596554, 40431279, 27123339, 78722744, 44953901,
-    75851499, 63856430, 76173993, 78209769, 76435697, 76693803, 76959526,
+    297029, 30459904, 543235, 9464372, 51440213, 10266665, 8704550, 8409348, 14486081, 12612200, 14231616, 14705273,
+    39127121, 11903096, 8953965, 71373446, 11568294, 35459180, 17594915, 13173376, 47565949, 15754834, 37812375,
+    42247925, 18406959, 28859544, 39395993, 16349409, 36998782, 66092674, 22609570, 41228375, 34395178, 49923218,
+    28071580, 66659898, 15529128, 37297787, 31027944, 26819743, 36265721, 62723687, 78966458, 26555547, 75847418,
+    79259371, 77945587, 77716258, 78737199, 78507818, 76693795, 76959015,
 )
 
 
-def experts_kernel(rows, x_ref, up_ref, gate_w, up_w, down_w, coeff, out, part_out, gathered,
+def experts_kernel(rows, rank, x_ref, up_ref, gate_w, up_w, down_w, coeff, own_up, middle, gain, matrix, weights, out_inner, mixed,
+                   grad_middle, grad_mixed, early, part_out, gathered,
+                   out, held_w, pairs, tail_sem,
                    block, part_buf, result, sib, cross_out, cross_in, hold, z_in, first_out, first_in, total,
                    local_sem, load_sem, part_sem, send, recv, sib_send, sib_recv, cross_send, cross_recv,
                    z_send, z_recv, first_send, first_recv):
@@ -604,6 +470,28 @@
     start = lambda copy: copy.start()
     done = lambda copy: copy.wait_send()
     mine = me // 2
+    barrier = pltpu.get_barrier_semaphore()
+
+    def greet(other):
+        pl.semaphore_signal(barrier, inc=1, device_id=(other,), device_id_type=MESH)
+
+    for other in (place.sibling, place.across_x, place.across_y):
+        greet(other)
+
+    @pl.when(place.z < LEVELS - 1)
+    def _():
+        greet(me + 8)
+
+    @pl.when(place.z > 0)
+    def _():
+        greet(me - 8)
+
+    tail = [
+        pltpu.make_async_copy(matrix, held_w, tail_sem.at[0]),
+        pltpu.make_async_copy(weights.at[:, :, pl.ds(384, 128)], pairs, tail_sem.at[1]),
+    ]
+    for copy in tail:
+        copy.start()
     own = [
         pltpu.make_async_copy(ref.at[pl.ds(h * half, half)], gathered.at[me, h, n], local_sem.at[n, h])
         for n, ref in enumerate((x_ref, up_ref)) for h in range(2)
@@ -612,6 +500,7 @@
         copy.start()
     for copy in own:
         copy.wait()
+    pl.semaphore_wait(barrier, 4 + inner)
     pieces = [(n, h) for n in range(2) for h in range(2)]
     def keep_part(o, slot):
         return pltpu.make_async_copy(part_buf.at[slot], part_out.at[o], part_sem.at[slot])
@@ -627,7 +516,8 @@
             to_sibling(slot).wait_send()
 
         load.wait()
-        c = coeff[pl.ds(2 * o, 2)].reshape(2 * rows, 1)
+        c = [jnp.broadcast_to(coeff[2 * o + side], (rows, rows)).T[:, 0:1] for side in range(2)]
+        c = jnp.concatenate(c, axis=0)
         x = block[:, :, 0].reshape(2 * rows, -1)
         gate = jnp.dot(x, gate_w[...], preferred_element_type=f32)
         up = jnp.dot(x, up_w[...], preferred_element_type=f32)
@@ -711,7 +601,7 @@
 
         @pl.when((level == place.z) & (k == 0))
         def _():
-            out[h] = total[...]
+            out[pl.ds(h * half, half)] = total[...]
 
     def step(code):
         kind, which = code // 32, code % 32
@@ -775,7 +665,29 @@
 
     for h in range(2):
         first(h).wait_recv()
-        out[h] += first_in[h].astype(f32)
+        out[pl.ds(h * half, half)] += first_in[h].astype(f32)
+    for copy in tail:
+        copy.wait()
+
+    ours = middle[...]
+    inverse = lax.rsqrt(jnp.mean(ours * ours, axis=-1, keepdims=True) + epsilon)
+    unit = ours * inverse
+    scaled = out[...] * gain[...]
+    grad = inverse * (scaled - unit * jnp.mean(scaled * unit, axis=-1, keepdims=True))
+    grad = own_up[...].astype(f32) + grad
+    grad_middle[...] = grad
+    grad = grad.astype(bf)
+    adapters = pairs[...].reshape(-1, 128)
+    lane = lax.broadcasted_iota(jnp.int32, (rows, 128), 1)
+    low = jnp.dot(grad, adapters, preferred_element_type=f32)
+    low = jnp.where(lane // rank == 7, low, 0.0).astype(bf)
+    low = pltpu.roll(low.astype(f32), 64, 1).astype(bf)
+    back = lax.dot_general(grad, held_w[...], flip, preferred_element_type=f32)
+    back += lax.dot_general(low, adapters, flip, preferred_element_type=f32)
+    grad_mixed[...] = back.astype(bf)
+    tall = (((0,), (0,)), ((), ()))
+    early[0:rank] = lax.dot_general(low, mixed[...], tall, preferred_element_type=f32)[3 * rank : 4 * rank]
+    early[rank:] = lax.dot_general(out_inner[...], grad, tall, preferred_element_type=f32)[3 * rank : 4 * rank]
 
     for n, h in pieces:
         move(n, h, mine, FIRST, place.first(h)).wait_send()
@@ -817,7 +729,7 @@
             along(h, k, level, 0, down_slot(level)).wait_send()
 
 
-def experts_pass(x, upstream, gate_w, up_w, down_w, coeff):
+def experts_pass(x, upstream, gate_w, up_w, down_w, coeff, middle, gain, matrix, weights, out_inner, mixed, rank):
     rows, width = x.shape
     devices = coeff.shape[0]
     half = rows // 2
@@ -825,16 +737,22 @@
     dma = pltpu.SemaphoreType.DMA
     vmem, anywhere = pl.BlockSpec(memory_space=pltpu.VMEM), pl.BlockSpec(memory_space=pl.ANY)
     piece = (half, width)
-    grad, part, _ = pl.pallas_call(
-        functools.partial(experts_kernel, rows),
+    return pl.pallas_call(
+        functools.partial(experts_kernel, rows, rank),
         out_shape=(
-            jax.ShapeDtypeStruct((2,) + piece, f32),
+            jax.ShapeDtypeStruct((rows, width), f32),
+            jax.ShapeDtypeStruct((rows, width), bf),
+            jax.ShapeDtypeStruct((2 * rank, width), f32),
             jax.ShapeDtypeStruct((CHIPS, 2) + piece, bf),
             jax.ShapeDtypeStruct((devices, 2, 2) + piece, bf),
         ),
-        in_specs=[anywhere, anywhere, vmem, vmem, vmem, vmem],
-        out_specs=(vmem, anywhere, anywhere),
+        in_specs=[anywhere, anywhere] + [vmem] * 7 + [anywhere, anywhere, vmem, vmem],
+        out_specs=(vmem, vmem, vmem, anywhere, anywhere),
         scratch_shapes=[
+            pltpu.VMEM((rows, width), f32),
+            pltpu.VMEM(matrix.shape, bf),
+            pltpu.VMEM(weights.shape[:2] + (128,), bf),
+            dma((2,)),
             pltpu.VMEM((2, 2, 2) + piece, bf),
             pltpu.VMEM((2, 2) + piece, bf),
             pltpu.VMEM((2, 2, 2, 2) + piece, bf),
@@ -850,17 +768,16 @@
             dma((2, 2, LEVELS)), dma((2, 2, LEVELS)),
             dma((2, 2, LEVELS)), dma((2, 2, LEVELS + 1)), dma((2,)), dma((2,)),
         ],
-        compiler_params=pltpu.CompilerParams(has_side_effects=True, vmem_limit_bytes=56 << 20),
+        compiler_params=pltpu.CompilerParams(collective_id=1, has_side_effects=True, vmem_limit_bytes=62 << 20),
         name="experts",
-    )(x, upstream, gate_w, up_w, down_w, coeff)
-    return grad.reshape(rows, width), part
-
-
-def front_kernel(rows, rank, picked, tokens, rows_gain, heads_w, downs, ups, routes, gates, out_w, near, far_turn,
-                 query_gain, key_gain, ffn_gain, q_seg, k_seg,
+    )(x, upstream, gate_w, up_w, down_w, coeff, upstream, middle, gain, matrix, weights, out_inner, mixed)
+
+
+def front_kernel(rows, rank, picked, tokens, rows_gain, query_w, key_w, value_w, segs, downs, ups, routes, gates, out_w, near, far_turn,
+                 query_gain, key_gain, ffn_gain,
                  middle, normed_ffn, normed, mixed, out_inner, weights, query_out, key_out, value_out,
                  query_proj, key_proj, inner_out, coeff_out, cosine, sine, out_all,
-                 held, mixed_buf, pair, coeff, wo,
+                 held, mixed_buf, pair, coeff, wo, heads_w,
                  local_sem, send, recv, w_send, w_recv, pair_send, pair_recv, c_send, c_recv, m_send, m_recv, m_local,
                  g_send, g_recv, keep_sem):
     place = Place()
@@ -916,6 +833,8 @@
     pair_other = pltpu.make_async_remote_copy(
         src_ref=pair.at[other // group], dst_ref=weights.at[me, :, pl.ds(wide, 128)], send_sem=pair_send.at[2, 0],
         recv_sem=pair_recv.at[me], device_id=(other,), device_id_type=MESH)
+    greet_all(me, 2 * group)
+
     UP, DOWN, G_LAST, G_SIB, G_FIRST = range(5)
 
     def g_move(h, o, kind, target):
@@ -967,15 +886,19 @@
         pltpu.make_async_copy(out_w.at[pl.ds(0, depth // 2)], wo.at[me, 0], local_sem.at[1]),
         pltpu.make_async_copy(out_w.at[pl.ds(depth // 2, depth // 2)], wo.at[me, 1], local_sem.at[2]),
     ]
+    for q in range(group):
+        for j, matrix in enumerate((query_w, key_w, value_w)):
+            heads_w[q, :, j * 128 : (j + 1) * 128] = matrix[:, q * 128 : (q + 1) * 128]
     for copy in own_copies:
         copy.start()
     ours = tokens[...].astype(f32)
     low = (ours * lax.rsqrt(jnp.mean(ours * ours, axis=-1, keepdims=True) + epsilon) * rows_gain[...]).astype(bf)
     held[p] = low
     normed[...] = low
+    pl.semaphore_wait(pltpu.get_barrier_semaphore(), 2 * group - 1)
     for h in range(2):
+        move(h, chip, ALONG, across_z).start()
         move(h, chip, FIRST, place.first(h)).start()
-        move(h, chip, ALONG, across_z).start()
     for h in range(2):
         move(h, chip, LAST, place.last(h)).start()
         move(h, chip, SIB, place.sibling).start()
@@ -1028,14 +951,14 @@
         pair_over((p + i) % group, 1).start()
 
     for h in range(2):
-        o = chip_at(h, 1, 0)
+        o = chip_at(h, 0, 1)
         arrived(h, o, False)
-        move(h, o, ALONG, across_z).start()
+        move(h, o, FIRST, place.first(h)).start()
         move(h, o, LAST, place.last(h)).start()
         move(h, o, SIB, place.sibling).start()
-    for k in range(2):
+    for far in range(2):
         for h in range(2):
-            o = chip_at(h, k, 1)
+            o = chip_at(h, 1, far)
             arrived(h, o, False)
             move(h, o, LAST, place.last(h)).start()
             move(h, o, SIB, place.sibling).start()
@@ -1133,7 +1056,12 @@
     def _(b):
         at = pl.ds(pl.multiple_of(b * span, span), span)
         scores = lax.dot_general(query_out[at], key_out[...], flip, preferred_element_type=f32)
-        weight = jnp.where(q_seg[at] == k_seg[...], jnp.exp2(scores * (scale * math.log2(math.e))), 0.0)
+        own_seg = [
+            jnp.broadcast_to(segments_at(segs, me // group, pl.ds(pl.multiple_of(b * span + i, 128), 128)), (128, 128)).T
+            for i in range(0, span, 128)
+        ]
+        own_seg = jnp.concatenate(own_seg, axis=0)[:, 0:1]
+        weight = jnp.where(own_seg == segments_at(segs, me // group, slice(None)), jnp.exp2(scores * (scale * math.log2(math.e))), 0.0)
         total = jnp.sum(weight, axis=-1, keepdims=True)
         value = jnp.dot(weight.astype(bf), value_out[...], preferred_element_type=f32) / total
         mixed_buf[pl.ds(2 * b, 2)] = value.astype(bf).reshape(2, rows, 128)
@@ -1202,12 +1130,12 @@
 
     pair_other.wait_send()
     for h in range(2):
-        move(h, chip, FIRST, place.first(h)).wait_send()
+        move(h, chip, ALONG, across_z).wait_send()
         for far in range(2):
             for k in range(2):
                 o = chip_at(h, k, far)
-                if far == 0:
-                    move(h, o, ALONG, across_z).wait_send()
+                if k == 0:
+                    move(h, o, FIRST, place.first(h)).wait_send()
                 move(h, o, LAST, place.last(h)).wait_send()
                 move(h, o, SIB, place.sibling).wait_send()
                 dx, dy = (1, k) if h == 0 else (k, 1)
@@ -1238,9 +1166,10 @@
     return tables
 
 
-def front(picked, tokens, rows_gain, heads_w, downs, ups, routes, gates, out_w, query_gain, key_gain, ffn_gain, q_seg, k_seg):
+def front(picked, tokens, rows_gain, query_w, key_w, value_w, segs, downs, ups, routes, gates, out_w,
+          query_gain, key_gain, ffn_gain):
     rows, width = tokens.shape
-    group, depth = heads_w.shape[0], heads_w.shape[1]
+    group, depth = SEQ_LEN // rows, out_w.shape[0]
     rank = downs.shape[3]
     devices, seq = 2 * group, rows * group
     bf, f32 = jnp.bfloat16, jnp.float32
@@ -1261,8 +1190,7 @@
             raw, raw,
             jax.ShapeDtypeStruct((devices, 2, depth // 2, width), bf),
         ),
-        in_specs=[pl.BlockSpec(memory_space=pltpu.SMEM), vmem, vmem, anywhere, vmem, vmem, vmem, vmem, anywhere]
-        + [vmem] * 7,
+        in_specs=[pl.BlockSpec(memory_space=pltpu.SMEM)] + [vmem] * 10 + [anywhere] + [vmem] * 5,
         out_specs=(vmem,) * 15 + (anywhere,),
         scratch_shapes=[
             pltpu.VMEM((group, rows, width), bf),
@@ -1270,22 +1198,27 @@
             pltpu.VMEM((2, depth, 128), bf),
             pltpu.VMEM((group, 1, rows), f32),
             pltpu.VMEM((devices, 2, depth // 2, width), bf),
+            pltpu.VMEM((group, depth, 384), bf),
             dma((3,)), dma((4, 2, group // 2)), dma((2, 2, group // 2)),
             dma((devices,)), dma((devices,)), dma((3, group)), dma((devices,)),
             dma((devices,)), dma((devices,)), dma((group,)), dma((group,)), dma,
             dma((5, 2, CHIPS)), dma((2, 2, CHIPS)), dma,
         ],
-        compiler_params=pltpu.CompilerParams(has_side_effects=True, vmem_limit_bytes=60 << 20),
+        compiler_params=pltpu.CompilerParams(collective_id=0, has_side_effects=True, vmem_limit_bytes=60 << 20),
         name="front",
-    )(picked, tokens, rows_gain, heads_w, downs, ups, routes, gates, out_w, jnp.asarray(near), jnp.asarray(far_turn),
-      query_gain, key_gain, ffn_gain, q_seg, k_seg)
+    )(picked, tokens, rows_gain, query_w, key_w, value_w, segs, downs, ups, routes, gates, out_w, jnp.asarray(near), jnp.asarray(far_turn),
+      query_gain, key_gain, ffn_gain)
+
+
+OUTER_DONE = (0, 1, 2, 2, 3, 4, 4, 5, 5, 6, 7, 9, 9, 9, 9, 9, 9, 9, 9, 9, 9, 11, 11, 12, 13, 13, 14, 14, 16)
+INNER_DONE = (0, 0, 0, 0, 0, 0, 0, 0, 0, 0, 0, 0, 0, 0, 0, 0, 0, 0, 6, 6, 6, 11, 11, 13, 13, 14, 14, 14, 16)
 
 
 def back_kernel(rows, rank, grad_mixed, part, weights, query, key, value, query_proj, key_proj, inner, cosine, sine,
-                query_gain, key_gain, q_seg, k_seg, rows_in, normed, rows_gain, grad_middle, middle, early,
+                query_gain, key_gain, segs, rows_in, normed, rows_gain, grad_middle, middle, early,
                 grad_rows, output, factors, out, up_terms, part_sum, late, early_in, late_in, owned,
                 e_send, e_recv, l_send, l_recv, f_send, f_recv, t_local,
-                grads, key_t, grad_key, grad_value, heads, result, sib, cross_out, cross_in, z_out, z_in, first_out, first_in,
+                grads, key_seg, key_t, grad_key, grad_value, heads, result, sib, cross_out, cross_in, z_out, z_in, first_out, first_in,
                 held, part_in, part_z, part_total, part_first_out, part_first_in,
                 held_sem, pc_send, pc_recv, pz_send, pz_recv, pf_send, pf_recv,
                 a_send, a_recv, a_local, sib_send, sib_recv, cross_send, cross_recv, z_send, z_recv, first_send, first_recv):
@@ -1373,6 +1306,24 @@
         def _():
             part_sum[h] = part_total[...]
 
+    upper = place.z // 2
+    inner_level = place.z * (1 - upper) + (3 - place.z) * upper
+
+    def part_steps(slot):
+        def bound(at):
+            if isinstance(at, int):
+                return OUTER_DONE[at] + inner_level * (INNER_DONE[at] - OUTER_DONE[at])
+            count = 0
+            for i, (outer, inside) in enumerate(zip(OUTER_DONE, INNER_DONE)):
+                count = jnp.where(at == i, jnp.where(inner_level == 0, outer, inside), count)
+            return count
+
+        def one(e, none):
+            part_event(e)
+            return none
+
+        lax.fori_loop(bound(slot), bound(slot + 1), one, 0)
+
     def to_head(q):
         return pltpu.make_async_remote_copy(
             src_ref=grad_mixed.at[:, pl.ds(q * 128, 128)], dst_ref=grads.at[p], send_sem=a_send.at[q],
@@ -1385,6 +1336,14 @@
 
     keep = pltpu.make_async_copy(grad_mixed.at[:, pl.ds(p * 128, 128)], grads.at[p], a_local)
     keep.start()
+    greet_all(me, 2 * group)
+    @pl.loop(0, group)
+    def _(i):
+        at = pl.ds(pl.multiple_of(i * 128, 128), 128)
+        key_seg[at] = jnp.broadcast_to(segments_at(segs, me // group, at), (128, 128)).T
+
+    key_t[...] = key[...].astype(f32).T.astype(bf)
+    pl.semaphore_wait(pltpu.get_barrier_semaphore(), 2 * group - 1)
 
     def early_to(q, frm):
         return pltpu.make_async_remote_copy(
@@ -1422,7 +1381,6 @@
                 part_across(h, k, level).start()
                 keep_piece(h, k, level).start()
 
-    key_t[...] = key[...].astype(f32).T.astype(bf)
     grad_key[...] = jnp.zeros_like(grad_key)
     grad_value[...] = jnp.zeros_like(grad_value)
     keep.wait()
@@ -1448,7 +1406,8 @@
         ours = query[at]
         grad = grads[pl.ds(2 * b, 2)].reshape(span, 128)
         scores = lax.dot_general(key[...], ours, flip, preferred_element_type=f32)
-        weight = jnp.where(k_seg[...] == q_seg[:, at], jnp.exp2(scores * (scale * math.log2(math.e))), 0.0)
+        own_seg = segments_at(segs, me // group, at)
+        weight = jnp.where(key_seg[:, 0:1] == own_seg, jnp.exp2(scores * (scale * math.log2(math.e))), 0.0)
         probs = weight * (1.0 / jnp.sum(weight, axis=0, keepdims=True))
         grad_probs = lax.dot_general(value[...], grad, flip, preferred_element_type=f32)
         mean = jnp.sum(probs * grad_probs, axis=0, keepdims=True)
@@ -1457,10 +1416,7 @@
         grad_value[...] += jnp.dot(probs.astype(bf), grad, preferred_element_type=f32)
         grad_query = jnp.dot(key_t[...], grad_scores, preferred_element_type=f32).T * scale
         heads[at, 0:128] = raw_grad(query_proj, query_gain, grad_query, at)
-
-        @pl.when((b >= 2) & (b % 2 == 0))
-        def _():
-            part_event(b // 2 - 1)
+        part_steps(b)
 
     up_own = weights[pl.ds(2 * p, 2), :, 384:512].reshape(2 * depth, 128)
     up_own = pltpu.roll(up_own.astype(f32), 64, 1).astype(bf)
@@ -1526,9 +1482,7 @@
         def _():
             pair_sum(c - 1)
 
-        @pl.when(c % 2 == 0)
-        def _():
-            part_event(3 + c // 2)
+        part_steps(group // 2 + c)
 
     @pl.loop(0, group // 2)
     def _(e):
@@ -1556,9 +1510,9 @@
             def _():
                 out[pl.ds(h * half, half)] = whole
 
-        @pl.when(e % 2 == 1)
-        def _():
-            part_event(8 + e // 2)
+        part_steps(group + 1 + e)
+
+    part_steps(25)
 
     owner = lax.broadcasted_iota(jnp.int32, (128, 128), 0) // rank
     up = jnp.zeros((128, 128), f32)
@@ -1569,6 +1523,7 @@
     for h in range(2):
         first(h).wait_recv()
         out[pl.ds(h * half, half)] += first_in[h].astype(f32)
+    part_steps(26)
     lane = lax.broadcasted_iota(jnp.int32, (rows, 128), 1)
     grad_inner = jnp.where(lane < 3 * rank, out[:, width:], 0.0).astype(bf)
     late[...] = lax.dot_general(grad_inner, normed[...], tall, preferred_element_type=f32)[: 3 * rank]
@@ -1586,6 +1541,7 @@
     scaled = grad_normed * rows_gain[...]
     grad = inverse * (scaled - unit * jnp.mean(scaled * unit, axis=-1, keepdims=True))
     grad_rows[...] = (grad_middle[...] + grad).astype(bf)
+    part_steps(27)
     early_keep.wait()
     late_keep.wait()
 
@@ -1611,10 +1567,6 @@
         def _():
             owned_keep.start()
 
-    @pl.loop(12, CHIPS)
-    def _(e):
-        part_event(e)
-
     for h in range(2):
         part_first(h).wait_recv()
         side = pl.ds(h * half, half)
@@ -1673,7 +1625,7 @@
 
 
 def back(grad_mixed, part, weights, query, key, value, query_proj, key_proj, inner, cosine, sine,
-         query_gain, key_gain, q_seg, k_seg, rows_in, normed, rows_gain, grad_middle, middle, early, rank):
+         query_gain, key_gain, segs, rows_in, normed, rows_gain, grad_middle, middle, early, rank):
     rows, width = grad_mixed.shape
     seq = query.shape[0]
     group = seq // rows
@@ -1690,7 +1642,7 @@
             jax.ShapeDtypeStruct((rows, width), bf),
             jax.ShapeDtypeStruct((2, 8 * rank, 128), f32),
         ),
-        in_specs=[vmem, pl.BlockSpec(memory_space=pl.ANY)] + [vmem] * 19,
+        in_specs=[vmem, pl.BlockSpec(memory_space=pl.ANY)] + [vmem] * 18,
         out_specs=(vmem, vmem, vmem),
         scratch_shapes=[
             pltpu.VMEM((rows, wide), f32),
@@ -1702,6 +1654,7 @@
             pltpu.VMEM((8 * rank, 128), f32),
             dma((group,)), dma((group,)), dma((group,)), dma((group,)), dma((2,)), dma((2,)), dma((3,)),
             pltpu.VMEM((group, rows, 128), bf),
+            pltpu.VMEM((seq, 128), f32),
             pltpu.VMEM((128, seq), bf),
             pltpu.VMEM((seq, 128), f32),
             pltpu.VMEM((seq, 128), f32),
@@ -1725,10 +1678,10 @@
             dma((group,)), dma((group,)), dma, dma((group // 2,)), dma((group // 2,)),
             dma((2, 2, 2)), dma((2, 2, 2)), dma((2, 2)), dma((2, 2)), dma((2,)), dma((2,)),
         ],
-        compiler_params=pltpu.CompilerParams(has_side_effects=True, vmem_limit_bytes=63 << 20),
+        compiler_params=pltpu.CompilerParams(collective_id=2, has_side_effects=True, vmem_limit_bytes=63 << 20),
         name="back",
     )(grad_mixed, part, weights, query, key, value, query_proj, key_proj, inner, cosine, sine,
-      query_gain, key_gain, q_seg, k_seg, rows_in, normed, rows_gain, grad_middle, middle, early)
+      query_gain, key_gain, segs, rows_in, normed, rows_gain, grad_middle, middle, early)
 
 
 def heads_plan(
@@ -1755,59 +1708,36 @@
     bf, f32 = jnp.bfloat16, jnp.float32
     devices = lax.axis_size("fsdp")
     rows_dev, width = tokens.shape
-    group = SEQ_LEN // rows_dev
     seqs = segments.shape[0]
     rank = adapter_down_factors.shape[3]
     slots = 4 * rank
     own_rows = query_weight.shape[0]
     device = lax.axis_index("fsdp")
-    sequence = device // group
-    segment_row = pick(segments, sequence)
     attn_scale = attention_norm_gain.astype(f32)
     query_scale = query_norm_gain.astype(f32)
     key_scale = key_norm_gain.astype(f32)
     ffn_scale = expert_norm_gain.astype(f32)
 
-    heads_w = jnp.concatenate(
-        [
-            weight.reshape(own_rows, group, HEAD_DIM)
-            for weight in (query_weight, key_weight, value_weight)
-        ],
-        axis=2,
-    ).transpose(1, 0, 2)
     head_gains = (query_scale.reshape(1, HEAD_DIM), key_scale.reshape(1, HEAD_DIM))
-    tall, flat = segment_row.reshape(SEQ_LEN, 1), segment_row.reshape(1, SEQ_LEN)
     (middle, normed_ffn, normed, mixed, out_inner, head_weights, query, key, value, query_proj, key_proj, inner_all,
      coeff_own, *turns, output_matrix) = front(
-        sequence_adapter_index, tokens, attn_scale.reshape(1, width), heads_w, adapter_down_factors,
-        adapter_up_factors, routes, gates, output_weight, *head_gains, ffn_scale.reshape(1, width), tall, flat,
-    )
-    output_matrix = output_matrix.reshape(width, width)
-    out_inner = out_inner[:, 3 * rank : slots]
-    weights = head_weights.reshape(width, 4 * HEAD_DIM)
-    down_out = weights[:, 3 * HEAD_DIM + 3 * rank : 3 * HEAD_DIM + slots]
-    up_out = weights[:, 3 * HEAD_DIM + slots + 3 * rank :]
-
+        sequence_adapter_index, tokens, attn_scale.reshape(1, width), query_weight, key_weight, value_weight,
+        segments, adapter_down_factors,
+        adapter_up_factors, routes, gates, output_weight, *head_gains, ffn_scale.reshape(1, width),
+    )
     slab_gate = expert_gate_weight[0]
     slab_up = expert_up_weight[0]
     slab_down = expert_down_weight[0]
-    coeff_own = coeff_own.reshape(devices, rows_dev, 1)
-    grad_ffn, part = experts_pass(normed_ffn, output_gradient, slab_gate, slab_up, slab_down, coeff_own)
-    upstream = output_gradient.astype(f32)
-    grad_middle = upstream + rms_back(middle, ffn_scale, grad_ffn)
-    grad_attn = grad_middle.astype(bf)
-
-    grad_inner_out = matmul(grad_attn, up_out).astype(bf)
-    grad_mixed = matmul(grad_attn, output_matrix.T) + matmul(grad_inner_out, down_out.T)
-    grad_mixed = grad_mixed.astype(bf)
-    up_out_terms = matmul(out_inner.T, grad_attn)
-    down_out_terms = matmul(grad_inner_out.T, mixed)
+    grad_middle, grad_mixed, early, part, _ = experts_pass(
+        normed_ffn, output_gradient, slab_gate, slab_up, slab_down, coeff_own, middle, ffn_scale.reshape(1, width),
+        output_matrix.reshape(width, width), head_weights, out_inner, mixed, rank,
+    )
 
     grad_tokens, output, terms = back(
         grad_mixed, part, head_weights, query, key, value, query_proj, key_proj, inner_all,
-        *turns, *head_gains, flat, tall,
+        *turns, *head_gains, segments,
         tokens, normed, attn_scale.reshape(1, width), grad_middle, middle,
-        jnp.concatenate([down_out_terms, up_out_terms], axis=0), rank,
+        early, rank,
     )
     terms = lax.dynamic_slice_in_dim(terms, device % 2 * own_rows, own_rows, 2)
     selected = (

time: 545 us -> 507 us (0.930)
  Pallas kernels: 513 us -> 493 us
  matrix products: 8.63 us -> 0 us
  local copies, waits for them, and re-layouts: 15.3 us -> 8.54 us
    pallas_call x1, Pallas kernels: 239 us -> 229 us  [experts_pass(): pl.pallas_call(functools.partial(experts_kernel, rows, rank), out_shape=(...]
    dot_general x5 -> x0, matrix products: 8.63 us -> none  [matmul(): return jnp.dot(left, right, preferred_element_type=jnp.float32)]
    reshape x5 -> x0, local copies, waits for them, and re-layouts: 6.06 us -> none  [the longest x1 2.77 us: heads_plan(): coeff_own = coeff_own.reshape(devices, rows_dev, 1)]
where the time goes in v6:
time: 507 us; the launch traced here: 506 us
  Pallas kernels  493 us (97%)
  local copies, waits for them, and re-layouts  8.54 us (2%)
    pallas_call x1, Pallas kernels, experts_pass(): pl.pallas_call(functools.partial(experts_kernel, rows, rank), out_shape=(...  229 us
    pallas_call x1, Pallas kernels, back(): pl.pallas_call(functools.partial(back_kernel, rows, rank), out_shape=(jax...  139 us
    pallas_call x1, Pallas kernels, front(): pl.pallas_call(functools.partial(front_kernel, rows, rank), out_shape=(ja...  125 us

profile of v6, /device:TPU:0, one launch (start us, length us, event | category | flops | bytes accessed | tf_op | source)
XLA Modules:
  0.0 506.1 jit_solution(15618488352435549608)
XLA Ops:
  0.6 1.3 bitcast_convert_fusion
  1.9 1.3 reshape.66
  3.2 1.3 reshape.72
  4.4 1.9 copy.31.downs
  6.4 1.4 copy.32.routes
  7.8 1.4 copy.33.gates
  9.2 125.2 %front.1 = (f32[128,2048]{1,0:T(8,128)}, bf16[128,2048]{1,0:T(8,128)(2,1)}, bf16[128,2048]{1,0:T(8,128)(2,1)}, bf16[128,2048]{1,0:T(8,128)(2,1)}, bf16[128,128]{...) custom-call(s32[2]{0:T(128)} %picked.1, ...), custom_call_target="tpu_custom_call" | custom-call | tf_op jit(solution)/shard_map/front/pallas_call | solution.py:1182
  134.4 229.1 %experts.1 = (f32[128,2048]{1,0:T(8,128)}, bf16[128,2048]{1,0:T(8,128)(2,1)}, f32[32,2048]{1,0:T(8,128)}, bf16[16,2,64,2048]{3,2,1,0:T(8,128)(2,1)}, bf16[32,2,2,64,2048]{4,3,2,1,0:T(8,128)(2,1)}) custom-call(bf16[128,2048]{1,0:T(8,128)(2,1)} %get-tuple-element.27.x_ref, bf16[128,2048]{1,0:T(8,128)(2,1)} %own_up.1, bf16[2048,512]{1,0:T(8,128)(2,1)} %bitcast.21, ...), custom_call_target="tpu_custom_call" | custom-call | tf_op jit(solution)/shard_map/experts/pallas_call | solution.py:740
  363.5 0.0 copy-start.2
  363.5 138.6 %back.1 = (bf16[128,2048]{1,0:T(8,128)(2,1)}, bf16[128,2048]{1,0:T(8,128)(2,1)}, f32[2,128,128]{2,1,0:T(8,128)}) custom-call(bf16[128,2048]{1,0:T(8,128)(2,1)} %get-tuple-element.34.grad_mixed, bf16[16,2,64,2048]{3,2,1,0:T(8,128)(2,1)} %get-tuple-element.35.part, bf16[32,64,512]{2,1,0:T(8,128)(2,1)} %get-tuple-element.31.weights, ...), custom_call_target="tpu_custom_call" | custom-call | tf_op jit(solution)/shard_map/back/pallas_call | solution.py:1638
  502.1 0.0 copy-start.1
  502.1 0.0 copy-start
  502.1 1.1 constant_dynamic-slice_fusion
  503.2 0.1 copy.34
  503.3 0.0 copy-done.2
  503.3 0.1 multiply_reduce_fusion
  503.4 0.2 copy.35
  503.6 0.8 slice_bitcast_fusion
  504.5 0.0 copy-done.1
  504.5 0.8 copy.38
  505.3 0.0 copy-done
  505.3 0.8 copy.39
  (1 shorter events, 0.0 us)
Async XLA Ops:
  363.5 139.8 %copy-start.2 = (s32[2]{0:T(128)S(1)}, s32[2]{0:T(128)}, u32[]{:S(2)}) copy-start(s32[2]{0:T(128)} %picked.1) | copy-start | bytes 28
  502.1 2.4 copy-start.1
  502.1 3.2 copy-start

commit v7 on v6

--- a/solution.py
+++ b/solution.py
@@ -402,7 +402,7 @@
 )
 
 
-def experts_kernel(rows, rank, x_ref, up_ref, gate_w, up_w, down_w, coeff, own_up, middle, gain, matrix, weights, out_inner, mixed,
+def experts_kernel(rows, rank, x_ref, up_ref, gate_w, up_w, down_w, coeff, own_up, middle, gains, matrix, weights, out_inner, mixed,
                    grad_middle, grad_mixed, early, part_out, gathered,
                    out, held_w, pairs, tail_sem,
                    block, part_buf, result, sib, cross_out, cross_in, hold, z_in, first_out, first_in, total,
@@ -672,7 +672,7 @@
     ours = middle[...]
     inverse = lax.rsqrt(jnp.mean(ours * ours, axis=-1, keepdims=True) + epsilon)
     unit = ours * inverse
-    scaled = out[...] * gain[...]
+    scaled = out[...] * gains[1:2]
     grad = inverse * (scaled - unit * jnp.mean(scaled * unit, axis=-1, keepdims=True))
     grad = own_up[...].astype(f32) + grad
     grad_middle[...] = grad
@@ -729,7 +729,7 @@
             along(h, k, level, 0, down_slot(level)).wait_send()
 
 
-def experts_pass(x, upstream, gate_w, up_w, down_w, coeff, middle, gain, matrix, weights, out_inner, mixed, rank):
+def experts_pass(x, upstream, gate_w, up_w, down_w, coeff, middle, gains, matrix, weights, out_inner, mixed, rank):
     rows, width = x.shape
     devices = coeff.shape[0]
     half = rows // 2
@@ -770,11 +770,11 @@
         ],
         compiler_params=pltpu.CompilerParams(collective_id=1, has_side_effects=True, vmem_limit_bytes=62 << 20),
         name="experts",
-    )(x, upstream, gate_w, up_w, down_w, coeff, upstream, middle, gain, matrix, weights, out_inner, mixed)
-
-
-def front_kernel(rows, rank, picked, tokens, rows_gain, query_w, key_w, value_w, segs, downs, ups, routes, gates, out_w, near, far_turn,
-                 query_gain, key_gain, ffn_gain,
+    )(x, upstream, gate_w, up_w, down_w, coeff, upstream, middle, gains, matrix, weights, out_inner, mixed)
+
+
+def front_kernel(rows, rank, picked, tokens, gains, query_w, key_w, value_w, segs, downs, ups, routes, gates, out_w, near, far_turn,
+                 query_gain, key_gain,
                  middle, normed_ffn, normed, mixed, out_inner, weights, query_out, key_out, value_out,
                  query_proj, key_proj, inner_out, coeff_out, cosine, sine, out_all,
                  held, mixed_buf, pair, coeff, wo, heads_w,
@@ -892,7 +892,7 @@
     for copy in own_copies:
         copy.start()
     ours = tokens[...].astype(f32)
-    low = (ours * lax.rsqrt(jnp.mean(ours * ours, axis=-1, keepdims=True) + epsilon) * rows_gain[...]).astype(bf)
+    low = (ours * lax.rsqrt(jnp.mean(ours * ours, axis=-1, keepdims=True) + epsilon) * gains[0:1]).astype(bf)
     held[p] = low
     normed[...] = low
     pl.semaphore_wait(pltpu.get_barrier_semaphore(), 2 * group - 1)
@@ -905,9 +905,8 @@
 
     for s in range(2):
         down, up = downs[picked[s]].astype(f32), ups[picked[s]].astype(f32)
-        down = jnp.concatenate([down[j] for j in range(4)], axis=1)
-        up = jnp.concatenate([up[j] for j in range(4)], axis=0).T
-        pair[s] = jnp.concatenate([down, up], axis=1).astype(bf)
+        both = [jnp.concatenate([side[j] for j in range(4)], axis=0).T for side in (down, up)]
+        pair[s] = jnp.concatenate(both, axis=1).astype(bf)
     weights[me, :, wide:] = pair[me // group]
     pair_other.start()
 
@@ -916,10 +915,10 @@
         to_heads(other_base + (p + i) % group).start()
 
     lane = lax.broadcasted_iota(jnp.int32, (rows, 128), 1)
-    gate = jnp.zeros((rows, 128), f32)
-    for k in range(routes.shape[1]):
-        gate += jnp.where(lane == routes[:, k : k + 1], gates[:, k : k + 1], 0.0)
-    gate = gate.T
+    expert = lax.broadcasted_iota(jnp.int32, (coeff.shape[0], rows), 0)
+    gate = jnp.zeros(expert.shape, f32)
+    for k in range(routes.shape[0]):
+        gate += jnp.where(expert == routes[k : k + 1], gates[k : k + 1], 0.0)
     for e in range(coeff.shape[0]):
         coeff[e] = gate[e : e + 1]
     coeff_out[me] = coeff[me // 2]
@@ -1106,7 +1105,7 @@
     total = total + lax.dot_general(shifted, matrix, flip, preferred_element_type=f32)
     middle[...] = total
     unit = total * lax.rsqrt(jnp.mean(total * total, axis=-1, keepdims=True) + epsilon)
-    normed_ffn[...] = (unit * ffn_gain[...]).astype(bf)
+    normed_ffn[...] = (unit * gains[1:2]).astype(bf)
 
     keep_out.wait()
     for h in range(2):
@@ -1166,11 +1165,11 @@
     return tables
 
 
-def front(picked, tokens, rows_gain, query_w, key_w, value_w, segs, downs, ups, routes, gates, out_w,
-          query_gain, key_gain, ffn_gain):
+def front(picked, tokens, gains, query_w, key_w, value_w, segs, downs, ups, routes, gates, out_w,
+          query_gain, key_gain):
     rows, width = tokens.shape
     group, depth = SEQ_LEN // rows, out_w.shape[0]
-    rank = downs.shape[3]
+    rank = downs.shape[2]
     devices, seq = 2 * group, rows * group
     bf, f32 = jnp.bfloat16, jnp.float32
     dma = pltpu.SemaphoreType.DMA
@@ -1190,7 +1189,7 @@
             raw, raw,
             jax.ShapeDtypeStruct((devices, 2, depth // 2, width), bf),
         ),
-        in_specs=[pl.BlockSpec(memory_space=pltpu.SMEM)] + [vmem] * 10 + [anywhere] + [vmem] * 5,
+        in_specs=[pl.BlockSpec(memory_space=pltpu.SMEM)] + [vmem] * 10 + [anywhere] + [vmem] * 4,
         out_specs=(vmem,) * 15 + (anywhere,),
         scratch_shapes=[
             pltpu.VMEM((group, rows, width), bf),
@@ -1206,8 +1205,8 @@
         ],
         compiler_params=pltpu.CompilerParams(collective_id=0, has_side_effects=True, vmem_limit_bytes=60 << 20),
         name="front",
-    )(picked, tokens, rows_gain, query_w, key_w, value_w, segs, downs, ups, routes, gates, out_w, jnp.asarray(near), jnp.asarray(far_turn),
-      query_gain, key_gain, ffn_gain)
+    )(picked, tokens, gains, query_w, key_w, value_w, segs, downs, ups, routes, gates, out_w, jnp.asarray(near), jnp.asarray(far_turn),
+      query_gain, key_gain)
 
 
 OUTER_DONE = (0, 1, 2, 2, 3, 4, 4, 5, 5, 6, 7, 9, 9, 9, 9, 9, 9, 9, 9, 9, 9, 11, 11, 12, 13, 13, 14, 14, 16)
@@ -1215,7 +1214,7 @@
 
 
 def back_kernel(rows, rank, grad_mixed, part, weights, query, key, value, query_proj, key_proj, inner, cosine, sine,
-                query_gain, key_gain, segs, rows_in, normed, rows_gain, grad_middle, middle, early,
+                query_gain, key_gain, segs, rows_in, normed, gains, grad_middle, middle, early,
                 grad_rows, output, factors, out, up_terms, part_sum, late, early_in, late_in, owned,
                 e_send, e_recv, l_send, l_recv, f_send, f_recv, t_local,
                 grads, key_seg, key_t, grad_key, grad_value, heads, result, sib, cross_out, cross_in, z_out, z_in, first_out, first_in,
@@ -1538,7 +1537,7 @@
     ours = rows_in[...].astype(f32)
     inverse = lax.rsqrt(jnp.mean(ours * ours, axis=-1, keepdims=True) + epsilon)
     unit = ours * inverse
-    scaled = grad_normed * rows_gain[...]
+    scaled = grad_normed * gains[0:1]
     grad = inverse * (scaled - unit * jnp.mean(scaled * unit, axis=-1, keepdims=True))
     grad_rows[...] = (grad_middle[...] + grad).astype(bf)
     part_steps(27)
@@ -1625,7 +1624,7 @@
 
 
 def back(grad_mixed, part, weights, query, key, value, query_proj, key_proj, inner, cosine, sine,
-         query_gain, key_gain, segs, rows_in, normed, rows_gain, grad_middle, middle, early, rank):
+         query_gain, key_gain, segs, rows_in, normed, gains, grad_middle, middle, early, rank):
     rows, width = grad_mixed.shape
     seq = query.shape[0]
     group = seq // rows
@@ -1681,7 +1680,7 @@
         compiler_params=pltpu.CompilerParams(collective_id=2, has_side_effects=True, vmem_limit_bytes=63 << 20),
         name="back",
     )(grad_mixed, part, weights, query, key, value, query_proj, key_proj, inner, cosine, sine,
-      query_gain, key_gain, segs, rows_in, normed, rows_gain, grad_middle, middle, early)
+      query_gain, key_gain, segs, rows_in, normed, gains, grad_middle, middle, early)
 
 
 def heads_plan(
@@ -1713,30 +1712,29 @@
     slots = 4 * rank
     own_rows = query_weight.shape[0]
     device = lax.axis_index("fsdp")
-    attn_scale = attention_norm_gain.astype(f32)
+    gains = jnp.stack([attention_norm_gain, expert_norm_gain]).astype(f32)
     query_scale = query_norm_gain.astype(f32)
     key_scale = key_norm_gain.astype(f32)
-    ffn_scale = expert_norm_gain.astype(f32)
 
     head_gains = (query_scale.reshape(1, HEAD_DIM), key_scale.reshape(1, HEAD_DIM))
     (middle, normed_ffn, normed, mixed, out_inner, head_weights, query, key, value, query_proj, key_proj, inner_all,
      coeff_own, *turns, output_matrix) = front(
-        sequence_adapter_index, tokens, attn_scale.reshape(1, width), query_weight, key_weight, value_weight,
-        segments, adapter_down_factors,
-        adapter_up_factors, routes, gates, output_weight, *head_gains, ffn_scale.reshape(1, width),
+        sequence_adapter_index, tokens, gains, query_weight, key_weight, value_weight,
+        segments, adapter_down_factors.swapaxes(2, 3),
+        adapter_up_factors, routes.T, gates.T, output_weight, *head_gains,
     )
     slab_gate = expert_gate_weight[0]
     slab_up = expert_up_weight[0]
     slab_down = expert_down_weight[0]
     grad_middle, grad_mixed, early, part, _ = experts_pass(
-        normed_ffn, output_gradient, slab_gate, slab_up, slab_down, coeff_own, middle, ffn_scale.reshape(1, width),
+        normed_ffn, output_gradient, slab_gate, slab_up, slab_down, coeff_own, middle, gains,
         output_matrix.reshape(width, width), head_weights, out_inner, mixed, rank,
     )
 
     grad_tokens, output, terms = back(
         grad_mixed, part, head_weights, query, key, value, query_proj, key_proj, inner_all,
         *turns, *head_gains, segments,
-        tokens, normed, attn_scale.reshape(1, width), grad_middle, middle,
+        tokens, normed, gains, grad_middle, middle,
         early, rank,
     )
     terms = lax.dynamic_slice_in_dim(terms, device % 2 * own_rows, own_rows, 2)

time: 507 us -> 502 us (level)
  no operation moved by 1% of the time
where the time goes in v7:
time: 502 us; the launch traced here: 500 us
  Pallas kernels  493 us (98%)
  local copies, waits for them, and re-layouts  5.19 us (1%)
    pallas_call x1, Pallas kernels, experts_pass(): pl.pallas_call(functools.partial(experts_kernel, rows, rank), out_shape=(...  229 us
    pallas_call x1, Pallas kernels, back(): pl.pallas_call(functools.partial(back_kernel, rows, rank), out_shape=(jax...  138 us
    pallas_call x1, Pallas kernels, front(): pl.pallas_call(functools.partial(front_kernel, rows, rank), out_shape=(ja...  125 us

profile of v7, /device:TPU:0, one launch (start us, length us, event | category | flops | bytes accessed | tf_op | source)
XLA Modules:
  0.0 500.4 jit_solution(17348873496922228213)
XLA Ops:
  0.6 0.7 stack.10
  1.3 0.7 stack.9
  2.0 0.6 maximum_convert_fusion.gains
  2.6 1.2 bitcast_convert_fusion
  3.8 125.0 %front.1 = (f32[128,2048]{1,0:T(8,128)}, bf16[128,2048]{1,0:T(8,128)(2,1)}, bf16[128,2048]{1,0:T(8,128)(2,1)}, bf16[128,2048]{1,0:T(8,128)(2,1)}, bf16[128,128]{...) custom-call(s32[2]{0:T(128)} %picked.1, ...), custom_call_target="tpu_custom_call" | custom-call | tf_op jit(solution)/shard_map/front/pallas_call | solution.py:1181
  128.8 229.1 %experts.1 = (f32[128,2048]{1,0:T(8,128)}, bf16[128,2048]{1,0:T(8,128)(2,1)}, f32[32,2048]{1,0:T(8,128)}, bf16[16,2,64,2048]{3,2,1,0:T(8,128)(2,1)}, bf16[32,2,2,64,2048]{4,3,2,1,0:T(8,128)(2,1)}) custom-call(bf16[128,2048]{1,0:T(8,128)(2,1)} %get-tuple-element.27.x_ref, bf16[128,2048]{1,0:T(8,128)(2,1)} %own_up.1, bf16[2048,512]{1,0:T(8,128)(2,1)} %bitcast.21, ...), custom_call_target="tpu_custom_call" | custom-call | tf_op jit(solution)/shard_map/experts/pallas_call | solution.py:740
  358.0 0.0 copy-start.2
  358.0 138.5 %back.1 = (bf16[128,2048]{1,0:T(8,128)(2,1)}, bf16[128,2048]{1,0:T(8,128)(2,1)}, f32[2,128,128]{2,1,0:T(8,128)}) custom-call(bf16[128,2048]{1,0:T(8,128)(2,1)} %get-tuple-element.34.grad_mixed, bf16[16,2,64,2048]{3,2,1,0:T(8,128)(2,1)} %get-tuple-element.35.part, bf16[32,64,512]{2,1,0:T(8,128)(2,1)} %get-tuple-element.31.weights, ...), custom_call_target="tpu_custom_call" | custom-call | tf_op jit(solution)/shard_map/back/pallas_call | solution.py:1637
  496.5 0.0 copy-start.1
  496.5 0.0 copy-start
  496.5 1.1 constant_dynamic-slice_fusion
  497.6 0.1 copy.25
  497.7 0.0 copy-done.2
  497.7 0.1 multiply_reduce_fusion
  497.8 0.2 copy.26
  498.0 0.8 slice_bitcast_fusion
  498.9 0.0 copy-done.1
  498.9 0.8 copy.29
  499.6 0.0 copy-done
  499.6 0.8 copy.30
  (1 shorter events, 0.0 us)
Async XLA Ops:
  358.0 139.7 %copy-start.2 = (s32[2]{0:T(128)S(1)}, s32[2]{0:T(128)}, u32[]{:S(2)}) copy-start(s32[2]{0:T(128)} %picked.1) | copy-start | bytes 28
  496.5 2.4 copy-start.1
  496.5 3.2 copy-start

commit v8 on v7

--- a/solution.py
+++ b/solution.py
@@ -506,16 +506,24 @@
         return pltpu.make_async_copy(part_buf.at[slot], part_out.at[o], part_sem.at[slot])
 
     def compute(o, slot, again):
-        for n, h in pieces:
-            arrived(n, h, o, True)
-        load = pltpu.make_async_copy(gathered.at[pl.ds(2 * o, 2)], block, load_sem)
-        load.start()
+        def load(n, sibling):
+            side = 1 - core if sibling else core
+            return pltpu.make_async_copy(
+                gathered.at[2 * o + side, :, n], block.at[side, :, n], load_sem.at[n, 1 if sibling else 0])
+
+        for n in range(2):
+            load(n, False).start()
+        for n in range(2):
+            for h in range(2):
+                arrived(n, h, o, True)
+            load(n, True).start()
 
         @pl.when(again)
         def _():
             to_sibling(slot).wait_send()
 
-        load.wait()
+        load(0, False).wait()
+        load(0, True).wait()
         c = [jnp.broadcast_to(coeff[2 * o + side], (rows, rows)).T[:, 0:1] for side in range(2)]
         c = jnp.concatenate(c, axis=0)
         x = block[:, :, 0].reshape(2 * rows, -1)
@@ -528,6 +536,8 @@
         part = part.reshape(2, 2, half, -1)
         result[slot, 0, 1] = part[0]
         result[slot, 1, 1] = part[1]
+        load(1, False).wait()
+        load(1, True).wait()
         upstream = (c * block[:, :, 1].reshape(2 * rows, -1).astype(f32)).astype(bf)
         grad_hidden = lax.dot_general(upstream, down_w[...], flip, preferred_element_type=f32)
         grad_gate = (grad_hidden * up * sig * (1.0 + gate * (1.0 - sig))).astype(bf)
@@ -764,7 +774,7 @@
             pltpu.VMEM((2,) + piece, bf),
             pltpu.VMEM((2,) + piece, bf),
             pltpu.VMEM(piece, f32),
-            dma((2, 2)), dma, dma((2,)), dma((5, 2, 2, CHIPS)), dma((2, 2, 2, CHIPS)), dma((2,)), dma((2,)),
+            dma((2, 2)), dma((2, 2)), dma((2,)), dma((5, 2, 2, CHIPS)), dma((2, 2, 2, CHIPS)), dma((2,)), dma((2,)),
             dma((2, 2, LEVELS)), dma((2, 2, LEVELS)),
             dma((2, 2, LEVELS)), dma((2, 2, LEVELS + 1)), dma((2,)), dma((2,)),
         ],
@@ -903,16 +913,16 @@
         move(h, chip, LAST, place.last(h)).start()
         move(h, chip, SIB, place.sibling).start()
 
+    @pl.loop(0, group)
+    def _(i):
+        to_heads(other_base + (p + i) % group).start()
+
     for s in range(2):
         down, up = downs[picked[s]].astype(f32), ups[picked[s]].astype(f32)
         both = [jnp.concatenate([side[j] for j in range(4)], axis=0).T for side in (down, up)]
         pair[s] = jnp.concatenate(both, axis=1).astype(bf)
     weights[me, :, wide:] = pair[me // group]
     pair_other.start()
-
-    @pl.loop(0, group)
-    def _(i):
-        to_heads(other_base + (p + i) % group).start()
 
     lane = lax.broadcasted_iota(jnp.int32, (rows, 128), 1)
     expert = lax.broadcasted_iota(jnp.int32, (coeff.shape[0], rows), 0)

time: 502 us -> 501 us (level)
  no operation moved by 1% of the time
where the time goes in v8:
time: 501 us; the launch traced here: 500 us
  Pallas kernels  492 us (98%)
  local copies, waits for them, and re-layouts  5.19 us (1%)
    pallas_call x1, Pallas kernels, experts_pass(): pl.pallas_call(functools.partial(experts_kernel, rows, rank), out_shape=(...  230 us
    pallas_call x1, Pallas kernels, back(): pl.pallas_call(functools.partial(back_kernel, rows, rank), out_shape=(jax...  137 us
    pallas_call x1, Pallas kernels, front(): pl.pallas_call(functools.partial(front_kernel, rows, rank), out_shape=(ja...  124 us

profile of v8, /device:TPU:0, one launch (start us, length us, event | category | flops | bytes accessed | tf_op | source)
XLA Modules:
  0.0 499.5 jit_solution(775865019103873087)
XLA Ops:
  0.6 0.7 stack.10
  1.3 0.7 stack.9
  2.0 0.6 maximum_convert_fusion.gains
  2.6 1.2 bitcast_convert_fusion
  3.8 124.3 %front.1 = (f32[128,2048]{1,0:T(8,128)}, bf16[128,2048]{1,0:T(8,128)(2,1)}, bf16[128,2048]{1,0:T(8,128)(2,1)}, bf16[128,2048]{1,0:T(8,128)(2,1)}, bf16[128,128]{...) custom-call(s32[2]{0:T(128)} %picked.1, ...), custom_call_target="tpu_custom_call" | custom-call | tf_op jit(solution)/shard_map/front/pallas_call | solution.py:1191
  128.2 229.9 %experts.1 = (f32[128,2048]{1,0:T(8,128)}, bf16[128,2048]{1,0:T(8,128)(2,1)}, f32[32,2048]{1,0:T(8,128)}, bf16[16,2,64,2048]{3,2,1,0:T(8,128)(2,1)}, bf16[32,2,2,64,2048]{4,3,2,1,0:T(8,128)(2,1)}) custom-call(bf16[128,2048]{1,0:T(8,128)(2,1)} %get-tuple-element.27.x_ref, bf16[128,2048]{1,0:T(8,128)(2,1)} %own_up.1, bf16[2048,512]{1,0:T(8,128)(2,1)} %bitcast.21, ...), custom_call_target="tpu_custom_call" | custom-call | tf_op jit(solution)/shard_map/experts/pallas_call | solution.py:750
  358.1 0.0 copy-start.2
  358.1 137.4 %back.1 = (bf16[128,2048]{1,0:T(8,128)(2,1)}, bf16[128,2048]{1,0:T(8,128)(2,1)}, f32[2,128,128]{2,1,0:T(8,128)}) custom-call(bf16[128,2048]{1,0:T(8,128)(2,1)} %get-tuple-element.34.grad_mixed, bf16[16,2,64,2048]{3,2,1,0:T(8,128)(2,1)} %get-tuple-element.35.part, bf16[32,64,512]{2,1,0:T(8,128)(2,1)} %get-tuple-element.31.weights, ...), custom_call_target="tpu_custom_call" | custom-call | tf_op jit(solution)/shard_map/back/pallas_call | solution.py:1647
  495.5 0.0 copy-start.1
  495.5 0.0 copy-start
  495.6 1.1 constant_dynamic-slice_fusion
  496.7 0.1 copy.25
  496.7 0.0 copy-done.2
  496.8 0.1 multiply_reduce_fusion
  496.9 0.2 copy.26
  497.1 0.8 slice_bitcast_fusion
  497.9 0.0 copy-done.1
  497.9 0.8 copy.29
  498.7 0.0 copy-done
  498.7 0.8 copy.30
  (1 shorter events, 0.0 us)
Async XLA Ops:
  358.1 138.6 %copy-start.2 = (s32[2]{0:T(128)S(1)}, s32[2]{0:T(128)}, u32[]{:S(2)}) copy-start(s32[2]{0:T(128)} %picked.1) | copy-start | bytes 28
  495.5 2.4 copy-start.1
  495.5 3.2 copy-start
